TPU v7x, 256 devices: a whole 4x4x8 slice. The times are simulated.
256 devices in a mesh: dp: 4 (over y), sy: 4 (over z_lo, core), sx: 16 (over x, z_hi).
Axes of the slice: x: 4, y: 4, z: 8 (z_hi: 4, z_lo: 2; z = z_hi * 2 + z_lo), core: 2. Of those that a mesh axis runs over, the one named last changes fastest.
Arguments:
- inputs: bfloat16 [4, 8, 32, 32, 512], P('dp', None, 'sy', 'sx'), may hold values from -6 to 6
- pre_activation: bfloat16 [4, 8, 32, 32, 512], P('dp', None, 'sy', 'sx'), may hold values from -6 to 6
- upstream: bfloat16 [4, 8, 32, 32, 512], P('dp', None, 'sy', 'sx'), may hold values from -6 to 6
- weight: bfloat16 [27, 512, 512], P(None, 'dp'), may hold values from -0.0546875 to 0.0546875
- first_moment: float32 [13824, 128], P(('dp', 'sy', 'sx')), may hold values from -4 to 4
- second_moment: float32 [13824, 128], P(('dp', 'sy', 'sx')), may hold values from 0.05 to 1
- hash_seed: int32 [], replicated, may hold values from 0 to 999999
- step_count: int32 [], replicated, may hold values from 1 to 29
Outputs:
- input_grad: bfloat16 [4, 8, 32, 32, 512], P('dp', None, 'sy', 'sx')
- new_first: float32 [13824, 128], P(('dp', 'sy', 'sx'))
- new_second: float32 [13824, 128], P(('dp', 'sy', 'sx'))
- scales: float32 [13824], P(('dp', 'sy', 'sx'))
All inputs are finite; a program needn't handle non-finite values.
Results may differ from a plain program's by a relative error of at most 0.004.
Values may be sent and summed in bfloat16 or wider, within the bound.
No kernel may reach another device: no remote copies, remote signals or barrier semaphores. Data moves between devices by JAX's collectives and lax.ppermute only.
A program may use at most 128 MiB of HBM per device.

v0:
```python
import math

import jax
import jax.numpy as jnp
from jax import lax
from jax.sharding import PartitionSpec as P


def extended(cells, sides, width):
    for axis, dim in sides:
        count = lax.axis_size(axis)
        ends = count - 1
        head = lax.slice_in_dim(cells, 0, width, axis=dim)
        tail = lax.slice_in_dim(cells, cells.shape[dim] - width, cells.shape[dim], axis=dim)
        cells = jnp.concatenate(
            [
                lax.ppermute(tail, axis, [(i, (i + 1) % count) for i in range(ends)]),
                cells,
                lax.ppermute(head, axis, [((i + 1) % count, i) for i in range(ends)]),
            ],
            axis=dim,
        )
    return cells


def in_blocks(value, dim, devices):
    dims = value.shape
    parts = value.reshape(*dims[:dim], devices, dims[dim] // devices, *dims[dim + 1 :])
    return jnp.moveaxis(parts, dim, 0)


def own_tiles(value, axis, dim):
    devices = lax.axis_size(axis)
    parts = in_blocks(value, dim, devices)
    lines = parts.reshape(devices, -1)
    span = max(16, -(-lines.shape[1] // 1024) * 8)
    lines = jnp.pad(lines, ((0, 0), (0, span * 128 - lines.shape[1]))).reshape(-1, 128)
    own = lax.psum_scatter(lines, axis, scatter_dimension=0, tiled=True)
    return own.reshape(-1)[: parts[0].size].reshape(parts.shape[1:])


def projection(hash_seed, rows_count, cols_count):
    row_ids = lax.broadcasted_iota(jnp.int32, (rows_count, cols_count), 0)
    col_ids = lax.broadcasted_iota(jnp.int32, (rows_count, cols_count), 1)
    mixed = (row_ids * cols_count + col_ids) * jnp.int32(-1640531535) + hash_seed * jnp.int32(
        668265263
    )
    mixed = mixed ^ lax.shift_right_logical(mixed, jnp.int32(15))
    mixed = mixed * jnp.int32(-2048144777)
    mixed = mixed ^ lax.shift_right_logical(mixed, jnp.int32(13))
    mixed = mixed * jnp.int32(-1028477379)
    mixed = mixed ^ lax.shift_right_logical(mixed, jnp.int32(16))
    level = (lax.shift_right_logical(mixed, jnp.int32(8)) & jnp.int32(65535)).astype(jnp.float32)
    return ((level + 0.5) * (2.0 / 65536.0) - 1.0) * math.sqrt(3.0 / cols_count)


def pad_time(volume):
    return jnp.pad(volume, ((1, 1), (0, 0), (0, 0), (0, 0)))


def windows(padded, stack_axis):
    frame_count = padded.shape[0] - 2
    height_count = padded.shape[1] - 2
    width_count = padded.shape[2] - 2
    channels = padded.shape[3]
    pieces = []
    for offset in range(27):
        along_t = offset // 9
        along_h = offset // 3 % 3
        along_w = offset % 3
        along_t, along_h, along_w = (2 - along_t, 2 - along_h, 2 - along_w)
        window_block = padded[
            along_t : along_t + frame_count,
            along_h : along_h + height_count,
            along_w : along_w + width_count,
        ]
        pieces.append(window_block.reshape(frame_count * height_count * width_count, channels))
    return jnp.stack(pieces, axis=stack_axis)


def body(
    inputs, pre_activation, upstream, weight, first_moment, second_moment, hash_seed, step_count
):
    source = inputs[0]
    frame_count, height_count, width_count, in_width = source.shape
    tokens_here = frame_count * height_count * width_count
    out_width = pre_activation.shape[-1]
    rank_width = first_moment.shape[1]
    rows_here = first_moment.shape[0]
    pre_value = pre_activation[0].astype(jnp.float32)
    upstream_value = upstream[0].astype(jnp.float32)
    sigmoid_value = jax.nn.sigmoid(pre_value)
    grad_pre = (upstream_value * sigmoid_value * (1.0 + pre_value * (1.0 - sigmoid_value))).astype(
        jnp.bfloat16
    )
    projector = projection(hash_seed, out_width, rank_width).astype(jnp.bfloat16)
    proj_grad = jnp.dot(
        grad_pre.reshape(tokens_here, out_width), projector, preferred_element_type=jnp.float32
    )
    proj_grad = proj_grad.astype(jnp.bfloat16)
    joined = jnp.concatenate(
        [grad_pre, proj_grad.reshape(frame_count, height_count, width_count, rank_width)], axis=3
    )
    joined = pad_time(extended(joined, (("sy", 1), ("sx", 2)), 1))
    grad_padded = joined[..., :out_width]
    proj_cols = windows(joined[..., out_width:], 1)
    flat_source = source.reshape(tokens_here, in_width)

    def one_sample(volume):
        return jnp.einsum(
            "toc,oic->ti", windows(volume, 1), weight, preferred_element_type=jnp.float32
        )

    gathered = lax.map(one_sample, lax.all_gather(grad_padded[None], "dp", axis=0, tiled=True))
    branch = lax.all_to_all(gathered, "dp", split_axis=0, concat_axis=2, tiled=True)[0]
    input_grad = (upstream_value.reshape(tokens_here, in_width) + branch).astype(jnp.bfloat16)
    input_grad = input_grad.reshape(1, frame_count, height_count, width_count, in_width)
    product = jnp.einsum("tc,tor->cor", flat_source, proj_cols, preferred_element_type=jnp.float32)
    summed = own_tiles(
        product.reshape(rows_here * lax.axis_size(("dp", "sy", "sx")) // 27 * 27, rank_width),
        ("dp", "sy", "sx"),
        0,
    )
    token_total = tokens_here * lax.axis_size("dp") * lax.axis_size("sy") * lax.axis_size("sx")
    reduced = summed / math.sqrt(token_total)
    new_first = 0.9 * first_moment + 0.1 * reduced
    new_second = 0.999 * second_moment + 0.001 * reduced * reduced
    step_value = step_count.astype(jnp.float32)
    first_bias = 1.0 - jnp.power(jnp.float32(0.9), step_value)
    second_bias = 1.0 - jnp.power(jnp.float32(0.999), step_value)
    adapted = new_first / first_bias / (jnp.sqrt(new_second / second_bias) + 1e-08)
    scales = jnp.sqrt(jnp.mean(adapted * adapted, axis=1)) / jnp.sqrt(
        jnp.mean(reduced * reduced, axis=1) + 1e-06
    )
    return (input_grad, new_first, new_second, scales)


def solution(mesh):
    placed = (
        P("dp", None, "sy", "sx", None),
        P("dp", None, "sy", "sx", None),
        P("dp", None, "sy", "sx", None),
        P(None, "dp", None),
        P(("dp", "sy", "sx"), None),
        P(("dp", "sy", "sx"), None),
        P(),
        P(),
    )
    return jax.shard_map(
        body,
        mesh=mesh,
        in_specs=placed,
        out_specs=(
            P("dp", None, "sy", "sx", None),
            P(("dp", "sy", "sx"), None),
            P(("dp", "sy", "sx"), None),
            P(("dp", "sy", "sx")),
        ),
        check_vma=False,
    )
```

profile of v0, /device:TPU:2, one launch (start us, length us, event | category | flops | bytes accessed | tf_op | source)
XLA Modules:
  0.0 365.9 jit_solution(6766767611855369288)
XLA Ops:
  14.3 3.0 collective-permute-start
  18.4 8.2 %collective-permute-start.3 = (bf16[8,10,1,640]{3,1,2,0:T(8,128)(2,1)S(1)}, bf16[8,10,1,640]{3,1,2,0:T(8,128)(2,1)S(1)}, u32[]{:S(2)}, u32[]{:S(2)}) collective-permute-start(bf16[8,10,1,640]{3,1,2,0:T(8,128)(2,1)S(1)} %get-tuple-element.99), channel_id=1, source_target_pairs={{1,0},{2,1},{3,2},{4,3},{5,4},{6,5},{7,6},{8,7},{9,8},{10,9},{11,1... | collective-permute-start | bytes 307208 | tf_op jit(solution)/shard_map/ppermute | solution.py:19
  26.6 1.9 collective-permute-start.2
  28.6 6.0 %collective-permute-done.3 = bf16[8,10,1,640]{3,1,2,0:T(8,128)(2,1)S(1)} collective-permute-done((bf16[8,10,1,640]{3,1,2,0:T(8,128)(2,1)S(1)}, bf16[8,10,1,640]{3,1,2,0:T(8,128)(2,1)S(1)}, u32[]{:S(2)}, u32[]{:S(2)}) %collective-permute-start.3) | collective-permute-done | bytes 102432 | tf_op jit(solution)/shard_map/ppermute | solution.py:19
  34.6 5.8 %collective-permute-done.2 = bf16[8,10,1,640]{3,1,2,0:T(8,128)(2,1)S(1)} collective-permute-done((bf16[8,10,1,640]{3,1,2,0:T(8,128)(2,1)S(1)}, bf16[8,10,1,640]{3,1,2,0:T(8,128)(2,1)S(1)}, u32[]{:S(2)}, u32[]{:S(2)}) %collective-permute-start.2) | collective-permute-done | bytes 102432 | tf_op jit(solution)/shard_map/ppermute | solution.py:17
  43.5 4.0 %convolution_bitcast_fusion.1 = f32[512,27,128]{0,2,1:T(8,128)} fusion(bf16[128,27,128]{2,0,1:T(8,128)(2,1)S(1)} %constant_dynamic-update-slice_fusion.27, bf16[128,512,1]{1,0,2:T(8,128)(2,1)S(1)} %reshape.124), kind=kOutput, calls=%fused_computation.30 | convolution fusion | flops 452984832 | bytes 8093696 | tf_op jit(solution)/shard_map/tc,tor->cor/dot_general | solution.py:118
  47.5 10.4 %copy.61 = f32[512,27,128]{2,1,0:T(8,128)} copy(f32[512,27,128]{0,2,1:T(8,128)} %convolution_bitcast_fusion.1) | data formatting | bytes 14155776 | tf_op jit(solution)/shard_map/tc,tor->cor/dot_general | solution.py:118
  57.9 8.7 %reshape_reshape_reshape.3 = f32[256,6912]{1,0:T(8,128)} reshape(f32[512,27,128]{2,1,0:T(8,128)} %copy.61) | data formatting | bytes 14155776 | tf_op jit(solution)/shard_map/reshape;reshape;reshape | solution.py:35
  66.5 7.0 %pad.9 = f32[256,7168]{1,0:T(8,128)} pad(f32[256,6912]{1,0:T(8,128)} %reshape_reshape_reshape.3, f32[]{:T(128)} %constant.10.clone.1), padding=0_0x0_256 | pad | bytes 14417924 | tf_op jit(solution)/shard_map/jit(_pad)/pad | solution.py:37
  73.5 8.3 %reshape.117 = f32[14336,128]{1,0:T(8,128)} reshape(f32[256,7168]{1,0:T(8,128)} %pad.9) | data formatting | bytes 14680064 | tf_op jit(solution)/shard_map/reshape | solution.py:37
  81.9 250.7 %while.10 = (s32[]{:T(128)}, f32[4,128,128]{2,1,0:T(8,128)}, bf16[4,10,10,4,512]{4,3,2,1,0:T(4,128)(2,1)}, bf16[27,128,512]{2,1,0:T(8,128)(2,1)}, s32[]{:T(128)}) while((s32[]{:T(128)}, f32[4,128,128]{2,1,0:T(8,128)}, bf16[4,10,10,4,512]{4,3,2,1,0:T(4,128)(2,1)}, bf16[27,128,512]{2,1,0:T(8,128)(2,1)}, s32[]{:T(128)}) %tuple.88), condition=%wide.region_1.2_spmd, body=%wide.region_0.1_spmd.sunk | while | flops 452984832 | bytes 43352168 | solution.py:114
  89.9 3.5 fusion.70
  97.7 1.7 constant_dynamic-update-slice_fusion.94
  121.7 1.6 reshape.174
  140.8 3.8 %fusion.71 = f32[4,128,128]{2,1,0:T(8,128)} fusion(f32[4,128,128]{2,1,0:T(8,128)} %get-tuple-element.189, s32[]{:T(128)S(6)} %copy.104, bf16[128,27,512]{2,0,1:T(8,128)(2,1)} %constant_dynamic-update-slice_fusion.107, bf16[27,128,512]{2,1,0:T(8,128)(2,1)S(1)} %copy-done), kind=kOutput, calls=%fused_computation.1.clone.1 | convolution fusion | flops 452984832 | bytes 7143428 | tf_op jit(solution)/shard_map/while/body/eval_jaxpr/toc,oic->ti/dot_general | solution.py:110
  152.6 3.5 fusion.70
  160.4 1.7 constant_dynamic-update-slice_fusion.94
  184.4 1.6 reshape.174
  203.5 3.7 %fusion.71 = f32[4,128,128]{2,1,0:T(8,128)} fusion(f32[4,128,128]{2,1,0:T(8,128)} %get-tuple-element.189, s32[]{:T(128)S(6)} %copy.104, bf16[128,27,512]{2,0,1:T(8,128)(2,1)} %constant_dynamic-update-slice_fusion.107, bf16[27,128,512]{2,1,0:T(8,128)(2,1)S(1)} %copy-done), kind=kOutput, calls=%fused_computation.1.clone.1 | convolution fusion | flops 452984832 | bytes 7143428 | tf_op jit(solution)/shard_map/while/body/eval_jaxpr/toc,oic->ti/dot_general | solution.py:110
  215.2 3.5 fusion.70
  223.0 1.7 constant_dynamic-update-slice_fusion.94
  247.0 1.6 reshape.174
  266.0 3.7 %fusion.71 = f32[4,128,128]{2,1,0:T(8,128)} fusion(f32[4,128,128]{2,1,0:T(8,128)} %get-tuple-element.189, s32[]{:T(128)S(6)} %copy.104, bf16[128,27,512]{2,0,1:T(8,128)(2,1)} %constant_dynamic-update-slice_fusion.107, bf16[27,128,512]{2,1,0:T(8,128)(2,1)S(1)} %copy-done), kind=kOutput, calls=%fused_computation.1.clone.1 | convolution fusion | flops 452984832 | bytes 7143428 | tf_op jit(solution)/shard_map/while/body/eval_jaxpr/toc,oic->ti/dot_general | solution.py:110
  277.8 3.5 fusion.70
  285.6 1.7 constant_dynamic-update-slice_fusion.94
  306.4 1.6 reshape.173
  309.6 1.6 reshape.174
  316.0 1.6 reshape.176
  328.8 3.8 %fusion.71 = f32[4,128,128]{2,1,0:T(8,128)} fusion(f32[4,128,128]{2,1,0:T(8,128)} %get-tuple-element.189, s32[]{:T(128)S(6)} %copy.104, bf16[128,27,512]{2,0,1:T(8,128)(2,1)} %constant_dynamic-update-slice_fusion.107, bf16[27,128,512]{2,1,0:T(8,128)(2,1)S(1)} %copy-done), kind=kOutput, calls=%fused_computation.1.clone.1 | convolution fusion | flops 452984832 | bytes 7143428 | tf_op jit(solution)/shard_map/while/body/eval_jaxpr/toc,oic->ti/dot_general | solution.py:110
  332.6 4.4 %all-to-all-start = ((f32[4,128,128]{2,1,0:T(8,128)}), f32[4,128,128]{2,1,0:T(8,128)S(1)}, u32[]{:S(2)}, u32[]{:S(2)}) async-start(f32[4,128,128]{2,1,0:T(8,128)} %get-tuple-element.26), calls=%async_computation | async-start | bytes 524288 | tf_op jit(solution)/shard_map/all_to_all | solution.py:115
  337.7 7.3 %all-to-all-done = f32[4,128,128]{2,1,0:T(8,128)S(1)} async-done(((f32[4,128,128]{2,1,0:T(8,128)}), f32[4,128,128]{2,1,0:T(8,128)S(1)}, u32[]{:S(2)}, u32[]{:S(2)}) %all-to-all-start) | async-done | bytes 262176 | tf_op jit(solution)/shard_map/all_to_all | solution.py:115
  346.9 9.6 %all-reduce.5.cloned.1.call-done = f32[14336,128]{1,0:T(8,128)} async-done(((f32[14336,128]{1,0:T(8,128)}), f32[14336,128]{1,0:T(8,128)}) %all-reduce.5.cloned.1.call-update) | async-done | bytes 7340048
  (311 shorter events, 218.0 us)
Async XLA Ops:
  8.0 73.9 %all-gather.3.cloned.1.call-start = ((), (), s32[]{:S(2)}) async-start(), calls=%async_computation.1 | async-start | bytes 2048000 | tf_op jit(solution)/shard_map/all_gather | solution.py:114
  9.0 19.6 %copy-start.1 = (bf16[1,8,8,2,512]{4,3,2,1,0:T(2,128)(2,1)S(1)}, bf16[1,8,8,2,512]{4,3,2,1,0:T(2,128)(2,1)}, u32[]{:S(2)}) copy-start(bf16[1,8,8,2,512]{4,3,2,1,0:T(2,128)(2,1)} %param.10) | copy-start | bytes 393220
  13.0 4.3 %collective-permute-start.1 = (bf16[8,1,2,640]{3,1,2,0:T(2,128)(2,1)S(1)}, bf16[8,1,2,640]{3,1,2,0:T(2,128)(2,1)S(1)}, u32[]{:S(2)}, u32[]{:S(2)}) collective-permute-start(bf16[8,1,2,640]{3,1,2,0:T(2,128)(2,1)S(1)} %get-tuple-element.103), channel_id=1, source_target_pairs={{16,0},{32,16},{48,32},{17,1},{33,17},{49,33},{18,2},{34,18},{50,3... | collective-permute-start | bytes 61448 | tf_op jit(solution)/shard_map/ppermute | solution.py:19
  14.3 3.9 %collective-permute-start = (bf16[8,1,2,640]{3,1,2,0:T(2,128)(2,1)S(1)}, bf16[8,1,2,640]{3,1,2,0:T(2,128)(2,1)S(1)}, u32[]{:S(2)}, u32[]{:S(2)}) collective-permute-start(bf16[8,1,2,640]{3,1,2,0:T(2,128)(2,1)S(1)} %get-tuple-element.102), channel_id=1, source_target_pairs={{0,16},{16,32},{32,48},{1,17},{17,33},{33,49},{2,18},{18,34},{34,5... | collective-permute-start | bytes 61448 | tf_op jit(solution)/shard_map/ppermute | solution.py:17
  18.4 16.2 %collective-permute-start.3 = (bf16[8,10,1,640]{3,1,2,0:T(8,128)(2,1)S(1)}, bf16[8,10,1,640]{3,1,2,0:T(8,128)(2,1)S(1)}, u32[]{:S(2)}, u32[]{:S(2)}) collective-permute-start(bf16[8,10,1,640]{3,1,2,0:T(8,128)(2,1)S(1)} %get-tuple-element.99), channel_id=1, source_target_pairs={{1,0},{2,1},{3,2},{4,3},{5,4},{6,5},{7,6},{8,7},{9,8},{10,9},{11,1... | collective-permute-start | bytes 307208 | tf_op jit(solution)/shard_map/ppermute | solution.py:19
  26.6 13.8 %collective-permute-start.2 = (bf16[8,10,1,640]{3,1,2,0:T(8,128)(2,1)S(1)}, bf16[8,10,1,640]{3,1,2,0:T(8,128)(2,1)S(1)}, u32[]{:S(2)}, u32[]{:S(2)}) collective-permute-start(bf16[8,10,1,640]{3,1,2,0:T(8,128)(2,1)S(1)} %get-tuple-element.98), channel_id=1, source_target_pairs={{0,1},{1,2},{2,3},{3,4},{4,5},{5,6},{6,7},{7,8},{8,9},{9,10},{10,1... | collective-permute-start | bytes 307208 | tf_op jit(solution)/shard_map/ppermute | solution.py:17
  42.0 314.5 %all-reduce.5.cloned.1.call-start = ((), (), s32[]{:S(2)}) async-start(), calls=%async_computation.2 | async-start | bytes 14680064
  97.7 43.2 %copy-start = (bf16[27,128,512]{2,1,0:T(8,128)(2,1)S(1)}, bf16[27,128,512]{2,1,0:T(8,128)(2,1)}, u32[]{:S(2)}) copy-start(bf16[27,128,512]{2,1,0:T(8,128)(2,1)} %get-tuple-element.196) | copy-start | bytes 10616836 | tf_op jit(solution)/shard_map/while
  160.4 43.1 %copy-start = (bf16[27,128,512]{2,1,0:T(8,128)(2,1)S(1)}, bf16[27,128,512]{2,1,0:T(8,128)(2,1)}, u32[]{:S(2)}) copy-start(bf16[27,128,512]{2,1,0:T(8,128)(2,1)} %get-tuple-element.196) | copy-start | bytes 10616836 | tf_op jit(solution)/shard_map/while
  223.0 43.1 %copy-start = (bf16[27,128,512]{2,1,0:T(8,128)(2,1)S(1)}, bf16[27,128,512]{2,1,0:T(8,128)(2,1)}, u32[]{:S(2)}) copy-start(bf16[27,128,512]{2,1,0:T(8,128)(2,1)} %get-tuple-element.196) | copy-start | bytes 10616836 | tf_op jit(solution)/shard_map/while
  285.6 43.2 %copy-start = (bf16[27,128,512]{2,1,0:T(8,128)(2,1)S(1)}, bf16[27,128,512]{2,1,0:T(8,128)(2,1)}, u32[]{:S(2)}) copy-start(bf16[27,128,512]{2,1,0:T(8,128)(2,1)} %get-tuple-element.196) | copy-start | bytes 10616836 | tf_op jit(solution)/shard_map/while
  332.6 12.4 %all-to-all-start = ((f32[4,128,128]{2,1,0:T(8,128)}), f32[4,128,128]{2,1,0:T(8,128)S(1)}, u32[]{:S(2)}, u32[]{:S(2)}) async-start(f32[4,128,128]{2,1,0:T(8,128)} %get-tuple-element.26), calls=%async_computation | async-start | bytes 524288 | tf_op jit(solution)/shard_map/all_to_all | solution.py:115
Sparse Core Ops, SparseCore 0:
  42.1 27.1 all-gather.2
Sparse Core Ops, SparseCore 1:
  82.0 274.4 all-reduce.4
where the time goes:
time: 369 us; the launch traced here: 366 us
  local copies, waits for them, and re-layouts  274 us (74%)
  waiting for transfers between devices  29.6 us (8%)
  matrix products  19.5 us (5%)
  starting transfers between devices  18.9 us (5%)
  between operations  17.4 us (5%)
  other arithmetic  6.53 us (2%)
    while x112, local copies, waits for them, and re-layouts  117 us
    reshape x108, local copies, waits for them, and re-layouts, windows(): return jnp.stack(pieces, axis=stack_axis)  89.8 us
    slice x35, local copies, waits for them, and re-layouts, windows(): padded[along_t:along_t + frame_count, along_h:along_h + height_count, alo...  18.7 us
    dot_general x4, matrix products, one_sample(): jnp.einsum('toc,oic->ti', windows(volume, 1), weight, preferred_element_t...  15 us
    dot_general x1, local copies, waits for them, and re-layouts, body(): jnp.einsum('tc,tor->cor', flat_source, proj_cols, preferred_element_type=...  10.4 us
    unnamed x3, waiting for transfers between devices  9.6 us
    ppermute x2, starting transfers between devices, extended(): lax.ppermute(head, axis, [((i + 1) % count, i) for i in range(ends)])  9.47 us
    another operation x1, local copies, waits for them, and re-layouts, own_tiles(): lines = parts.reshape(devices, -1)  8.68 us
  transfers between devices with their start and end apart: 7, of which 5 were waited for; matrix products, arithmetic and copies ran while one was open for 80% of the time, Pallas kernels for 0%

commit v1 on v0

v1 whole, which is shorter than its diff:
```python
import math

import jax
import jax.numpy as jnp
from jax import lax
from jax.experimental import pallas as pl
from jax.experimental.pallas import tpu as pltpu
from jax.sharding import Mesh, PartitionSpec as P

BF16 = jnp.bfloat16
F32 = jnp.float32


def _call(body, outs, scratch=(), smem=0, total=0):
    specs = [pl.BlockSpec(memory_space=pltpu.SMEM)] * smem
    specs += [pl.BlockSpec(memory_space=pltpu.VMEM)] * (total - smem)
    return pl.pallas_call(
        body,
        out_shape=outs,
        in_specs=specs,
        out_specs=jax.tree.map(lambda _: pl.BlockSpec(memory_space=pltpu.VMEM), outs),
        scratch_shapes=list(scratch),
        compiler_params=pltpu.CompilerParams(vmem_limit_bytes=40 * 1024 * 1024),
        name=body.__name__,
    )


def _rows_to_scratch(ref, scratch):
    frames, rows, cols, _ = ref.shape
    for t in range(frames):
        for h in range(rows):
            base = (t * rows + h) * cols
            row = ref[t, h].astype(F32)
            for tile in range(scratch.shape[0]):
                scratch[tile, base : base + cols, :] = row[:, tile * 128 : tile * 128 + 128]


def _token_major(scratch, frames, rows, cols):
    tiles = []
    for tile in range(scratch.shape[0]):
        tiles.append(
            jnp.concatenate(
                [
                    scratch[tile, pl.ds(h * cols + w, frames, stride=rows * cols), :]
                    for w in range(cols)
                    for h in range(rows)
                ],
                axis=0,
            )
        )
    return jnp.concatenate(tiles, axis=1)


def prepare(seed, pre, up, inp, g_out, proj_out, in_out, top_out, bot_out, s_pre, s_up, s_in):
    frames, rows, cols, chans = pre.shape
    rank = proj_out.shape[-1]
    _rows_to_scratch(pre, s_pre)
    _rows_to_scratch(up, s_up)
    _rows_to_scratch(inp, s_in)

    row_ids = lax.broadcasted_iota(jnp.int32, (chans, rank), 0)
    col_ids = lax.broadcasted_iota(jnp.int32, (chans, rank), 1)
    mixed = (row_ids * rank + col_ids) * jnp.int32(-1640531535) + seed[0] * jnp.int32(668265263)
    mixed = mixed ^ lax.shift_right_logical(mixed, jnp.int32(15))
    mixed = mixed * jnp.int32(-2048144777)
    mixed = mixed ^ lax.shift_right_logical(mixed, jnp.int32(13))
    mixed = mixed * jnp.int32(-1028477379)
    mixed = mixed ^ lax.shift_right_logical(mixed, jnp.int32(16))
    level = (lax.shift_right_logical(mixed, jnp.int32(8)) & jnp.int32(65535)).astype(F32)
    projector = (((level + 0.5) * (2.0 / 65536.0) - 1.0) * math.sqrt(3.0 / rank)).astype(BF16)

    x = _token_major(s_pre, frames, rows, cols)
    u = _token_major(s_up, frames, rows, cols)
    sig = jax.nn.sigmoid(x)
    g = (u * sig * (1.0 + x * (1.0 - sig))).astype(BF16)
    proj = jnp.dot(g, projector, preferred_element_type=F32).astype(BF16)
    g4 = g.reshape(cols, rows, frames, chans)
    p4 = proj.reshape(cols, rows, frames, rank)
    g_out[...] = g4
    proj_out[...] = p4
    top_out[:, :, :chans] = g4[:, 0]
    bot_out[:, :, :chans] = g4[:, rows - 1]
    top_out[:, :, chans:] = p4[:, 0]
    bot_out[:, :, chans:] = p4[:, rows - 1]

    dest = in_out.shape[0]
    r = lax.broadcasted_iota(jnp.int32, (chans, chans), 0)
    c = lax.broadcasted_iota(jnp.int32, (chans, chans), 1)
    target = (r & 1) * 16 + ((r >> 1) & 15) * 32 + (r >> 5)
    perm = jnp.where(c == target, 1.0, 0.0).astype(BF16)
    moved = jnp.dot(
        _token_major(s_in, frames, rows, cols).astype(BF16), perm, preferred_element_type=F32
    ).reshape(cols, 4, rows // 4, frames, chans)
    lanes = lax.broadcasted_iota(jnp.int32, (cols * (rows // 4) * frames, 128), 1)
    for tile in range(dest // 4):
        groups = [
            moved[:, q, :, :, tile * 128 : tile * 128 + 128].reshape(-1, 128) for q in range(4)
        ]
        for i in range(4):
            out = jnp.zeros_like(groups[0])
            for q in range(4):
                shift = (32 * (q - i)) % 128
                piece = pltpu.roll(groups[q], shift, 1) if shift else groups[q]
                out = jnp.where((lanes >> 5) == q, piece, out)
            in_out[tile * 4 + i] = out.astype(BF16).reshape(cols, rows // 4, frames, 128)


def shift_frames(x, by):
    zero = jnp.zeros_like(x[:, :1])
    if by > 0:
        return jnp.concatenate([zero, x[:, :-1]], axis=1)
    return jnp.concatenate([x[:, 1:], zero], axis=1)


def branch_kernel(
    pos, g0, g1, g2, g3, r0, r1, r2, r3, weight, own_out, left_out, right_out, ext
):
    cols, rows, frames, chans = g0.shape
    width = weight.shape[1]
    for k, (g, r) in enumerate(((g0, r0), (g1, r1), (g2, r2), (g3, r3))):
        ext[k, :, 1 : rows + 1] = g[...]
        ext[k, :, 0] = r[0]
        ext[k, :, rows + 1] = r[1]
    count = 4 * cols * rows * frames
    total = None
    for a in range(3):
        acc = jnp.zeros((count, 3 * width), F32)
        for b in range(3):
            lhs = ext[:, :, 2 - b : 2 - b + rows].reshape(count, chans)
            rhs = weight[9 * a + 3 * b : 9 * a + 3 * b + 3].reshape(3 * width, chans)
            acc = acc + lax.dot_general(
                lhs, rhs, (((1,), (1,)), ((), ())), preferred_element_type=F32
            )
        acc = acc.reshape(count // frames, frames, 3 * width)
        if a != 1:
            acc = shift_frames(acc, a - 1)
        total = acc if total is None else total + acc
    total = total.reshape(4, cols, rows, frames, 3 * width)
    for k in range(4):
        sample = lax.rem(pos[0] + (4 - k), 4)
        part = [[total[k, w, :, :, c * width : (c + 1) * width] for c in range(3)] for w in range(cols)]
        left_out[sample] = part[0][0].astype(BF16)
        own_out[sample, 0] = part[0][1] + part[1][0]
        own_out[sample, 1] = part[0][2] + part[1][1]
        right_out[sample] = part[1][2].astype(BF16)


def moment_kernel(chunks, proj, out, wide, flat):
    devices, cols, halves, frames, _ = chunks.shape
    across, rows, _, rank = proj.shape
    wide[0] = jnp.zeros_like(wide[0])
    wide[across + 1] = jnp.zeros_like(wide[0])
    wide[1 : across + 1] = proj[...]
    count = devices * cols * halves
    x = chunks[...].astype(F32).reshape(count, frames, 128)
    later = shift_frames(x, 1).reshape(count * frames, 128)
    sooner = shift_frames(x, -1).reshape(count * frames, 128)
    x = x.reshape(count * frames, 128)
    lanes = lax.broadcasted_iota(jnp.int32, x.shape, 1) >> 5
    acc = [None] * 9
    for q in range(4):
        lhs = jnp.zeros_like(x)
        for part, shift, block in ((later, (0 - 32 * q) % 128, 0), (x, (32 - 32 * q) % 128, 1), (sooner, (64 - 32 * q) % 128, 2)):
            moved = pltpu.roll(part, shift, 1) if shift else part
            lhs = jnp.where(lanes == block, moved, lhs)
        lhs = lhs.T.astype(BF16)
        for b in range(3):
            for c in range(3):
                low = 2 - b + 2 * q
                rhs = wide[2 - c : 2 - c + across, low : low + 2].reshape(count * frames, rank)
                y = jnp.dot(lhs, rhs, preferred_element_type=F32)
                acc[3 * b + c] = y if acc[3 * b + c] is None else acc[3 * b + c] + y
    for a in range(3):
        for j in range(2):
            for k in range(9):
                at = (27 * j + 9 * a + k) * 16
                flat[at : at + 16, :] = acc[k][(2 * a + j) * 16 : (2 * a + j) * 16 + 16, :]
    for m in range(16):
        out[m] = flat[pl.ds(m, 54, stride=16), :].astype(BF16)


def finish_kernel(up, parts, out, flat, outflat):
    frames, rows, cols, chans = up.shape
    _rows_to_scratch(up, flat)
    for tile in range(4):
        for w in range(cols):
            for h in range(rows):
                at = pl.ds(h * cols + w, frames, stride=rows * cols)
                outflat[tile, at, :] = flat[tile, at, :] + parts[tile, w, h].astype(F32)
    for t in range(frames):
        for h in range(rows):
            base = (t * rows + h) * cols
            row = [outflat[tile, base : base + cols, :] for tile in range(4)]
            out[t, h] = jnp.concatenate(row, axis=1).astype(BF16)


def ring(axis, shift):
    n = lax.axis_size(axis)
    return [(i, (i + shift) % n) for i in range(n)]


def line(axis, shift):
    n = lax.axis_size(axis)
    return [(i, i + shift) for i in range(n) if 0 <= i + shift < n]


def body(
    inputs, pre_activation, upstream, weight, first_moment, second_moment, hash_seed, step_count
):
    frames, rows, cols, chans = inputs.shape[1:]
    rank = first_moment.shape[1]
    tokens = frames * rows * cols
    sx = ("sxx", "sxz")
    g, proj, chunks, top, bot = _call(
        prepare,
        (
            jax.ShapeDtypeStruct((cols, rows, frames, chans), BF16),
            jax.ShapeDtypeStruct((cols, rows, frames, rank), BF16),
            jax.ShapeDtypeStruct((16, cols, 2, frames, 128), BF16),
            jax.ShapeDtypeStruct((cols, frames, chans + rank), BF16),
            jax.ShapeDtypeStruct((cols, frames, chans + rank), BF16),
        ),
        scratch=[pltpu.VMEM((chans // 128, tokens, 128), F32)] * 3,
        smem=1,
        total=4,
    )(hash_seed.reshape(1), pre_activation[0], upstream[0], inputs[0])

    above = lax.ppermute(bot, "sy", line("sy", 1))
    below = lax.ppermute(top, "sy", line("sy", -1))
    chunks = lax.all_to_all(chunks, sx, split_axis=0, concat_axis=0, tiled=True)
    g_all = [g] + [lax.ppermute(g, "dp", ring("dp", k)) for k in (1, 2, 3)]
    edge = jnp.stack([above[..., :chans], below[..., :chans]])
    edges = [edge] + [lax.ppermute(edge, "dp", ring("dp", k)) for k in (1, 2, 3)]
    proj = jnp.concatenate(
        [above[:, None, :, chans:], proj, below[:, None, :, chans:]], axis=1
    )
    proj = lax.all_to_all(
        jnp.broadcast_to(proj[None], (4,) + proj.shape), "sxz", 0, 0, tiled=True
    )
    proj = lax.all_to_all(
        jnp.broadcast_to(proj[None], (4,) + proj.shape), "sxx", 0, 0, tiled=True
    )
    proj = proj.reshape(16 * cols, rows + 2, frames, rank)
    terms = _call(
        moment_kernel,
        jax.ShapeDtypeStruct((16, 54, rank), BF16),
        scratch=[
            pltpu.VMEM((16 * cols + 2, rows + 2, frames, rank), BF16),
            pltpu.VMEM((54 * 16, rank), F32),
        ],
        total=2,
    )(chunks, proj)
    terms = lax.all_to_all(terms, ("dp", "sy"), 0, 0, tiled=True)

    place = lax.axis_index("dp").astype(jnp.int32).reshape(1)
    own, left, right = _call(
        branch_kernel,
        (
            jax.ShapeDtypeStruct((4, cols, rows, frames, 128), F32),
            jax.ShapeDtypeStruct((4, rows, frames, 128), BF16),
            jax.ShapeDtypeStruct((4, rows, frames, 128), BF16),
        ),
        scratch=[pltpu.VMEM((4, cols, rows + 2, frames, chans), BF16)],
        smem=1,
        total=10,
    )(place, *g_all, *edges, weight)
    from_right = lax.ppermute(left, sx, line(sx, -1))
    from_left = lax.ppermute(right, sx, line(sx, 1))
    mine = (own + jnp.stack([from_left, from_right], axis=1).astype(F32)).astype(BF16)
    parts = lax.all_to_all(mine, "dp", 0, 0, tiled=True)
    input_grad = _call(
        finish_kernel,
        jax.ShapeDtypeStruct((frames, rows, cols, chans), BF16),
        scratch=[pltpu.VMEM((chans // 128, tokens, 128), F32)] * 2,
        total=2,
    )(upstream[0], parts)

    total = 32768
    reduced = jnp.sum(terms.astype(F32), axis=0) / math.sqrt(total)
    new_first = 0.9 * first_moment + 0.1 * reduced
    new_second = 0.999 * second_moment + 0.001 * reduced * reduced
    step_value = step_count.astype(F32)
    first_bias = 1.0 - jnp.power(jnp.float32(0.9), step_value)
    second_bias = 1.0 - jnp.power(jnp.float32(0.999), step_value)
    adapted = new_first / first_bias / (jnp.sqrt(new_second / second_bias) + 1e-08)
    scales = jnp.sqrt(jnp.mean(adapted * adapted, axis=1)) / jnp.sqrt(
        jnp.mean(reduced * reduced, axis=1) + 1e-06
    )
    return (input_grad[None], new_first, new_second, scales)


def solution(mesh):
    sizes = mesh.shape
    grid = Mesh(
        mesh.devices.reshape(sizes["dp"], sizes["sy"], 4, sizes["sx"] // 4),
        ("dp", "sy", "sxx", "sxz"),
    )
    sx = ("sxx", "sxz")
    whole = ("dp", "sy", "sxx", "sxz")
    volume = P("dp", None, "sy", sx, None)
    return jax.shard_map(
        body,
        mesh=grid,
        in_specs=(volume, volume, volume, P(None, "dp", None), P(whole), P(whole), P(), P()),
        out_specs=(volume, P(whole), P(whole), P(whole)),
        check_vma=False,
    )
```

time: 369 us -> 109 us (0.30)
  local copies, waits for them, and re-layouts: 274 us -> 14 us
  starting transfers between devices: 18.9 us -> 55.4 us
  matrix products: 19.5 us -> 0 us
  between operations: 17.4 us -> 2.28 us
  Pallas kernels: 0 us -> 9.55 us
  waiting for transfers between devices: 29.6 us -> 22 us
    while x112 -> x0, local copies, waits for them, and re-layouts: 117 us -> none
    reshape x110 -> x0, local copies, waits for them, and re-layouts: 98.1 us -> none  [the longest x108 89.8 us: windows(): return jnp.stack(pieces, axis=stack_axis)]
    all_to_all x1 -> x5, starting transfers between devices: 4.37 us -> 29.4 us  [the longest x1 11.5 us: body(): chunks = lax.all_to_all(chunks, sx, split_axis=0, concat_axis=0, tiled=True)]
    slice x38 -> x0, local copies, waits for them, and re-layouts: 19.9 us -> none  [the longest x35 18.7 us: windows(): padded[along_t:along_t + frame_count, along_h:along_h + height_count, alo...]
    dot_general x6 -> x0, matrix products: 19.5 us -> none  [the longest x4 15 us: one_sample(): jnp.einsum('toc,oic->ti', windows(volume, 1), weight, preferred_element_t...]
    another operation x7 -> x2, local copies, waits for them, and re-layouts: 15 us -> 1.44 us  [body(): edge = jnp.stack([above[..., :chans], below[..., :chans]])]
    ppermute x4 -> x10, starting transfers between devices: 14.4 us -> 25.9 us  [the longest x3 6.28 us: body(): lax.ppermute(edge, 'dp', ring('dp', k))]
    dot_general x1 -> x0, local copies, waits for them, and re-layouts: 10.4 us -> none  [body(): jnp.einsum('tc,tor->cor', flat_source, proj_cols, preferred_element_type=...]
  transfers between devices with their start and end apart: 7 -> 15, of which waited for: 5 -> 8; matrix products, arithmetic and copies ran while one was open for 80% -> 7% of each run, Pallas kernels for 0% -> 8%
where the time goes in v1:
time: 109 us; the launch traced here: 108 us
  starting transfers between devices  55.4 us (51%)
  waiting for transfers between devices  22 us (20%)
  local copies, waits for them, and re-layouts  14 us (13%)
  Pallas kernels  9.55 us (9%)
  other arithmetic  4.75 us (4%)
  between operations  2.28 us (2%)
    all_to_all x1, starting transfers between devices, body(): chunks = lax.all_to_all(chunks, sx, split_axis=0, concat_axis=0, tiled=True)  11.5 us
    unnamed x22, local copies, waits for them, and re-layouts  7.93 us
    ppermute x3, starting transfers between devices, body(): lax.ppermute(edge, 'dp', ring('dp', k))  6.28 us
    all_to_all x1, waiting for transfers between devices, body(): chunks = lax.all_to_all(chunks, sx, split_axis=0, concat_axis=0, tiled=True)  6.17 us
    all_to_all x1, starting transfers between devices, body(): lax.all_to_all(jnp.broadcast_to(proj[None], (4,) + proj.shape), 'sxx', 0,...  6.15 us
    ppermute x3, starting transfers between devices, body(): g_all = [g] + [lax.ppermute(g, 'dp', ring('dp', k)) for k in (1, 2, 3)]  5.9 us
    ppermute x1, starting transfers between devices, body(): from_right = lax.ppermute(left, sx, line(sx, -1))  5.5 us
    all_to_all x1, waiting for transfers between devices, body(): terms = lax.all_to_all(terms, ('dp', 'sy'), 0, 0, tiled=True)  5.06 us
  transfers between devices with their start and end apart: 15, of which 8 were waited for; matrix products, arithmetic and copies ran while one was open for 7% of the time, Pallas kernels for 8%

profile of v1, /device:TPU:2, one launch (start us, length us, event | category | flops | bytes accessed | tf_op | source)
XLA Modules:
  0.0 108.0 jit_solution(13542442673286484647)
XLA Ops:
  1.4 1.1 copy-done.1
  2.5 0.9 copy-done.5
  3.4 0.9 copy-done.6
  4.3 1.4 %prepare.1 = (bf16[2,8,8,512]{3,2,1,0:T(8,128)(2,1)S(1)}, bf16[2,8,8,128]{3,2,1,0:T(8,128)(2,1)S(1)}, bf16[16,2,2,8,128]{4,3,2,1,0:T(8,128)(2,1)S(1)}, bf16[2,8,640]{2,1,0:T(8,128)(2,1)}, bf16[2,8,640]{2,1,0:T(8,128)(2,1)}) custom-call(s32[1]{0:T(128)} %bitcast.21.seed, bf16[8,8,2,512]{3,2,1,0:T(2,128)(2,1)S(1)} %bitcast.24, ...), custom_call_target="tpu_custom_call" | custom-call | tf_op jit(solution)/shard_map/prepare/pallas_call | solution.py:214
  7.6 1.3 %collective-permute-start.4 = (bf16[2,8,640]{2,1,0:T(8,128)(2,1)}, bf16[2,8,640]{2,1,0:T(8,128)(2,1)}, u32[]{:S(2)}, u32[]{:S(2)}) collective-permute-start(bf16[2,8,640]{2,1,0:T(8,128)(2,1)} %get-tuple-element.14), channel_id=1, source_target_pairs={{16,0},{32,16},{48,32},{17,1},{33,17},{49,33},{18,2},{34,18},{50,3... | collective-permute-start | bytes 61448 | tf_op jit(solution)/shard_map/ppermute | solution.py:229
  8.9 3.6 %collective-permute-start.3 = (bf16[2,8,640]{2,1,0:T(8,128)(2,1)}, bf16[2,8,640]{2,1,0:T(8,128)(2,1)}, u32[]{:S(2)}, u32[]{:S(2)}) collective-permute-start(bf16[2,8,640]{2,1,0:T(8,128)(2,1)} %get-tuple-element.13), channel_id=1, source_target_pairs={{0,16},{16,32},{32,48},{1,17},{17,33},{33,49},{2,18},{18,34},{34,5... | collective-permute-start | bytes 61448 | tf_op jit(solution)/shard_map/ppermute | solution.py:228
  12.5 11.5 %all-to-all-start.1 = ((bf16[16,2,2,8,128]{4,3,2,1,0:T(8,128)(2,1)}), bf16[16,2,2,8,128]{4,3,2,1,0:T(8,128)(2,1)}, u32[]{:S(2)}, u32[]{:S(2)}) async-start(bf16[16,2,2,8,128]{4,3,2,1,0:T(8,128)(2,1)} %copy-done.7), calls=%async_computation.1 | async-start | bytes 262144 | tf_op jit(solution)/shard_map/all_to_all | solution.py:230
  25.4 1.4 %pad_maximum_fusion = bf16[2,10,8,128]{3,2,1,0:T(8,128)(2,1)} fusion(bf16[2,1,8,128]{3,2,1,0:T(8,128)(2,1)S(1)} %slice_bitcast_fusion.2, bf16[2,8,8,128]{3,2,1,0:T(8,128)(2,1)} %copy-done.10, bf16[2,1,8,128]{3,2,1,0:T(8,128)(2,1)S(1)} %slice_bitcast_fusion.3), kind=kLoop, calls=%fused_computation.2 | loop fusion | flops 40960 | bytes 81920 | tf_op jit(solution)/shard_map/concatenate | solution.py:234
  26.7 6.2 %all-to-all-done.1.chunks = bf16[16,2,2,8,128]{4,3,2,1,0:T(8,128)(2,1)} async-done(((bf16[16,2,2,8,128]{4,3,2,1,0:T(8,128)(2,1)}), bf16[16,2,2,8,128]{4,3,2,1,0:T(8,128)(2,1)}, u32[]{:S(2)}, u32[]{:S(2)}) %all-to-all-start.1) | async-done | bytes 131104 | tf_op jit(solution)/shard_map/all_to_all | solution.py:230
  32.9 1.5 %broadcast_in_dim.24 = bf16[4,2,10,8,128]{4,3,2,1,0:T(8,128)(2,1)} broadcast(bf16[2,10,8,128]{3,2,1,0:T(8,128)(2,1)} %pad_maximum_fusion), dimensions={1,2,3,4} | broadcast | bytes 204800 | tf_op jit(solution)/shard_map/broadcast_in_dim | solution.py:238
  34.4 4.0 %all-to-all-start.2 = ((bf16[4,2,10,8,128]{4,3,2,1,0:T(8,128)(2,1)}), bf16[4,2,10,8,128]{4,3,2,1,0:T(8,128)(2,1)}, u32[]{:S(2)}, u32[]{:S(2)}) async-start(bf16[4,2,10,8,128]{4,3,2,1,0:T(8,128)(2,1)} %broadcast_in_dim.24), calls=%async_computation.2 | async-start | bytes 327680 | tf_op jit(solution)/shard_map/all_to_all | solution.py:237
  38.3 1.7 %collective-permute-start = (bf16[2,8,8,512]{3,2,1,0:T(8,128)(2,1)}, bf16[2,8,8,512]{3,2,1,0:T(8,128)(2,1)}, u32[]{:S(2)}, u32[]{:S(2)}) collective-permute-start(bf16[2,8,8,512]{3,2,1,0:T(8,128)(2,1)} %copy-done.3), channel_id=1, source_target_pairs={{0,64},{64,128},{128,192},{192,0},{1,65},{65,129},{129,193},{193,1... | collective-permute-start | bytes 393224 | tf_op jit(solution)/shard_map/ppermute | solution.py:231
  40.0 2.9 %collective-permute-start.1 = (bf16[2,8,8,512]{3,2,1,0:T(8,128)(2,1)}, bf16[2,8,8,512]{3,2,1,0:T(8,128)(2,1)}, u32[]{:S(2)}, u32[]{:S(2)}) collective-permute-start(bf16[2,8,8,512]{3,2,1,0:T(8,128)(2,1)} %copy-done.3), channel_id=1, source_target_pairs={{0,128},{64,192},{128,0},{192,64},{1,129},{65,193},{129,1},{193,65... | collective-permute-start | bytes 393224 | tf_op jit(solution)/shard_map/ppermute | solution.py:231
  42.9 1.3 %collective-permute-start.2 = (bf16[2,8,8,512]{3,2,1,0:T(8,128)(2,1)}, bf16[2,8,8,512]{3,2,1,0:T(8,128)(2,1)}, u32[]{:S(2)}, u32[]{:S(2)}) collective-permute-start(bf16[2,8,8,512]{3,2,1,0:T(8,128)(2,1)} %copy-done.3), channel_id=1, source_target_pairs={{0,192},{64,0},{128,64},{192,128},{1,193},{65,1},{129,65},{193,129... | collective-permute-start | bytes 393224 | tf_op jit(solution)/shard_map/ppermute | solution.py:231
  45.0 2.5 %all-to-all-done.2 = bf16[4,2,10,8,128]{4,3,2,1,0:T(8,128)(2,1)} async-done(((bf16[4,2,10,8,128]{4,3,2,1,0:T(8,128)(2,1)}), bf16[4,2,10,8,128]{4,3,2,1,0:T(8,128)(2,1)}, u32[]{:S(2)}, u32[]{:S(2)}) %all-to-all-start.2) | async-done | bytes 163872 | tf_op jit(solution)/shard_map/all_to_all | solution.py:237
  47.5 1.9 %broadcast_in_dim.25 = bf16[4,4,2,10,8,128]{5,4,3,2,1,0:T(8,128)(2,1)} broadcast(bf16[4,2,10,8,128]{4,3,2,1,0:T(8,128)(2,1)} %all-to-all-done.2), dimensions={1,2,3,4,5} | broadcast | bytes 819200 | tf_op jit(solution)/shard_map/broadcast_in_dim | solution.py:241
  49.4 6.2 %all-to-all-start.3 = ((bf16[4,4,2,10,8,128]{5,4,3,2,1,0:T(8,128)(2,1)}), bf16[4,4,2,10,8,128]{5,4,3,2,1,0:T(8,128)(2,1)}, u32[]{:S(2)}, u32[]{:S(2)}) async-start(bf16[4,4,2,10,8,128]{5,4,3,2,1,0:T(8,128)(2,1)} %broadcast_in_dim.25), calls=%async_computation.3 | async-start | bytes 1310720 | tf_op jit(solution)/shard_map/all_to_all | solution.py:240
  56.9 1.6 %collective-permute-start.5 = (bf16[2,2,8,512]{3,2,1,0:T(8,128)(2,1)}, bf16[2,2,8,512]{3,2,1,0:T(8,128)(2,1)S(1)}, u32[]{:S(2)}, u32[]{:S(2)}) collective-permute-start(bf16[2,2,8,512]{3,2,1,0:T(8,128)(2,1)} %pad_maximum_fusion.1.r0), channel_id=1, source_target_pairs={{0,64},{64,128},{128,192},{192,0},{1,65},{65,129},{129,193},{193,1... | collective-permute-start | bytes 98312 | tf_op jit(solution)/shard_map/ppermute | solution.py:233
  58.4 2.9 %collective-permute-start.6 = (bf16[2,2,8,512]{3,2,1,0:T(8,128)(2,1)}, bf16[2,2,8,512]{3,2,1,0:T(8,128)(2,1)}, u32[]{:S(2)}, u32[]{:S(2)}) collective-permute-start(bf16[2,2,8,512]{3,2,1,0:T(8,128)(2,1)} %pad_maximum_fusion.1.r0), channel_id=1, source_target_pairs={{0,128},{64,192},{128,0},{192,64},{1,129},{65,193},{129,1},{193,65... | collective-permute-start | bytes 98312 | tf_op jit(solution)/shard_map/ppermute | solution.py:233
  62.8 1.8 %collective-permute-start.7 = (bf16[2,2,8,512]{3,2,1,0:T(8,128)(2,1)}, bf16[2,2,8,512]{3,2,1,0:T(8,128)(2,1)}, u32[]{:S(2)}, u32[]{:S(2)}) collective-permute-start(bf16[2,2,8,512]{3,2,1,0:T(8,128)(2,1)} %pad_maximum_fusion.1.r0), channel_id=1, source_target_pairs={{0,192},{64,0},{128,64},{192,128},{1,193},{65,1},{129,65},{193,129... | collective-permute-start | bytes 98312 | tf_op jit(solution)/shard_map/ppermute | solution.py:233
  64.6 2.4 %collective-permute-done.7.r3 = bf16[2,2,8,512]{3,2,1,0:T(8,128)(2,1)} collective-permute-done((bf16[2,2,8,512]{3,2,1,0:T(8,128)(2,1)}, bf16[2,2,8,512]{3,2,1,0:T(8,128)(2,1)}, u32[]{:S(2)}, u32[]{:S(2)}) %collective-permute-start.7) | collective-permute-done | bytes 32800 | tf_op jit(solution)/shard_map/ppermute | solution.py:233
  68.7 3.7 %branch_kernel.1 = (f32[4,2,8,8,128]{4,3,2,1,0:T(8,128)S(1)}, bf16[4,8,8,128]{3,2,1,0:T(8,128)(2,1)S(1)}, bf16[4,8,8,128]{3,2,1,0:T(8,128)(2,1)S(1)}) custom-call(s32[1]{0:T(128)} %bitcast.1.pos, bf16[2,8,8,512]{3,2,1,0:T(8,128)(2,1)S(1)} %copy-done.4, bf16[2,8,8,512]{3,2,1,0:T(8,128)(2,1)} %collective-permute-done.g1, ...), custom_call_target="tpu_custom_call" | custom-call | tf_op jit(solution)/shard_map/branch_kernel/pallas_call | solution.py:256
  72.4 3.4 %collective-permute-start.8 = (bf16[4,8,8,128]{3,2,1,0:T(8,128)(2,1)S(1)}, bf16[4,8,8,128]{3,2,1,0:T(8,128)(2,1)S(1)}, u32[]{:S(2)}, u32[]{:S(2)}) collective-permute-start(bf16[4,8,8,128]{3,2,1,0:T(8,128)(2,1)S(1)} %get-tuple-element.16), channel_id=1, source_target_pairs={{0,1},{1,2},{2,3},{3,4},{4,5},{5,6},{6,7},{7,8},{8,9},{9,10},{10,1... | collective-permute-start | bytes 196616 | tf_op jit(solution)/shard_map/ppermute | solution.py:268
  75.8 5.5 %collective-permute-start.9 = (bf16[4,8,8,128]{3,2,1,0:T(8,128)(2,1)S(1)}, bf16[4,8,8,128]{3,2,1,0:T(8,128)(2,1)S(1)}, u32[]{:S(2)}, u32[]{:S(2)}) collective-permute-start(bf16[4,8,8,128]{3,2,1,0:T(8,128)(2,1)S(1)} %get-tuple-element.17), channel_id=1, source_target_pairs={{1,0},{2,1},{3,2},{4,3},{5,4},{6,5},{7,6},{8,7},{9,8},{10,9},{11,1... | collective-permute-start | bytes 196616 | tf_op jit(solution)/shard_map/ppermute | solution.py:267
  81.6 2.1 %collective-permute-done.9 = bf16[4,8,8,128]{3,2,1,0:T(8,128)(2,1)S(1)} collective-permute-done((bf16[4,8,8,128]{3,2,1,0:T(8,128)(2,1)S(1)}, bf16[4,8,8,128]{3,2,1,0:T(8,128)(2,1)S(1)}, u32[]{:S(2)}, u32[]{:S(2)}) %collective-permute-start.9) | collective-permute-done | bytes 65568 | tf_op jit(solution)/shard_map/ppermute | solution.py:267
  84.4 4.3 %all-to-all-start = ((bf16[4,2,8,8,128]{4,3,2,1,0:T(8,128)(2,1)}), bf16[4,2,8,8,128]{4,3,2,1,0:T(8,128)(2,1)S(1)}, u32[]{:S(2)}, u32[]{:S(2)}) async-start(bf16[4,2,8,8,128]{4,3,2,1,0:T(8,128)(2,1)} %add_convert_fusion), calls=%async_computation | async-start | bytes 262144 | tf_op jit(solution)/shard_map/all_to_all | solution.py:270
  88.7 3.6 %moment_kernel.1 = bf16[16,54,128]{2,1,0:T(8,128)(2,1)} custom-call(bf16[16,2,2,8,128]{4,3,2,1,0:T(8,128)(2,1)} %all-to-all-done.1.chunks, bf16[32,10,8,128]{3,2,1,0:T(8,128)(2,1)} %bitcast.14.proj), custom_call_target="tpu_custom_call" | custom-call | tf_op jit(solution)/shard_map/moment_kernel/pallas_call | solution.py:244
  92.3 2.4 %all-to-all-done.parts = bf16[4,2,8,8,128]{4,3,2,1,0:T(8,128)(2,1)S(1)} async-done(((bf16[4,2,8,8,128]{4,3,2,1,0:T(8,128)(2,1)}), bf16[4,2,8,8,128]{4,3,2,1,0:T(8,128)(2,1)S(1)}, u32[]{:S(2)}, u32[]{:S(2)}) %all-to-all-start) | async-done | bytes 131104 | tf_op jit(solution)/shard_map/all_to_all | solution.py:270
  94.7 3.5 %all-to-all-start.4 = ((bf16[16,54,128]{2,1,0:T(8,128)(2,1)}), bf16[16,54,128]{2,1,0:T(8,128)(2,1)S(1)}, u32[]{:S(2)}, u32[]{:S(2)}) async-start(bf16[16,54,128]{2,1,0:T(8,128)(2,1)} %moment_kernel.1), calls=%async_computation.4 | async-start | bytes 458752 | tf_op jit(solution)/shard_map/all_to_all | solution.py:253
  99.9 0.9 finish_kernel.1
  100.8 5.1 %all-to-all-done.4 = bf16[16,54,128]{2,1,0:T(8,128)(2,1)S(1)} async-done(((bf16[16,54,128]{2,1,0:T(8,128)(2,1)}), bf16[16,54,128]{2,1,0:T(8,128)(2,1)S(1)}, u32[]{:S(2)}, u32[]{:S(2)}) %all-to-all-start.4) | async-done | bytes 221216 | tf_op jit(solution)/shard_map/all_to_all | solution.py:253
  105.9 1.5 %multiply_reduce_fusion.1 = (f32[54]{0:T(128)S(1)}, f32[54,128]{1,0:T(8,128)}, f32[54,128]{1,0:T(8,128)}, f32[54]{0:T(128)S(1)}) fusion(f32[]{:T(128)S(6)} %sub.7, f32[]{:T(128)S(6)} %sub.6, f32[54,128]{1,0:T(8,128)S(1)} %convert_reduce_fusion, f32[54,128]{1,0:T(8,128)} %param.13, f32[54,128]{1,0:T(8,128)} %param.12), kind=kLoop, calls=%fused_computation.5 | loop fusion | flops 110484 | bytes 138680 | tf_op jit(solution)/shard_map/reduce_sum | solution.py:286
  (36 shorter events, 11.0 us)
Async XLA Ops:
  0.6 66.4 %copy-start = (bf16[27,128,512]{2,1,0:T(8,128)(2,1)S(1)}, bf16[27,128,512]{2,1,0:T(8,128)(2,1)}, u32[]{:S(2)}) copy-start(bf16[27,128,512]{2,1,0:T(8,128)(2,1)} %weight.1) | copy-start | bytes 10616836
  1.4 1.1 copy-start.1
  2.5 0.9 copy-start.5
  3.4 0.9 copy-start.6
  5.7 0.7 copy-start.3
  6.3 0.6 copy-start.7
  7.0 0.6 copy-start.10
  7.6 16.4 %collective-permute-start.4 = (bf16[2,8,640]{2,1,0:T(8,128)(2,1)}, bf16[2,8,640]{2,1,0:T(8,128)(2,1)}, u32[]{:S(2)}, u32[]{:S(2)}) collective-permute-start(bf16[2,8,640]{2,1,0:T(8,128)(2,1)} %get-tuple-element.14), channel_id=1, source_target_pairs={{16,0},{32,16},{48,32},{17,1},{33,17},{49,33},{18,2},{34,18},{50,3... | collective-permute-start | bytes 61448 | tf_op jit(solution)/shard_map/ppermute | solution.py:229
  8.9 15.8 %collective-permute-start.3 = (bf16[2,8,640]{2,1,0:T(8,128)(2,1)}, bf16[2,8,640]{2,1,0:T(8,128)(2,1)}, u32[]{:S(2)}, u32[]{:S(2)}) collective-permute-start(bf16[2,8,640]{2,1,0:T(8,128)(2,1)} %get-tuple-element.13), channel_id=1, source_target_pairs={{0,16},{16,32},{32,48},{1,17},{17,33},{33,49},{2,18},{18,34},{34,5... | collective-permute-start | bytes 61448 | tf_op jit(solution)/shard_map/ppermute | solution.py:228
  12.5 20.4 %all-to-all-start.1 = ((bf16[16,2,2,8,128]{4,3,2,1,0:T(8,128)(2,1)}), bf16[16,2,2,8,128]{4,3,2,1,0:T(8,128)(2,1)}, u32[]{:S(2)}, u32[]{:S(2)}) async-start(bf16[16,2,2,8,128]{4,3,2,1,0:T(8,128)(2,1)} %copy-done.7), calls=%async_computation.1 | async-start | bytes 262144 | tf_op jit(solution)/shard_map/all_to_all | solution.py:230
  34.4 13.1 %all-to-all-start.2 = ((bf16[4,2,10,8,128]{4,3,2,1,0:T(8,128)(2,1)}), bf16[4,2,10,8,128]{4,3,2,1,0:T(8,128)(2,1)}, u32[]{:S(2)}, u32[]{:S(2)}) async-start(bf16[4,2,10,8,128]{4,3,2,1,0:T(8,128)(2,1)} %broadcast_in_dim.24), calls=%async_computation.2 | async-start | bytes 327680 | tf_op jit(solution)/shard_map/all_to_all | solution.py:237
  38.3 28.7 %collective-permute-start = (bf16[2,8,8,512]{3,2,1,0:T(8,128)(2,1)}, bf16[2,8,8,512]{3,2,1,0:T(8,128)(2,1)}, u32[]{:S(2)}, u32[]{:S(2)}) collective-permute-start(bf16[2,8,8,512]{3,2,1,0:T(8,128)(2,1)} %copy-done.3), channel_id=1, source_target_pairs={{0,64},{64,128},{128,192},{192,0},{1,65},{65,129},{129,193},{193,1... | collective-permute-start | bytes 393224 | tf_op jit(solution)/shard_map/ppermute | solution.py:231
  40.0 27.0 %collective-permute-start.1 = (bf16[2,8,8,512]{3,2,1,0:T(8,128)(2,1)}, bf16[2,8,8,512]{3,2,1,0:T(8,128)(2,1)}, u32[]{:S(2)}, u32[]{:S(2)}) collective-permute-start(bf16[2,8,8,512]{3,2,1,0:T(8,128)(2,1)} %copy-done.3), channel_id=1, source_target_pairs={{0,128},{64,192},{128,0},{192,64},{1,129},{65,193},{129,1},{193,65... | collective-permute-start | bytes 393224 | tf_op jit(solution)/shard_map/ppermute | solution.py:231
  42.9 24.1 %collective-permute-start.2 = (bf16[2,8,8,512]{3,2,1,0:T(8,128)(2,1)}, bf16[2,8,8,512]{3,2,1,0:T(8,128)(2,1)}, u32[]{:S(2)}, u32[]{:S(2)}) collective-permute-start(bf16[2,8,8,512]{3,2,1,0:T(8,128)(2,1)} %copy-done.3), channel_id=1, source_target_pairs={{0,192},{64,0},{128,64},{192,128},{1,193},{65,1},{129,65},{193,129... | collective-permute-start | bytes 393224 | tf_op jit(solution)/shard_map/ppermute | solution.py:231
  49.4 35.1 %all-to-all-start.3 = ((bf16[4,4,2,10,8,128]{5,4,3,2,1,0:T(8,128)(2,1)}), bf16[4,4,2,10,8,128]{5,4,3,2,1,0:T(8,128)(2,1)}, u32[]{:S(2)}, u32[]{:S(2)}) async-start(bf16[4,4,2,10,8,128]{5,4,3,2,1,0:T(8,128)(2,1)} %broadcast_in_dim.25), calls=%async_computation.3 | async-start | bytes 1310720 | tf_op jit(solution)/shard_map/all_to_all | solution.py:240
  56.9 5.3 %collective-permute-start.5 = (bf16[2,2,8,512]{3,2,1,0:T(8,128)(2,1)}, bf16[2,2,8,512]{3,2,1,0:T(8,128)(2,1)S(1)}, u32[]{:S(2)}, u32[]{:S(2)}) collective-permute-start(bf16[2,2,8,512]{3,2,1,0:T(8,128)(2,1)} %pad_maximum_fusion.1.r0), channel_id=1, source_target_pairs={{0,64},{64,128},{128,192},{192,0},{1,65},{65,129},{129,193},{193,1... | collective-permute-start | bytes 98312 | tf_op jit(solution)/shard_map/ppermute | solution.py:233
  58.4 6.2 %collective-permute-start.6 = (bf16[2,2,8,512]{3,2,1,0:T(8,128)(2,1)}, bf16[2,2,8,512]{3,2,1,0:T(8,128)(2,1)}, u32[]{:S(2)}, u32[]{:S(2)}) collective-permute-start(bf16[2,2,8,512]{3,2,1,0:T(8,128)(2,1)} %pad_maximum_fusion.1.r0), channel_id=1, source_target_pairs={{0,128},{64,192},{128,0},{192,64},{1,129},{65,193},{129,1},{193,65... | collective-permute-start | bytes 98312 | tf_op jit(solution)/shard_map/ppermute | solution.py:233
  62.2 0.6 copy-start.8
  62.8 4.2 %collective-permute-start.7 = (bf16[2,2,8,512]{3,2,1,0:T(8,128)(2,1)}, bf16[2,2,8,512]{3,2,1,0:T(8,128)(2,1)}, u32[]{:S(2)}, u32[]{:S(2)}) collective-permute-start(bf16[2,2,8,512]{3,2,1,0:T(8,128)(2,1)} %pad_maximum_fusion.1.r0), channel_id=1, source_target_pairs={{0,192},{64,0},{128,64},{192,128},{1,193},{65,1},{129,65},{193,129... | collective-permute-start | bytes 98312 | tf_op jit(solution)/shard_map/ppermute | solution.py:233
  67.0 0.9 copy-start.4
  68.0 0.8 copy-start.9
  72.4 9.2 %collective-permute-start.8 = (bf16[4,8,8,128]{3,2,1,0:T(8,128)(2,1)S(1)}, bf16[4,8,8,128]{3,2,1,0:T(8,128)(2,1)S(1)}, u32[]{:S(2)}, u32[]{:S(2)}) collective-permute-start(bf16[4,8,8,128]{3,2,1,0:T(8,128)(2,1)S(1)} %get-tuple-element.16), channel_id=1, source_target_pairs={{0,1},{1,2},{2,3},{3,4},{4,5},{5,6},{6,7},{7,8},{8,9},{9,10},{10,1... | collective-permute-start | bytes 196616 | tf_op jit(solution)/shard_map/ppermute | solution.py:268
  75.8 8.0 %collective-permute-start.9 = (bf16[4,8,8,128]{3,2,1,0:T(8,128)(2,1)S(1)}, bf16[4,8,8,128]{3,2,1,0:T(8,128)(2,1)S(1)}, u32[]{:S(2)}, u32[]{:S(2)}) collective-permute-start(bf16[4,8,8,128]{3,2,1,0:T(8,128)(2,1)S(1)} %get-tuple-element.17), channel_id=1, source_target_pairs={{1,0},{2,1},{3,2},{4,3},{5,4},{6,5},{7,6},{8,7},{9,8},{10,9},{11,1... | collective-permute-start | bytes 196616 | tf_op jit(solution)/shard_map/ppermute | solution.py:267
  84.4 10.3 %all-to-all-start = ((bf16[4,2,8,8,128]{4,3,2,1,0:T(8,128)(2,1)}), bf16[4,2,8,8,128]{4,3,2,1,0:T(8,128)(2,1)S(1)}, u32[]{:S(2)}, u32[]{:S(2)}) async-start(bf16[4,2,8,8,128]{4,3,2,1,0:T(8,128)(2,1)} %add_convert_fusion), calls=%async_computation | async-start | bytes 262144 | tf_op jit(solution)/shard_map/all_to_all | solution.py:270
  94.7 11.2 %all-to-all-start.4 = ((bf16[16,54,128]{2,1,0:T(8,128)(2,1)}), bf16[16,54,128]{2,1,0:T(8,128)(2,1)S(1)}, u32[]{:S(2)}, u32[]{:S(2)}) async-start(bf16[16,54,128]{2,1,0:T(8,128)(2,1)} %moment_kernel.1), calls=%async_computation.4 | async-start | bytes 458752 | tf_op jit(solution)/shard_map/all_to_all | solution.py:253
  99.0 0.9 copy-start.2

commit v2 on v1

--- a/solution.py
+++ b/solution.py
@@ -11,18 +11,74 @@
 F32 = jnp.float32
 
 
-def _call(body, outs, scratch=(), smem=0, total=0):
-    specs = [pl.BlockSpec(memory_space=pltpu.SMEM)] * smem
-    specs += [pl.BlockSpec(memory_space=pltpu.VMEM)] * (total - smem)
+def _call(kernel, ins, outs, scratch=()):
+    moved = [i for i, (_, space) in enumerate(ins) if space in ("hbm", "arg")]
+    late = [i for i, (_, space) in enumerate(ins) if space == "late"]
+    count = len(ins)
+
+    def run(*refs):
+        given = list(refs[:count])
+        results = refs[count : count + len(outs)]
+        rest = refs[count + len(outs) :]
+        in_bufs = rest[: len(moved)]
+        out_bufs = rest[len(moved) : len(moved) + len(outs)]
+        late_bufs = rest[len(moved) + len(outs) :][: len(late)]
+        own = rest[len(moved) + len(outs) + len(late) : -3]
+        in_sem, late_sem, out_sem = rest[-3:]
+        copies = []
+        for n, i in enumerate(moved):
+            copies.append(pltpu.make_async_copy(given[i], in_bufs[n], in_sem.at[n]))
+            given[i] = in_bufs[n]
+        for n, i in enumerate(late):
+            third = given[i].shape[0] // 3
+            pieces = [
+                pltpu.make_async_copy(
+                    given[i].at[pl.ds(a * third, third)],
+                    late_bufs[n].at[pl.ds(a * third, third)],
+                    late_sem.at[3 * n + a],
+                )
+                for a in range(3)
+            ]
+            for piece in pieces:
+                piece.start()
+            given[i] = (late_bufs[n], pieces)
+        for copy in copies:
+            copy.start()
+        for copy in copies:
+            copy.wait()
+        kernel(*given, *out_bufs, *own)
+        copies = [
+            pltpu.make_async_copy(out_bufs[n], results[n], out_sem.at[n]) for n in range(len(outs))
+        ]
+        for copy in copies:
+            copy.start()
+        for copy in copies:
+            copy.wait()
+
+    buffers = [pltpu.VMEM(ins[i][0].shape, ins[i][0].dtype) for i in moved]
+    buffers += [pltpu.VMEM(shape, dtype) for shape, dtype in outs]
+    buffers += [pltpu.VMEM(ins[i][0].shape, ins[i][0].dtype) for i in late]
+    arrays = [
+        pltpu.with_memory_space_constraint(array, pltpu.HBM) if space in ("arg", "late") else array
+        for array, space in ins
+    ]
     return pl.pallas_call(
-        body,
-        out_shape=outs,
-        in_specs=specs,
-        out_specs=jax.tree.map(lambda _: pl.BlockSpec(memory_space=pltpu.VMEM), outs),
-        scratch_shapes=list(scratch),
+        run,
+        out_shape=[jax.ShapeDtypeStruct(shape, dtype) for shape, dtype in outs],
+        in_specs=[
+            pl.BlockSpec(memory_space=pltpu.SMEM if space == "smem" else pltpu.HBM)
+            for _, space in ins
+        ],
+        out_specs=[pl.BlockSpec(memory_space=pltpu.HBM) for _ in outs],
+        scratch_shapes=buffers
+        + list(scratch)
+        + [
+            pltpu.SemaphoreType.DMA((max(1, len(moved)),)),
+            pltpu.SemaphoreType.DMA((max(1, 3 * len(late)),)),
+            pltpu.SemaphoreType.DMA((len(outs),)),
+        ],
         compiler_params=pltpu.CompilerParams(vmem_limit_bytes=40 * 1024 * 1024),
-        name=body.__name__,
-    )
+    )(*arrays)
 
 
 def _rows_to_scratch(ref, scratch):
@@ -105,6 +161,36 @@
             in_out[tile * 4 + i] = out.astype(BF16).reshape(cols, rows // 4, frames, 128)
 
 
+def assemble(pos, g, proj, chunks, above, below, g_out, *sends):
+    _, rows, _, chans = g.shape
+    depth = len(sends)
+    top = jnp.where(pos[0] > 0, above[...], jnp.zeros_like(above[...]))
+    bot = jnp.where(pos[0] < 3, below[...], jnp.zeros_like(below[...]))
+    g_out[:, 1 : rows + 1] = g[...]
+    g_out[:, 0] = top[:, :, :chans]
+    g_out[:, rows + 1] = bot[:, :, :chans]
+    for k, send in enumerate(sends):
+        send[:, 1 : rows + 1] = proj[...]
+        send[:, 0] = top[:, :, chans:]
+        send[:, rows + 1] = bot[:, :, chans:]
+        for x in range(chunks.shape[0] // depth):
+            at = rows + 2 + 2 * x
+            send[:, at : at + 2] = chunks[depth * x + lax.rem(pos[2] + k, depth)]
+
+
+def across_x(pos, *refs):
+    depth = len(refs) // 2
+    along = depth
+    rows = refs[0].shape[1] - 2 * along
+    for m in range(along):
+        send = refs[depth + m]
+        at = rows + 2 * lax.rem(pos[1] + m, along)
+        for k in range(depth):
+            send[k, :, :rows] = refs[k][:, :rows]
+            for w in range(refs[k].shape[0]):
+                send[k, w, rows:] = refs[k][w, pl.ds(at, 2)]
+
+
 def shift_frames(x, by):
     zero = jnp.zeros_like(x[:, :1])
     if by > 0:
@@ -112,18 +198,17 @@
     return jnp.concatenate([x[:, 1:], zero], axis=1)
 
 
-def branch_kernel(
-    pos, g0, g1, g2, g3, r0, r1, r2, r3, weight, own_out, left_out, right_out, ext
-):
+def branch_kernel(g0, g1, g2, g3, weight, own_out, left_out, right_out, ext):
     cols, rows, frames, chans = g0.shape
+    rows = rows - 2
+    weight, pieces = weight
     width = weight.shape[1]
-    for k, (g, r) in enumerate(((g0, r0), (g1, r1), (g2, r2), (g3, r3))):
-        ext[k, :, 1 : rows + 1] = g[...]
-        ext[k, :, 0] = r[0]
-        ext[k, :, rows + 1] = r[1]
+    for k, g in enumerate((g0, g1, g2, g3)):
+        ext[k] = g[...]
     count = 4 * cols * rows * frames
     total = None
     for a in range(3):
+        pieces[a].wait()
         acc = jnp.zeros((count, 3 * width), F32)
         for b in range(3):
             lhs = ext[:, :, 2 - b : 2 - b + rows].reshape(count, chans)
@@ -137,22 +222,40 @@
         total = acc if total is None else total + acc
     total = total.reshape(4, cols, rows, frames, 3 * width)
     for k in range(4):
-        sample = lax.rem(pos[0] + (4 - k), 4)
         part = [[total[k, w, :, :, c * width : (c + 1) * width] for c in range(3)] for w in range(cols)]
-        left_out[sample] = part[0][0].astype(BF16)
-        own_out[sample, 0] = part[0][1] + part[1][0]
-        own_out[sample, 1] = part[0][2] + part[1][1]
-        right_out[sample] = part[1][2].astype(BF16)
-
-
-def moment_kernel(chunks, proj, out, wide, flat):
-    devices, cols, halves, frames, _ = chunks.shape
-    across, rows, _, rank = proj.shape
+        left_out[k] = part[0][0].astype(BF16)
+        own_out[k, 0] = part[0][1] + part[1][0]
+        own_out[k, 1] = part[0][2] + part[1][1]
+        right_out[k] = part[1][2].astype(BF16)
+
+
+def merge_kernel(pos, own, from_left, from_right, *outs):
+    first = (pos[0] == 0) & (pos[1] == 0)
+    last = (pos[0] == 3) & (pos[1] == 3)
+    for k, out in enumerate(outs):
+        left = from_left[k].astype(F32)
+        right = from_right[k].astype(F32)
+        out[0] = (own[k, 0] + jnp.where(first, 0.0, left)).astype(BF16)
+        out[1] = (own[k, 1] + jnp.where(last, 0.0, right)).astype(BF16)
+
+
+def moment_kernel(pos, g0, g1, g2, g3, out, wide, inner, flat):
+    rows = wide.shape[1]
+    depth, cols, _, frames, rank = g0.shape
+    devices = 4 * depth
+    halves = 2
+    across = devices * cols
+    for m, got in enumerate((g0, g1, g2, g3)):
+        x_at = lax.rem(pos[0] + (4 - m), 4)
+        for k in range(depth):
+            at = depth * x_at + lax.rem(pos[1] + (depth - k), depth)
+            inner[at] = got[k, :, rows:]
+            for w in range(cols):
+                wide[1 + cols * at + w] = got[k, w, :rows]
     wide[0] = jnp.zeros_like(wide[0])
     wide[across + 1] = jnp.zeros_like(wide[0])
-    wide[1 : across + 1] = proj[...]
     count = devices * cols * halves
-    x = chunks[...].astype(F32).reshape(count, frames, 128)
+    x = inner[...].astype(F32).reshape(count, frames, 128)
     later = shift_frames(x, 1).reshape(count * frames, 128)
     sooner = shift_frames(x, -1).reshape(count * frames, 128)
     x = x.reshape(count * frames, 128)
@@ -179,14 +282,15 @@
         out[m] = flat[pl.ds(m, 54, stride=16), :].astype(BF16)
 
 
-def finish_kernel(up, parts, out, flat, outflat):
-    frames, rows, cols, chans = up.shape
+def finish_kernel(pos, up, p0, p1, p2, p3, out, flat, outflat):
+    frames, rows, cols, _ = up.shape
     _rows_to_scratch(up, flat)
-    for tile in range(4):
+    for k, part in enumerate((p0, p1, p2, p3)):
+        tile = lax.rem(pos[0] + k, 4)
         for w in range(cols):
             for h in range(rows):
                 at = pl.ds(h * cols + w, frames, stride=rows * cols)
-                outflat[tile, at, :] = flat[tile, at, :] + parts[tile, w, h].astype(F32)
+                outflat[tile, at, :] = flat[tile, at, :] + part[w, h].astype(F32)
     for t in range(frames):
         for h in range(rows):
             base = (t * rows + h) * cols
@@ -199,81 +303,97 @@
     return [(i, (i + shift) % n) for i in range(n)]
 
 
-def line(axis, shift):
-    n = lax.axis_size(axis)
-    return [(i, i + shift) for i in range(n) if 0 <= i + shift < n]
-
-
-def body(
+def around(arrays, axis, sign=1):
+    got = list(arrays)
+    for k in (1, 3, 2):
+        got[k] = lax.ppermute(arrays[k], axis, ring(axis, sign * k))
+    return got
+
+
+def step(
     inputs, pre_activation, upstream, weight, first_moment, second_moment, hash_seed, step_count
 ):
     frames, rows, cols, chans = inputs.shape[1:]
     rank = first_moment.shape[1]
     tokens = frames * rows * cols
     sx = ("sxx", "sxz")
+    spread = pltpu.VMEM((chans // 128, tokens, 128), F32)
     g, proj, chunks, top, bot = _call(
         prepare,
-        (
-            jax.ShapeDtypeStruct((cols, rows, frames, chans), BF16),
-            jax.ShapeDtypeStruct((cols, rows, frames, rank), BF16),
-            jax.ShapeDtypeStruct((16, cols, 2, frames, 128), BF16),
-            jax.ShapeDtypeStruct((cols, frames, chans + rank), BF16),
-            jax.ShapeDtypeStruct((cols, frames, chans + rank), BF16),
-        ),
-        scratch=[pltpu.VMEM((chans // 128, tokens, 128), F32)] * 3,
-        smem=1,
-        total=4,
-    )(hash_seed.reshape(1), pre_activation[0], upstream[0], inputs[0])
-
-    above = lax.ppermute(bot, "sy", line("sy", 1))
-    below = lax.ppermute(top, "sy", line("sy", -1))
-    chunks = lax.all_to_all(chunks, sx, split_axis=0, concat_axis=0, tiled=True)
-    g_all = [g] + [lax.ppermute(g, "dp", ring("dp", k)) for k in (1, 2, 3)]
-    edge = jnp.stack([above[..., :chans], below[..., :chans]])
-    edges = [edge] + [lax.ppermute(edge, "dp", ring("dp", k)) for k in (1, 2, 3)]
-    proj = jnp.concatenate(
-        [above[:, None, :, chans:], proj, below[:, None, :, chans:]], axis=1
-    )
-    proj = lax.all_to_all(
-        jnp.broadcast_to(proj[None], (4,) + proj.shape), "sxz", 0, 0, tiled=True
-    )
-    proj = lax.all_to_all(
-        jnp.broadcast_to(proj[None], (4,) + proj.shape), "sxx", 0, 0, tiled=True
-    )
-    proj = proj.reshape(16 * cols, rows + 2, frames, rank)
-    terms = _call(
+        [
+            (hash_seed.reshape(1), "smem"),
+            (pre_activation[0], "arg"),
+            (upstream[0], "arg"),
+            (inputs[0], "arg"),
+        ],
+        [
+            ((cols, rows, frames, chans), BF16),
+            ((cols, rows, frames, rank), BF16),
+            ((16, cols, 2, frames, 128), BF16),
+            ((cols, frames, chans + rank), BF16),
+            ((cols, frames, chans + rank), BF16),
+        ],
+        [spread] * 3,
+    )
+    place = {a: lax.axis_index(a).astype(jnp.int32) for a in ("dp", "sy", "sxx", "sxz")}
+
+    def places(*axes):
+        return (jnp.stack([place[a] for a in axes]), "smem")
+
+    above = lax.ppermute(bot, "sy", ring("sy", 1))
+    below = lax.ppermute(top, "sy", ring("sy", -1))
+    along_z = ((cols, rows + 2 + 8, frames, 128), BF16)
+    along_x = ((4, cols, rows + 4, frames, 128), BF16)
+    g, *sends = _call(
+        assemble,
+        [places("sy", "sxx", "sxz")]
+        + [(a, "hbm") for a in (g, proj, chunks, above, below)],
+        [((cols, rows + 2, frames, chans), BF16)] + [along_z] * 4,
+    )
+    got = around(sends, "sxz")
+    sends = _call(
+        across_x,
+        [places("sy", "sxx", "sxz")] + [(a, "hbm") for a in got],
+        [along_x] * 4,
+    )
+    got = around(sends, "sxx")
+    g_all = around([g] * 4, "dp")
+    (terms,) = _call(
         moment_kernel,
-        jax.ShapeDtypeStruct((16, 54, rank), BF16),
-        scratch=[
+        [places("sxx", "sxz")] + [(a, "hbm") for a in got],
+        [((16, 54, rank), BF16)],
+        [
             pltpu.VMEM((16 * cols + 2, rows + 2, frames, rank), BF16),
+            pltpu.VMEM((16, cols, 2, frames, 128), BF16),
             pltpu.VMEM((54 * 16, rank), F32),
         ],
-        total=2,
-    )(chunks, proj)
+    )
     terms = lax.all_to_all(terms, ("dp", "sy"), 0, 0, tiled=True)
 
-    place = lax.axis_index("dp").astype(jnp.int32).reshape(1)
     own, left, right = _call(
         branch_kernel,
-        (
-            jax.ShapeDtypeStruct((4, cols, rows, frames, 128), F32),
-            jax.ShapeDtypeStruct((4, rows, frames, 128), BF16),
-            jax.ShapeDtypeStruct((4, rows, frames, 128), BF16),
-        ),
-        scratch=[pltpu.VMEM((4, cols, rows + 2, frames, chans), BF16)],
-        smem=1,
-        total=10,
-    )(place, *g_all, *edges, weight)
-    from_right = lax.ppermute(left, sx, line(sx, -1))
-    from_left = lax.ppermute(right, sx, line(sx, 1))
-    mine = (own + jnp.stack([from_left, from_right], axis=1).astype(F32)).astype(BF16)
-    parts = lax.all_to_all(mine, "dp", 0, 0, tiled=True)
-    input_grad = _call(
+        [(x, "hbm") for x in g_all] + [(weight, "late")],
+        [
+            ((4, cols, rows, frames, 128), F32),
+            ((4, rows, frames, 128), BF16),
+            ((4, rows, frames, 128), BF16),
+        ],
+        [pltpu.VMEM((4, cols, rows + 2, frames, chans), BF16)],
+    )
+    from_right = lax.ppermute(left, sx, ring(sx, -1))
+    from_left = lax.ppermute(right, sx, ring(sx, 1))
+    mine = _call(
+        merge_kernel,
+        [places("sxx", "sxz")] + [(a, "hbm") for a in (own, from_left, from_right)],
+        [((cols, rows, frames, 128), BF16)] * 4,
+    )
+    parts = around(mine, "dp", -1)
+    (input_grad,) = _call(
         finish_kernel,
-        jax.ShapeDtypeStruct((frames, rows, cols, chans), BF16),
-        scratch=[pltpu.VMEM((chans // 128, tokens, 128), F32)] * 2,
-        total=2,
-    )(upstream[0], parts)
+        [places("dp"), (upstream[0], "arg")] + [(a, "hbm") for a in parts],
+        [((frames, rows, cols, chans), BF16)],
+        [spread] * 2,
+    )
 
     total = 32768
     reduced = jnp.sum(terms.astype(F32), axis=0) / math.sqrt(total)
@@ -299,7 +419,7 @@
     whole = ("dp", "sy", "sxx", "sxz")
     volume = P("dp", None, "sy", sx, None)
     return jax.shard_map(
-        body,
+        step,
         mesh=grid,
         in_specs=(volume, volume, volume, P(None, "dp", None), P(whole), P(whole), P(), P()),
         out_specs=(volume, P(whole), P(whole), P(whole)),

time: 109 us -> 89.7 us (0.82)
  starting transfers between devices: 55.4 us -> 36.3 us
  local copies, waits for them, and re-layouts: 14 us -> 0.01 us
  waiting for transfers between devices: 22 us -> 30.8 us
  Pallas kernels: 9.55 us -> 17.9 us
  other arithmetic: 4.75 us -> 1.46 us
    ppermute x10 -> x16, waiting for transfers between devices: 5.79 us -> 30.8 us  [the longest x12 26.3 us: around(): got[k] = lax.ppermute(arrays[k], axis, ring(axis, sign * k))]
    all_to_all x5 -> x1, starting transfers between devices: 29.4 us -> 4.59 us  [step(): terms = lax.all_to_all(terms, ('dp', 'sy'), 0, 0, tiled=True)]
    all_to_all x5 -> x1, waiting for transfers between devices: 16.2 us -> 0.01 us  [step(): terms = lax.all_to_all(terms, ('dp', 'sy'), 0, 0, tiled=True)]
    pallas_call x4 -> x7, Pallas kernels: 9.55 us -> 17.9 us  [_call(): pl.pallas_call(run, out_shape=[jax.ShapeDtypeStruct(shape, dtype) for sha...]
    unnamed x22 -> x4, local copies, waits for them, and re-layouts: 7.93 us -> 0.01 us
    ppermute x10 -> x16, starting transfers between devices: 25.9 us -> 31.7 us  [the longest x12 24.8 us: around(): got[k] = lax.ppermute(arrays[k], axis, ring(axis, sign * k))]
    broadcast_in_dim x4 -> x0, local copies, waits for them, and re-layouts: 4.68 us -> none  [the longest x2 3.32 us: body(): jnp.broadcast_to(proj[None], (4,) + proj.shape)]
    another operation x2 -> x0, local copies, waits for them, and re-layouts: 1.44 us -> none  [body(): edge = jnp.stack([above[..., :chans], below[..., :chans]])]
  transfers between devices with their start and end apart: 15 -> 17, of which waited for: 8 -> 13; matrix products, arithmetic and copies ran while one was open for 7% -> 0% of each run, Pallas kernels for 8% -> 8%
where the time goes in v2:
time: 89.7 us; the launch traced here: 88.6 us
  starting transfers between devices  36.3 us (40%)
  waiting for transfers between devices  30.8 us (34%)
  Pallas kernels  17.9 us (20%)
  between operations  2.15 us (2%)
  other arithmetic  1.46 us (2%)
    ppermute x12, waiting for transfers between devices, around(): got[k] = lax.ppermute(arrays[k], axis, ring(axis, sign * k))  26.3 us
    ppermute x12, starting transfers between devices, around(): got[k] = lax.ppermute(arrays[k], axis, ring(axis, sign * k))  24.8 us
    pallas_call x7, Pallas kernels, _call(): pl.pallas_call(run, out_shape=[jax.ShapeDtypeStruct(shape, dtype) for sha...  17.9 us
    all_to_all x1, starting transfers between devices, step(): terms = lax.all_to_all(terms, ('dp', 'sy'), 0, 0, tiled=True)  4.59 us
    ppermute x1, starting transfers between devices, step(): from_right = lax.ppermute(left, sx, ring(sx, -1))  3.26 us
    ppermute x1, waiting for transfers between devices, step(): from_left = lax.ppermute(right, sx, ring(sx, 1))  3.03 us
    ppermute x1, starting transfers between devices, step(): from_left = lax.ppermute(right, sx, ring(sx, 1))  1.85 us
  transfers between devices with their start and end apart: 17, of which 13 were waited for; matrix products, arithmetic and copies ran while one was open for 0% of the time, Pallas kernels for 8%

profile of v2, /device:TPU:2, one launch (start us, length us, event | category | flops | bytes accessed | tf_op | source)
XLA Modules:
  0.0 88.6 jit_solution(12395804986813093592)
XLA Ops:
  1.3 2.6 %shard_map.111 = (bf16[2,8,8,512]{3,2,1,0:T(8,128)(2,1)S(1)}, bf16[2,8,8,128]{3,2,1,0:T(8,128)(2,1)S(1)}, bf16[16,2,2,8,128]{4,3,2,1,0:T(8,128)(2,1)S(1)}, bf16[...) custom-call(s32[1]{0:T(128)} %bitcast.9.refs_0_, bf16[8,8,2,512]{3,2,1,0:T(2,128)(2,1)} %bitcast.12, ...), custom_call_target="tpu_custom_call" | custom-call | tf_op jit(solution)/shard_map/pallas_call | solution.py:65
  3.9 1.7 %collective-permute-start.1 = (bf16[2,8,640]{2,1,0:T(8,128)(2,1)S(1)}, bf16[2,8,640]{2,1,0:T(8,128)(2,1)S(1)}, u32[]{:S(2)}, u32[]{:S(2)}) collective-permute-start(bf16[2,8,640]{2,1,0:T(8,128)(2,1)S(1)} %get-tuple-element.29), channel_id=1, source_target_pairs={{0,48},{16,0},{32,16},{48,32},{1,49},{17,1},{33,17},{49,33},{2,50}... | collective-permute-start | bytes 61448 | tf_op jit(solution)/shard_map/ppermute | solution.py:344
  5.8 1.4 %collective-permute-done.refs_4_ = bf16[2,8,640]{2,1,0:T(8,128)(2,1)S(1)} collective-permute-done((bf16[2,8,640]{2,1,0:T(8,128)(2,1)S(1)}, bf16[2,8,640]{2,1,0:T(8,128)(2,1)S(1)}, u32[]{:S(2)}, u32[]{:S(2)}) %collective-permute-start) | collective-permute-done | bytes 20512 | tf_op jit(solution)/shard_map/ppermute | solution.py:343
  7.2 1.7 %shard_map.112 = (bf16[2,10,8,512]{3,2,1,0:T(8,128)(2,1)S(1)}, bf16[2,18,8,128]{3,2,1,0:T(8,128)(2,1)S(1)}, bf16[2,18,8,128]{3,2,1,0:T(8,128)(2,1)S(1)}, bf16[2,...) custom-call(s32[3]{0:T(128)S(1)} %pad_add_fusion.1.refs_0_, bf16[2,8,8,512]{3,2,1,0:T(8,128)(2,1)S(1)} %get-tuple-element.25.refs_1_, ...), custom_call_target="tpu_custom_call" | custom-call | tf_op jit(solution)/shard_map/pallas_call | solution.py:65
  8.9 3.4 %collective-permute-start.10 = (bf16[2,18,8,128]{3,2,1,0:T(8,128)(2,1)S(1)}, bf16[2,18,8,128]{3,2,1,0:T(8,128)(2,1)S(1)}, u32[]{:S(2)}, u32[]{:S(2)}) collective-permute-start(bf16[2,18,8,128]{3,2,1,0:T(8,128)(2,1)S(1)} %get-tuple-element.39), channel_id=1, source_target_pairs={{0,1},{1,2},{2,3},{3,0},{4,5},{5,6},{6,7},{7,4},{8,9},{9,10},{10,1... | collective-permute-start | bytes 221192 | tf_op jit(solution)/shard_map/ppermute | solution.py:309
  12.3 5.4 %collective-permute-start.11 = (bf16[2,18,8,128]{3,2,1,0:T(8,128)(2,1)S(1)}, bf16[2,18,8,128]{3,2,1,0:T(8,128)(2,1)S(1)}, u32[]{:S(2)}, u32[]{:S(2)}) collective-permute-start(bf16[2,18,8,128]{3,2,1,0:T(8,128)(2,1)S(1)} %get-tuple-element.40), channel_id=1, source_target_pairs={{0,2},{1,3},{2,0},{3,1},{4,6},{5,7},{6,4},{7,5},{8,10},{9,11},{10,... | collective-permute-start | bytes 221192 | tf_op jit(solution)/shard_map/ppermute | solution.py:309
  17.6 2.7 %collective-permute-start.12 = (bf16[2,18,8,128]{3,2,1,0:T(8,128)(2,1)S(1)}, bf16[2,18,8,128]{3,2,1,0:T(8,128)(2,1)S(1)}, u32[]{:S(2)}, u32[]{:S(2)}) collective-permute-start(bf16[2,18,8,128]{3,2,1,0:T(8,128)(2,1)S(1)} %get-tuple-element.41), channel_id=1, source_target_pairs={{0,3},{1,0},{2,1},{3,2},{4,7},{5,4},{6,5},{7,6},{8,11},{9,8},{10,9... | collective-permute-start | bytes 221192 | tf_op jit(solution)/shard_map/ppermute | solution.py:309
  20.3 3.2 %collective-permute-done.11.refs_3_ = bf16[2,18,8,128]{3,2,1,0:T(8,128)(2,1)S(1)} collective-permute-done((bf16[2,18,8,128]{3,2,1,0:T(8,128)(2,1)S(1)}, bf16[2,18,8,128]{3,2,1,0:T(8,128)(2,1)S(1)}, u32[]{:S(2)}, u32[]{:S(2)}) %collective-permute-start.11) | collective-permute-done | bytes 73760 | tf_op jit(solution)/shard_map/ppermute | solution.py:309
  23.5 2.5 %collective-permute-done.12.refs_4_ = bf16[2,18,8,128]{3,2,1,0:T(8,128)(2,1)S(1)} collective-permute-done((bf16[2,18,8,128]{3,2,1,0:T(8,128)(2,1)S(1)}, bf16[2,18,8,128]{3,2,1,0:T(8,128)(2,1)S(1)}, u32[]{:S(2)}, u32[]{:S(2)}) %collective-permute-start.12) | collective-permute-done | bytes 73760 | tf_op jit(solution)/shard_map/ppermute | solution.py:309
  26.1 2.1 %shard_map.116 = (bf16[4,2,12,8,128]{4,3,2,1,0:T(8,128)(2,1)S(1)}, bf16[4,2,12,8,128]{4,3,2,1,0:T(8,128)(2,1)S(1)}, bf16[4,2,12,8,128]{4,3,2,1,0:T(8,128)(2,1)S(1)}, bf16[4,2,12,8,128]{4,3,2,1,0:T(8,128)(2,1)S(1)}) custom-call(s32[3]{0:T(128)S(1)} %pad_add_fusion.1.refs_0_, bf16[2,18,8,128]{3,2,1,0:T(8,128)(2,1)S(1)} %get-tuple-element.38.refs_1_, ...), custom_call_target="tpu_custom_call" | custom-call | tf_op jit(solution)/shard_map/pallas_call | solution.py:65
  28.2 1.6 %collective-permute-start.13 = (bf16[4,2,12,8,128]{4,3,2,1,0:T(8,128)(2,1)S(1)}, bf16[4,2,12,8,128]{4,3,2,1,0:T(8,128)(2,1)S(1)}, u32[]{:S(2)}, u32[]{:S(2)}) collective-permute-start(bf16[4,2,12,8,128]{4,3,2,1,0:T(8,128)(2,1)S(1)} %get-tuple-element.43), channel_id=1, source_target_pairs={{0,4},{4,8},{8,12},{12,0},{1,5},{5,9},{9,13},{13,1},{2,6},{6,10},{... | collective-permute-start | bytes 589832 | tf_op jit(solution)/shard_map/ppermute | solution.py:309
  29.7 1.1 %collective-permute-start.14 = (bf16[4,2,12,8,128]{4,3,2,1,0:T(8,128)(2,1)S(1)}, bf16[4,2,12,8,128]{4,3,2,1,0:T(8,128)(2,1)S(1)}, u32[]{:S(2)}, u32[]{:S(2)}) collective-permute-start(bf16[4,2,12,8,128]{4,3,2,1,0:T(8,128)(2,1)S(1)} %get-tuple-element.44), channel_id=1, source_target_pairs={{0,8},{4,12},{8,0},{12,4},{1,9},{5,13},{9,1},{13,5},{2,10},{6,14},... | collective-permute-start | bytes 589832 | tf_op jit(solution)/shard_map/ppermute | solution.py:309
  30.9 2.2 %collective-permute-start.15 = (bf16[4,2,12,8,128]{4,3,2,1,0:T(8,128)(2,1)S(1)}, bf16[4,2,12,8,128]{4,3,2,1,0:T(8,128)(2,1)S(1)}, u32[]{:S(2)}, u32[]{:S(2)}) collective-permute-start(bf16[4,2,12,8,128]{4,3,2,1,0:T(8,128)(2,1)S(1)} %get-tuple-element.45), channel_id=1, source_target_pairs={{0,12},{4,0},{8,4},{12,8},{1,13},{5,1},{9,5},{13,9},{2,14},{6,2},{... | collective-permute-start | bytes 589832 | tf_op jit(solution)/shard_map/ppermute | solution.py:309
  33.1 2.9 %collective-permute-done.13.refs_2_ = bf16[4,2,12,8,128]{4,3,2,1,0:T(8,128)(2,1)S(1)} collective-permute-done((bf16[4,2,12,8,128]{4,3,2,1,0:T(8,128)(2,1)S(1)}, bf16[4,2,12,8,128]{4,3,2,1,0:T(8,128)(2,1)S(1)}, u32[]{:S(2)}, u32[]{:S(2)}) %collective-permute-start.13) | collective-permute-done | bytes 196640 | tf_op jit(solution)/shard_map/ppermute | solution.py:309
  36.0 3.0 %collective-permute-done.14.refs_3_ = bf16[4,2,12,8,128]{4,3,2,1,0:T(8,128)(2,1)S(1)} collective-permute-done((bf16[4,2,12,8,128]{4,3,2,1,0:T(8,128)(2,1)S(1)}, bf16[4,2,12,8,128]{4,3,2,1,0:T(8,128)(2,1)S(1)}, u32[]{:S(2)}, u32[]{:S(2)}) %collective-permute-start.14) | collective-permute-done | bytes 196640 | tf_op jit(solution)/shard_map/ppermute | solution.py:309
  39.0 2.4 %collective-permute-done.15.refs_4_ = bf16[4,2,12,8,128]{4,3,2,1,0:T(8,128)(2,1)S(1)} collective-permute-done((bf16[4,2,12,8,128]{4,3,2,1,0:T(8,128)(2,1)S(1)}, bf16[4,2,12,8,128]{4,3,2,1,0:T(8,128)(2,1)S(1)}, u32[]{:S(2)}, u32[]{:S(2)}) %collective-permute-start.15) | collective-permute-done | bytes 196640 | tf_op jit(solution)/shard_map/ppermute | solution.py:309
  41.4 4.1 %shard_map.117 = bf16[16,54,128]{2,1,0:T(8,128)(2,1)} custom-call(s32[2]{0:T(128)S(1)} %pad_add_fusion.refs_0_, bf16[4,2,12,8,128]{4,3,2,1,0:T(8,128)(2,1)S(1)} %get-tuple-element.42.refs_1_, bf16[4,2,12,8,128]{4,3,2,1,0:T(8,128)(2,1)S(1)} %collective-permute-done.13.refs_2_, bf16[4,2,12,8,128]{4,3,2,1,0:T(8,128)(2,1)S(1)} %collective-permute-done.14.refs_3_, ...), custom_call_target="tpu_custom_call" | custom-call | tf_op jit(solution)/shard_map/pallas_call | solution.py:65
  45.4 4.6 %all-to-all-start = ((bf16[16,54,128]{2,1,0:T(8,128)(2,1)}), bf16[16,54,128]{2,1,0:T(8,128)(2,1)S(1)}, u32[]{:S(2)}, u32[]{:S(2)}) async-start(bf16[16,54,128]{2,1,0:T(8,128)(2,1)} %shard_map.117), calls=%async_computation | async-start | bytes 458752 | tf_op jit(solution)/shard_map/all_to_all | solution.py:371
  50.0 1.9 %collective-permute-start.2 = (bf16[2,10,8,512]{3,2,1,0:T(8,128)(2,1)S(1)}, bf16[2,10,8,512]{3,2,1,0:T(8,128)(2,1)S(1)}, u32[]{:S(2)}, u32[]{:S(2)}) collective-permute-start(bf16[2,10,8,512]{3,2,1,0:T(8,128)(2,1)S(1)} %get-tuple-element.30.refs_0_), channel_id=1, source_target_pairs={{0,64},{64,128},{128,192},{192,0},{1,65},{65,129},{129,193},{193,1... | collective-permute-start | bytes 491528 | tf_op jit(solution)/shard_map/ppermute | solution.py:309
  52.0 2.7 %collective-permute-start.3 = (bf16[2,10,8,512]{3,2,1,0:T(8,128)(2,1)S(1)}, bf16[2,10,8,512]{3,2,1,0:T(8,128)(2,1)S(1)}, u32[]{:S(2)}, u32[]{:S(2)}) collective-permute-start(bf16[2,10,8,512]{3,2,1,0:T(8,128)(2,1)S(1)} %get-tuple-element.30.refs_0_), channel_id=1, source_target_pairs={{0,128},{64,192},{128,0},{192,64},{1,129},{65,193},{129,1},{193,65... | collective-permute-start | bytes 491528 | tf_op jit(solution)/shard_map/ppermute | solution.py:309
  54.6 1.5 %collective-permute-start.4 = (bf16[2,10,8,512]{3,2,1,0:T(8,128)(2,1)S(1)}, bf16[2,10,8,512]{3,2,1,0:T(8,128)(2,1)S(1)}, u32[]{:S(2)}, u32[]{:S(2)}) collective-permute-start(bf16[2,10,8,512]{3,2,1,0:T(8,128)(2,1)S(1)} %get-tuple-element.30.refs_0_), channel_id=1, source_target_pairs={{0,192},{64,0},{128,64},{192,128},{1,193},{65,1},{129,65},{193,129... | collective-permute-start | bytes 491528 | tf_op jit(solution)/shard_map/ppermute | solution.py:309
  56.1 4.5 %collective-permute-done.2.refs_1_ = bf16[2,10,8,512]{3,2,1,0:T(8,128)(2,1)S(1)} collective-permute-done((bf16[2,10,8,512]{3,2,1,0:T(8,128)(2,1)S(1)}, bf16[2,10,8,512]{3,2,1,0:T(8,128)(2,1)S(1)}, u32[]{:S(2)}, u32[]{:S(2)}) %collective-permute-start.2) | collective-permute-done | bytes 163872 | tf_op jit(solution)/shard_map/ppermute | solution.py:309
  60.6 3.6 %collective-permute-done.3.refs_2_ = bf16[2,10,8,512]{3,2,1,0:T(8,128)(2,1)S(1)} collective-permute-done((bf16[2,10,8,512]{3,2,1,0:T(8,128)(2,1)S(1)}, bf16[2,10,8,512]{3,2,1,0:T(8,128)(2,1)S(1)}, u32[]{:S(2)}, u32[]{:S(2)}) %collective-permute-start.3) | collective-permute-done | bytes 163872 | tf_op jit(solution)/shard_map/ppermute | solution.py:309
  64.1 4.6 %shard_map.113 = (f32[4,2,8,8,128]{4,3,2,1,0:T(8,128)S(1)}, bf16[4,8,8,128]{3,2,1,0:T(8,128)(2,1)S(1)}, bf16[4,8,8,128]{3,2,1,0:T(8,128)(2,1)S(1)}) custom-call(bf16[2,10,8,512]{3,2,1,0:T(8,128)(2,1)S(1)} %get-tuple-element.30.refs_0_, bf16[2,10,8,512]{3,2,1,0:T(8,128)(2,1)S(1)} %collective-permute-done.2.refs_1_, ...), custom_call_target="tpu_custom_call" | custom-call | tf_op jit(solution)/shard_map/pallas_call | solution.py:65
  68.7 1.9 %collective-permute-start.5 = (bf16[4,8,8,128]{3,2,1,0:T(8,128)(2,1)S(1)}, bf16[4,8,8,128]{3,2,1,0:T(8,128)(2,1)S(1)}, u32[]{:S(2)}, u32[]{:S(2)}) collective-permute-start(bf16[4,8,8,128]{3,2,1,0:T(8,128)(2,1)S(1)} %get-tuple-element.32), channel_id=1, source_target_pairs={{0,1},{1,2},{2,3},{3,4},{4,5},{5,6},{6,7},{7,8},{8,9},{9,10},{10,1... | collective-permute-start | bytes 196616 | tf_op jit(solution)/shard_map/ppermute | solution.py:384
  70.6 3.3 %collective-permute-start.6 = (bf16[4,8,8,128]{3,2,1,0:T(8,128)(2,1)S(1)}, bf16[4,8,8,128]{3,2,1,0:T(8,128)(2,1)S(1)}, u32[]{:S(2)}, u32[]{:S(2)}) collective-permute-start(bf16[4,8,8,128]{3,2,1,0:T(8,128)(2,1)S(1)} %get-tuple-element.33), channel_id=1, source_target_pairs={{0,15},{1,0},{2,1},{3,2},{4,3},{5,4},{6,5},{7,6},{8,7},{9,8},{10,9... | collective-permute-start | bytes 196616 | tf_op jit(solution)/shard_map/ppermute | solution.py:383
  73.8 3.0 %collective-permute-done.5.refs_2_ = bf16[4,8,8,128]{3,2,1,0:T(8,128)(2,1)S(1)} collective-permute-done((bf16[4,8,8,128]{3,2,1,0:T(8,128)(2,1)S(1)}, bf16[4,8,8,128]{3,2,1,0:T(8,128)(2,1)S(1)}, u32[]{:S(2)}, u32[]{:S(2)}) %collective-permute-start.5) | collective-permute-done | bytes 65568 | tf_op jit(solution)/shard_map/ppermute | solution.py:384
  77.0 1.0 %shard_map.114 = (bf16[2,8,8,128]{3,2,1,0:T(8,128)(2,1)S(1)}, bf16[2,8,8,128]{3,2,1,0:T(8,128)(2,1)S(1)}, bf16[2,8,8,128]{3,2,1,0:T(8,128)(2,1)S(1)}, bf16[2,8,8,128]{3,2,1,0:T(8,128)(2,1)S(1)}) custom-call(s32[2]{0:T(128)S(1)} %pad_add_fusion.refs_0_, f32[4,2,8,8,128]{4,3,2,1,0:T(8,128)S(1)} %get-tuple-element.31.refs_1_, ...), custom_call_target="tpu_custom_call" | custom-call | tf_op jit(solution)/shard_map/pallas_call | solution.py:65
  78.0 1.5 %collective-permute-start.7 = (bf16[2,8,8,128]{3,2,1,0:T(8,128)(2,1)S(1)}, bf16[2,8,8,128]{3,2,1,0:T(8,128)(2,1)S(1)}, u32[]{:S(2)}, u32[]{:S(2)}) collective-permute-start(bf16[2,8,8,128]{3,2,1,0:T(8,128)(2,1)S(1)} %get-tuple-element.35), channel_id=1, source_target_pairs={{0,192},{64,0},{128,64},{192,128},{1,193},{65,1},{129,65},{193,129... | collective-permute-start | bytes 98312 | tf_op jit(solution)/shard_map/ppermute | solution.py:309
  81.2 0.8 collective-permute-done.7.refs_3_
  82.0 2.9 %collective-permute-done.8.refs_4_ = bf16[2,8,8,128]{3,2,1,0:T(8,128)(2,1)S(1)} collective-permute-done((bf16[2,8,8,128]{3,2,1,0:T(8,128)(2,1)S(1)}, bf16[2,8,8,128]{3,2,1,0:T(8,128)(2,1)S(1)}, u32[]{:S(2)}, u32[]{:S(2)}) %collective-permute-start.8) | collective-permute-done | bytes 32800 | tf_op jit(solution)/shard_map/ppermute | solution.py:309
  85.4 1.9 %shard_map.115 = bf16[8,8,2,512]{3,2,1,0:T(2,128)(2,1)} custom-call(s32[1]{0:T(128)} %bitcast.refs_0_, bf16[8,8,2,512]{3,2,1,0:T(2,128)(2,1)} %bitcast.11, bf16[2,8,8,128]{3,2,1,0:T(8,128)(2,1)S(1)} %get-tuple-element.34.refs_2_, bf16[2,8,8,128]{3,2,1,0:T(8,128)(2,1)S(1)} %collective-permute-done.7.refs_3_, ...), custom_call_target="tpu_custom_call" | custom-call | tf_op jit(solution)/shard_map/pallas_call | solution.py:65
  (18 shorter events, 3.2 us)
Async XLA Ops:
  3.9 3.3 %collective-permute-start = (bf16[2,8,640]{2,1,0:T(8,128)(2,1)S(1)}, bf16[2,8,640]{2,1,0:T(8,128)(2,1)S(1)}, u32[]{:S(2)}, u32[]{:S(2)}) collective-permute-start(bf16[2,8,640]{2,1,0:T(8,128)(2,1)S(1)} %get-tuple-element.28), channel_id=1, source_target_pairs={{0,16},{16,32},{32,48},{48,0},{1,17},{17,33},{33,49},{49,1},{2,18}... | collective-permute-start | bytes 61448 | tf_op jit(solution)/shard_map/ppermute | solution.py:343
  3.9 3.2 %collective-permute-start.1 = (bf16[2,8,640]{2,1,0:T(8,128)(2,1)S(1)}, bf16[2,8,640]{2,1,0:T(8,128)(2,1)S(1)}, u32[]{:S(2)}, u32[]{:S(2)}) collective-permute-start(bf16[2,8,640]{2,1,0:T(8,128)(2,1)S(1)} %get-tuple-element.29), channel_id=1, source_target_pairs={{0,48},{16,0},{32,16},{48,32},{1,49},{17,1},{33,17},{49,33},{2,50}... | collective-permute-start | bytes 61448 | tf_op jit(solution)/shard_map/ppermute | solution.py:344
  8.9 78.5 %copy-start = (f32[54,128]{1,0:T(8,128)S(1)}, f32[54,128]{1,0:T(8,128)}, u32[]{:S(2)}) copy-start(f32[54,128]{1,0:T(8,128)} %param.13) | copy-start | bytes 82948
  8.9 78.5 %copy-start.1 = (f32[54,128]{1,0:T(8,128)S(1)}, f32[54,128]{1,0:T(8,128)}, u32[]{:S(2)}) copy-start(f32[54,128]{1,0:T(8,128)} %param.12) | copy-start | bytes 82948
  8.9 11.4 %collective-permute-start.10 = (bf16[2,18,8,128]{3,2,1,0:T(8,128)(2,1)S(1)}, bf16[2,18,8,128]{3,2,1,0:T(8,128)(2,1)S(1)}, u32[]{:S(2)}, u32[]{:S(2)}) collective-permute-start(bf16[2,18,8,128]{3,2,1,0:T(8,128)(2,1)S(1)} %get-tuple-element.39), channel_id=1, source_target_pairs={{0,1},{1,2},{2,3},{3,0},{4,5},{5,6},{6,7},{7,4},{8,9},{9,10},{10,1... | collective-permute-start | bytes 221192 | tf_op jit(solution)/shard_map/ppermute | solution.py:309
  12.3 11.3 %collective-permute-start.11 = (bf16[2,18,8,128]{3,2,1,0:T(8,128)(2,1)S(1)}, bf16[2,18,8,128]{3,2,1,0:T(8,128)(2,1)S(1)}, u32[]{:S(2)}, u32[]{:S(2)}) collective-permute-start(bf16[2,18,8,128]{3,2,1,0:T(8,128)(2,1)S(1)} %get-tuple-element.40), channel_id=1, source_target_pairs={{0,2},{1,3},{2,0},{3,1},{4,6},{5,7},{6,4},{7,5},{8,10},{9,11},{10,... | collective-permute-start | bytes 221192 | tf_op jit(solution)/shard_map/ppermute | solution.py:309
  17.6 8.4 %collective-permute-start.12 = (bf16[2,18,8,128]{3,2,1,0:T(8,128)(2,1)S(1)}, bf16[2,18,8,128]{3,2,1,0:T(8,128)(2,1)S(1)}, u32[]{:S(2)}, u32[]{:S(2)}) collective-permute-start(bf16[2,18,8,128]{3,2,1,0:T(8,128)(2,1)S(1)} %get-tuple-element.41), channel_id=1, source_target_pairs={{0,3},{1,0},{2,1},{3,2},{4,7},{5,4},{6,5},{7,6},{8,11},{9,8},{10,9... | collective-permute-start | bytes 221192 | tf_op jit(solution)/shard_map/ppermute | solution.py:309
  28.2 7.8 %collective-permute-start.13 = (bf16[4,2,12,8,128]{4,3,2,1,0:T(8,128)(2,1)S(1)}, bf16[4,2,12,8,128]{4,3,2,1,0:T(8,128)(2,1)S(1)}, u32[]{:S(2)}, u32[]{:S(2)}) collective-permute-start(bf16[4,2,12,8,128]{4,3,2,1,0:T(8,128)(2,1)S(1)} %get-tuple-element.43), channel_id=1, source_target_pairs={{0,4},{4,8},{8,12},{12,0},{1,5},{5,9},{9,13},{13,1},{2,6},{6,10},{... | collective-permute-start | bytes 589832 | tf_op jit(solution)/shard_map/ppermute | solution.py:309
  29.7 9.3 %collective-permute-start.14 = (bf16[4,2,12,8,128]{4,3,2,1,0:T(8,128)(2,1)S(1)}, bf16[4,2,12,8,128]{4,3,2,1,0:T(8,128)(2,1)S(1)}, u32[]{:S(2)}, u32[]{:S(2)}) collective-permute-start(bf16[4,2,12,8,128]{4,3,2,1,0:T(8,128)(2,1)S(1)} %get-tuple-element.44), channel_id=1, source_target_pairs={{0,8},{4,12},{8,0},{12,4},{1,9},{5,13},{9,1},{13,5},{2,10},{6,14},... | collective-permute-start | bytes 589832 | tf_op jit(solution)/shard_map/ppermute | solution.py:309
  30.9 10.5 %collective-permute-start.15 = (bf16[4,2,12,8,128]{4,3,2,1,0:T(8,128)(2,1)S(1)}, bf16[4,2,12,8,128]{4,3,2,1,0:T(8,128)(2,1)S(1)}, u32[]{:S(2)}, u32[]{:S(2)}) collective-permute-start(bf16[4,2,12,8,128]{4,3,2,1,0:T(8,128)(2,1)S(1)} %get-tuple-element.45), channel_id=1, source_target_pairs={{0,12},{4,0},{8,4},{12,8},{1,13},{5,1},{9,5},{13,9},{2,14},{6,2},{... | collective-permute-start | bytes 589832 | tf_op jit(solution)/shard_map/ppermute | solution.py:309
  45.4 41.8 %all-to-all-start = ((bf16[16,54,128]{2,1,0:T(8,128)(2,1)}), bf16[16,54,128]{2,1,0:T(8,128)(2,1)S(1)}, u32[]{:S(2)}, u32[]{:S(2)}) async-start(bf16[16,54,128]{2,1,0:T(8,128)(2,1)} %shard_map.117), calls=%async_computation | async-start | bytes 458752 | tf_op jit(solution)/shard_map/all_to_all | solution.py:371
  50.0 10.5 %collective-permute-start.2 = (bf16[2,10,8,512]{3,2,1,0:T(8,128)(2,1)S(1)}, bf16[2,10,8,512]{3,2,1,0:T(8,128)(2,1)S(1)}, u32[]{:S(2)}, u32[]{:S(2)}) collective-permute-start(bf16[2,10,8,512]{3,2,1,0:T(8,128)(2,1)S(1)} %get-tuple-element.30.refs_0_), channel_id=1, source_target_pairs={{0,64},{64,128},{128,192},{192,0},{1,65},{65,129},{129,193},{193,1... | collective-permute-start | bytes 491528 | tf_op jit(solution)/shard_map/ppermute | solution.py:309
  52.0 12.2 %collective-permute-start.3 = (bf16[2,10,8,512]{3,2,1,0:T(8,128)(2,1)S(1)}, bf16[2,10,8,512]{3,2,1,0:T(8,128)(2,1)S(1)}, u32[]{:S(2)}, u32[]{:S(2)}) collective-permute-start(bf16[2,10,8,512]{3,2,1,0:T(8,128)(2,1)S(1)} %get-tuple-element.30.refs_0_), channel_id=1, source_target_pairs={{0,128},{64,192},{128,0},{192,64},{1,129},{65,193},{129,1},{193,65... | collective-permute-start | bytes 491528 | tf_op jit(solution)/shard_map/ppermute | solution.py:309
  54.6 9.5 %collective-permute-start.4 = (bf16[2,10,8,512]{3,2,1,0:T(8,128)(2,1)S(1)}, bf16[2,10,8,512]{3,2,1,0:T(8,128)(2,1)S(1)}, u32[]{:S(2)}, u32[]{:S(2)}) collective-permute-start(bf16[2,10,8,512]{3,2,1,0:T(8,128)(2,1)S(1)} %get-tuple-element.30.refs_0_), channel_id=1, source_target_pairs={{0,192},{64,0},{128,64},{192,128},{1,193},{65,1},{129,65},{193,129... | collective-permute-start | bytes 491528 | tf_op jit(solution)/shard_map/ppermute | solution.py:309
  68.7 8.1 %collective-permute-start.5 = (bf16[4,8,8,128]{3,2,1,0:T(8,128)(2,1)S(1)}, bf16[4,8,8,128]{3,2,1,0:T(8,128)(2,1)S(1)}, u32[]{:S(2)}, u32[]{:S(2)}) collective-permute-start(bf16[4,8,8,128]{3,2,1,0:T(8,128)(2,1)S(1)} %get-tuple-element.32), channel_id=1, source_target_pairs={{0,1},{1,2},{2,3},{3,4},{4,5},{5,6},{6,7},{7,8},{8,9},{9,10},{10,1... | collective-permute-start | bytes 196616 | tf_op jit(solution)/shard_map/ppermute | solution.py:384
  70.6 6.4 %collective-permute-start.6 = (bf16[4,8,8,128]{3,2,1,0:T(8,128)(2,1)S(1)}, bf16[4,8,8,128]{3,2,1,0:T(8,128)(2,1)S(1)}, u32[]{:S(2)}, u32[]{:S(2)}) collective-permute-start(bf16[4,8,8,128]{3,2,1,0:T(8,128)(2,1)S(1)} %get-tuple-element.33), channel_id=1, source_target_pairs={{0,15},{1,0},{2,1},{3,2},{4,3},{5,4},{6,5},{7,6},{8,7},{9,8},{10,9... | collective-permute-start | bytes 196616 | tf_op jit(solution)/shard_map/ppermute | solution.py:383
  78.0 4.0 %collective-permute-start.7 = (bf16[2,8,8,128]{3,2,1,0:T(8,128)(2,1)S(1)}, bf16[2,8,8,128]{3,2,1,0:T(8,128)(2,1)S(1)}, u32[]{:S(2)}, u32[]{:S(2)}) collective-permute-start(bf16[2,8,8,128]{3,2,1,0:T(8,128)(2,1)S(1)} %get-tuple-element.35), channel_id=1, source_target_pairs={{0,192},{64,0},{128,64},{192,128},{1,193},{65,1},{129,65},{193,129... | collective-permute-start | bytes 98312 | tf_op jit(solution)/shard_map/ppermute | solution.py:309
  79.5 5.4 %collective-permute-start.8 = (bf16[2,8,8,128]{3,2,1,0:T(8,128)(2,1)S(1)}, bf16[2,8,8,128]{3,2,1,0:T(8,128)(2,1)S(1)}, u32[]{:S(2)}, u32[]{:S(2)}) collective-permute-start(bf16[2,8,8,128]{3,2,1,0:T(8,128)(2,1)S(1)} %get-tuple-element.36), channel_id=1, source_target_pairs={{0,128},{64,192},{128,0},{192,64},{1,129},{65,193},{129,1},{193,65... | collective-permute-start | bytes 98312 | tf_op jit(solution)/shard_map/ppermute | solution.py:309
  80.2 5.1 %collective-permute-start.9 = (bf16[2,8,8,128]{3,2,1,0:T(8,128)(2,1)S(1)}, bf16[2,8,8,128]{3,2,1,0:T(8,128)(2,1)S(1)}, u32[]{:S(2)}, u32[]{:S(2)}) collective-permute-start(bf16[2,8,8,128]{3,2,1,0:T(8,128)(2,1)S(1)} %get-tuple-element.37), channel_id=1, source_target_pairs={{0,64},{64,128},{128,192},{192,0},{1,65},{65,129},{129,193},{193,1... | collective-permute-start | bytes 98312 | tf_op jit(solution)/shard_map/ppermute | solution.py:309

commit v3 on v2

--- a/solution.py
+++ b/solution.py
@@ -12,7 +12,7 @@
 
 
 def _call(kernel, ins, outs, scratch=()):
-    moved = [i for i, (_, space) in enumerate(ins) if space in ("hbm", "arg")]
+    moved = [i for i, (_, space) in enumerate(ins) if space == "arg"]
     late = [i for i, (_, space) in enumerate(ins) if space == "late"]
     count = len(ins)
 
@@ -21,10 +21,9 @@
         results = refs[count : count + len(outs)]
         rest = refs[count + len(outs) :]
         in_bufs = rest[: len(moved)]
-        out_bufs = rest[len(moved) : len(moved) + len(outs)]
-        late_bufs = rest[len(moved) + len(outs) :][: len(late)]
-        own = rest[len(moved) + len(outs) + len(late) : -3]
-        in_sem, late_sem, out_sem = rest[-3:]
+        late_bufs = rest[len(moved) :][: len(late)]
+        own = rest[len(moved) + len(late) : -2]
+        in_sem, late_sem = rest[-2:]
         copies = []
         for n, i in enumerate(moved):
             copies.append(pltpu.make_async_copy(given[i], in_bufs[n], in_sem.at[n]))
@@ -46,17 +45,9 @@
             copy.start()
         for copy in copies:
             copy.wait()
-        kernel(*given, *out_bufs, *own)
-        copies = [
-            pltpu.make_async_copy(out_bufs[n], results[n], out_sem.at[n]) for n in range(len(outs))
-        ]
-        for copy in copies:
-            copy.start()
-        for copy in copies:
-            copy.wait()
+        kernel(*given, *results, *own)
 
     buffers = [pltpu.VMEM(ins[i][0].shape, ins[i][0].dtype) for i in moved]
-    buffers += [pltpu.VMEM(shape, dtype) for shape, dtype in outs]
     buffers += [pltpu.VMEM(ins[i][0].shape, ins[i][0].dtype) for i in late]
     arrays = [
         pltpu.with_memory_space_constraint(array, pltpu.HBM) if space in ("arg", "late") else array
@@ -66,16 +57,17 @@
         run,
         out_shape=[jax.ShapeDtypeStruct(shape, dtype) for shape, dtype in outs],
         in_specs=[
-            pl.BlockSpec(memory_space=pltpu.SMEM if space == "smem" else pltpu.HBM)
+            pl.BlockSpec(
+                memory_space={"smem": pltpu.SMEM, "vmem": pltpu.VMEM}.get(space, pltpu.HBM)
+            )
             for _, space in ins
         ],
-        out_specs=[pl.BlockSpec(memory_space=pltpu.HBM) for _ in outs],
+        out_specs=[pl.BlockSpec(memory_space=pltpu.VMEM) for _ in outs],
         scratch_shapes=buffers
         + list(scratch)
         + [
             pltpu.SemaphoreType.DMA((max(1, len(moved)),)),
             pltpu.SemaphoreType.DMA((max(1, 3 * len(late)),)),
-            pltpu.SemaphoreType.DMA((len(outs),)),
         ],
         compiler_params=pltpu.CompilerParams(vmem_limit_bytes=40 * 1024 * 1024),
     )(*arrays)
@@ -107,7 +99,7 @@
     return jnp.concatenate(tiles, axis=1)
 
 
-def prepare(seed, pre, up, inp, g_out, proj_out, in_out, top_out, bot_out, s_pre, s_up, s_in):
+def prepare(seed, pre, up, inp, g_out, proj_out, in_out, top_out, bot_out, up_out, s_pre, s_up, s_in):
     frames, rows, cols, chans = pre.shape
     rank = proj_out.shape[-1]
     _rows_to_scratch(pre, s_pre)
@@ -133,6 +125,7 @@
     g4 = g.reshape(cols, rows, frames, chans)
     p4 = proj.reshape(cols, rows, frames, rank)
     g_out[...] = g4
+    up_out[...] = u.astype(BF16).reshape(cols, rows, frames, chans)
     proj_out[...] = p4
     top_out[:, :, :chans] = g4[:, 0]
     bot_out[:, :, :chans] = g4[:, rows - 1]
@@ -283,14 +276,15 @@
 
 
 def finish_kernel(pos, up, p0, p1, p2, p3, out, flat, outflat):
-    frames, rows, cols, _ = up.shape
-    _rows_to_scratch(up, flat)
+    cols, rows, frames, _ = up.shape
+    for tile in range(4):
+        flat[tile] = up[:, :, :, tile * 128 : tile * 128 + 128].astype(F32)
     for k, part in enumerate((p0, p1, p2, p3)):
         tile = lax.rem(pos[0] + k, 4)
+        total = flat[tile] + part[...].astype(F32)
         for w in range(cols):
             for h in range(rows):
-                at = pl.ds(h * cols + w, frames, stride=rows * cols)
-                outflat[tile, at, :] = flat[tile, at, :] + part[w, h].astype(F32)
+                outflat[tile, pl.ds(h * cols + w, frames, stride=rows * cols), :] = total[w, h]
     for t in range(frames):
         for h in range(rows):
             base = (t * rows + h) * cols
@@ -318,7 +312,7 @@
     tokens = frames * rows * cols
     sx = ("sxx", "sxz")
     spread = pltpu.VMEM((chans // 128, tokens, 128), F32)
-    g, proj, chunks, top, bot = _call(
+    g, proj, chunks, top, bot, up = _call(
         prepare,
         [
             (hash_seed.reshape(1), "smem"),
@@ -332,6 +326,7 @@
             ((16, cols, 2, frames, 128), BF16),
             ((cols, frames, chans + rank), BF16),
             ((cols, frames, chans + rank), BF16),
+            ((cols, rows, frames, chans), BF16),
         ],
         [spread] * 3,
     )
@@ -347,20 +342,20 @@
     g, *sends = _call(
         assemble,
         [places("sy", "sxx", "sxz")]
-        + [(a, "hbm") for a in (g, proj, chunks, above, below)],
+        + [(a, "vmem") for a in (g, proj, chunks, above, below)],
         [((cols, rows + 2, frames, chans), BF16)] + [along_z] * 4,
     )
     got = around(sends, "sxz")
     sends = _call(
         across_x,
-        [places("sy", "sxx", "sxz")] + [(a, "hbm") for a in got],
+        [places("sy", "sxx", "sxz")] + [(a, "vmem") for a in got],
         [along_x] * 4,
     )
     got = around(sends, "sxx")
     g_all = around([g] * 4, "dp")
     (terms,) = _call(
         moment_kernel,
-        [places("sxx", "sxz")] + [(a, "hbm") for a in got],
+        [places("sxx", "sxz")] + [(a, "vmem") for a in got],
         [((16, 54, rank), BF16)],
         [
             pltpu.VMEM((16 * cols + 2, rows + 2, frames, rank), BF16),
@@ -372,7 +367,7 @@
 
     own, left, right = _call(
         branch_kernel,
-        [(x, "hbm") for x in g_all] + [(weight, "late")],
+        [(x, "vmem") for x in g_all] + [(weight, "late")],
         [
             ((4, cols, rows, frames, 128), F32),
             ((4, rows, frames, 128), BF16),
@@ -384,15 +379,15 @@
     from_left = lax.ppermute(right, sx, ring(sx, 1))
     mine = _call(
         merge_kernel,
-        [places("sxx", "sxz")] + [(a, "hbm") for a in (own, from_left, from_right)],
+        [places("sxx", "sxz")] + [(a, "vmem") for a in (own, from_left, from_right)],
         [((cols, rows, frames, 128), BF16)] * 4,
     )
     parts = around(mine, "dp", -1)
     (input_grad,) = _call(
         finish_kernel,
-        [places("dp"), (upstream[0], "arg")] + [(a, "hbm") for a in parts],
+        [places("dp"), (up, "vmem")] + [(a, "vmem") for a in parts],
         [((frames, rows, cols, chans), BF16)],
-        [spread] * 2,
+        [pltpu.VMEM((chans // 128, cols, rows, frames, 128), F32), spread],
     )
 
     total = 32768

time: 89.7 us -> 83.9 us (0.935)
  Pallas kernels: 17.9 us -> 12.1 us
    pallas_call x7, Pallas kernels: 17.9 us -> 12.1 us  [_call(): pl.pallas_call(run, out_shape=[jax.ShapeDtypeStruct(shape, dtype) for sha...]
  transfers between devices with their start and end apart: 17 -> 17, of which waited for: 13 -> 12; matrix products, arithmetic and copies ran while one was open for 0% -> 0% of each run, Pallas kernels for 8% -> 7%
where the time goes in v3:
time: 83.9 us; the launch traced here: 82.8 us
  starting transfers between devices  36.3 us (43%)
  waiting for transfers between devices  30.7 us (37%)
  Pallas kernels  12.1 us (14%)
  between operations  2.15 us (3%)
  other arithmetic  1.46 us (2%)
    ppermute x12, waiting for transfers between devices, around(): got[k] = lax.ppermute(arrays[k], axis, ring(axis, sign * k))  26.2 us
    ppermute x12, starting transfers between devices, around(): got[k] = lax.ppermute(arrays[k], axis, ring(axis, sign * k))  24.8 us
    pallas_call x7, Pallas kernels, _call(): pl.pallas_call(run, out_shape=[jax.ShapeDtypeStruct(shape, dtype) for sha...  12.1 us
    all_to_all x1, starting transfers between devices, step(): terms = lax.all_to_all(terms, ('dp', 'sy'), 0, 0, tiled=True)  4.58 us
    ppermute x1, starting transfers between devices, step(): from_right = lax.ppermute(left, sx, ring(sx, -1))  3.26 us
    ppermute x1, waiting for transfers between devices, step(): from_left = lax.ppermute(right, sx, ring(sx, 1))  3.05 us
    ppermute x1, starting transfers between devices, step(): from_left = lax.ppermute(right, sx, ring(sx, 1))  1.85 us
    ppermute x1, starting transfers between devices, step(): below = lax.ppermute(top, 'sy', ring('sy', -1))  1.73 us
  transfers between devices with their start and end apart: 17, of which 12 were waited for; matrix products, arithmetic and copies ran while one was open for 0% of the time, Pallas kernels for 7%

profile of v3, /device:TPU:2, one launch (start us, length us, event | category | flops | bytes accessed | tf_op | source)
XLA Modules:
  0.0 82.8 jit_solution(30303132274784873)
XLA Ops:
  1.3 2.1 %shard_map.111 = (bf16[2,8,8,512]{3,2,1,0:T(8,128)(2,1)S(1)}, bf16[2,8,8,128]{3,2,1,0:T(8,128)(2,1)S(1)}, bf16[16,2,2,8,128]{4,3,2,1,0:T(8,128)(2,1)S(1)}, bf16[...) custom-call(s32[1]{0:T(128)} %bitcast.9.refs_0_, ...), custom_call_target="tpu_custom_call" | custom-call | tf_op jit(solution)/shard_map/pallas_call | solution.py:56
  3.5 1.7 %collective-permute-start.1 = (bf16[2,8,640]{2,1,0:T(8,128)(2,1)S(1)}, bf16[2,8,640]{2,1,0:T(8,128)(2,1)S(1)}, u32[]{:S(2)}, u32[]{:S(2)}) collective-permute-start(bf16[2,8,640]{2,1,0:T(8,128)(2,1)S(1)} %get-tuple-element.31), channel_id=1, source_target_pairs={{0,48},{16,0},{32,16},{48,32},{1,49},{17,1},{33,17},{49,33},{2,50}... | collective-permute-start | bytes 61448 | tf_op jit(solution)/shard_map/ppermute | solution.py:339
  5.3 1.4 %collective-permute-done.refs_4_ = bf16[2,8,640]{2,1,0:T(8,128)(2,1)S(1)} collective-permute-done((bf16[2,8,640]{2,1,0:T(8,128)(2,1)S(1)}, bf16[2,8,640]{2,1,0:T(8,128)(2,1)S(1)}, u32[]{:S(2)}, u32[]{:S(2)}) %collective-permute-start) | collective-permute-done | bytes 20512 | tf_op jit(solution)/shard_map/ppermute | solution.py:338
  7.3 3.3 %collective-permute-start.10 = (bf16[2,18,8,128]{3,2,1,0:T(8,128)(2,1)S(1)}, bf16[2,18,8,128]{3,2,1,0:T(8,128)(2,1)S(1)}, u32[]{:S(2)}, u32[]{:S(2)}) collective-permute-start(bf16[2,18,8,128]{3,2,1,0:T(8,128)(2,1)S(1)} %get-tuple-element.41), channel_id=1, source_target_pairs={{0,1},{1,2},{2,3},{3,0},{4,5},{5,6},{6,7},{7,4},{8,9},{9,10},{10,1... | collective-permute-start | bytes 221192 | tf_op jit(solution)/shard_map/ppermute | solution.py:303
  10.7 5.4 %collective-permute-start.11 = (bf16[2,18,8,128]{3,2,1,0:T(8,128)(2,1)S(1)}, bf16[2,18,8,128]{3,2,1,0:T(8,128)(2,1)S(1)}, u32[]{:S(2)}, u32[]{:S(2)}) collective-permute-start(bf16[2,18,8,128]{3,2,1,0:T(8,128)(2,1)S(1)} %get-tuple-element.42), channel_id=1, source_target_pairs={{0,2},{1,3},{2,0},{3,1},{4,6},{5,7},{6,4},{7,5},{8,10},{9,11},{10,... | collective-permute-start | bytes 221192 | tf_op jit(solution)/shard_map/ppermute | solution.py:303
  16.1 2.7 %collective-permute-start.12 = (bf16[2,18,8,128]{3,2,1,0:T(8,128)(2,1)S(1)}, bf16[2,18,8,128]{3,2,1,0:T(8,128)(2,1)S(1)}, u32[]{:S(2)}, u32[]{:S(2)}) collective-permute-start(bf16[2,18,8,128]{3,2,1,0:T(8,128)(2,1)S(1)} %get-tuple-element.43), channel_id=1, source_target_pairs={{0,3},{1,0},{2,1},{3,2},{4,7},{5,4},{6,5},{7,6},{8,11},{9,8},{10,9... | collective-permute-start | bytes 221192 | tf_op jit(solution)/shard_map/ppermute | solution.py:303
  18.7 3.2 %collective-permute-done.11.refs_3_ = bf16[2,18,8,128]{3,2,1,0:T(8,128)(2,1)S(1)} collective-permute-done((bf16[2,18,8,128]{3,2,1,0:T(8,128)(2,1)S(1)}, bf16[2,18,8,128]{3,2,1,0:T(8,128)(2,1)S(1)}, u32[]{:S(2)}, u32[]{:S(2)}) %collective-permute-start.11) | collective-permute-done | bytes 73760 | tf_op jit(solution)/shard_map/ppermute | solution.py:303
  21.9 2.6 %collective-permute-done.12.refs_4_ = bf16[2,18,8,128]{3,2,1,0:T(8,128)(2,1)S(1)} collective-permute-done((bf16[2,18,8,128]{3,2,1,0:T(8,128)(2,1)S(1)}, bf16[2,18,8,128]{3,2,1,0:T(8,128)(2,1)S(1)}, u32[]{:S(2)}, u32[]{:S(2)}) %collective-permute-start.12) | collective-permute-done | bytes 73760 | tf_op jit(solution)/shard_map/ppermute | solution.py:303
  24.5 0.6 shard_map.116
  25.1 1.6 %collective-permute-start.13 = (bf16[4,2,12,8,128]{4,3,2,1,0:T(8,128)(2,1)S(1)}, bf16[4,2,12,8,128]{4,3,2,1,0:T(8,128)(2,1)S(1)}, u32[]{:S(2)}, u32[]{:S(2)}) collective-permute-start(bf16[4,2,12,8,128]{4,3,2,1,0:T(8,128)(2,1)S(1)} %get-tuple-element.45), channel_id=1, source_target_pairs={{0,4},{4,8},{8,12},{12,0},{1,5},{5,9},{9,13},{13,1},{2,6},{6,10},{... | collective-permute-start | bytes 589832 | tf_op jit(solution)/shard_map/ppermute | solution.py:303
  26.7 1.1 %collective-permute-start.14 = (bf16[4,2,12,8,128]{4,3,2,1,0:T(8,128)(2,1)S(1)}, bf16[4,2,12,8,128]{4,3,2,1,0:T(8,128)(2,1)S(1)}, u32[]{:S(2)}, u32[]{:S(2)}) collective-permute-start(bf16[4,2,12,8,128]{4,3,2,1,0:T(8,128)(2,1)S(1)} %get-tuple-element.46), channel_id=1, source_target_pairs={{0,8},{4,12},{8,0},{12,4},{1,9},{5,13},{9,1},{13,5},{2,10},{6,14},... | collective-permute-start | bytes 589832 | tf_op jit(solution)/shard_map/ppermute | solution.py:303
  27.8 2.1 %collective-permute-start.15 = (bf16[4,2,12,8,128]{4,3,2,1,0:T(8,128)(2,1)S(1)}, bf16[4,2,12,8,128]{4,3,2,1,0:T(8,128)(2,1)S(1)}, u32[]{:S(2)}, u32[]{:S(2)}) collective-permute-start(bf16[4,2,12,8,128]{4,3,2,1,0:T(8,128)(2,1)S(1)} %get-tuple-element.47), channel_id=1, source_target_pairs={{0,12},{4,0},{8,4},{12,8},{1,13},{5,1},{9,5},{13,9},{2,14},{6,2},{... | collective-permute-start | bytes 589832 | tf_op jit(solution)/shard_map/ppermute | solution.py:303
  30.0 2.9 %collective-permute-done.13.refs_2_ = bf16[4,2,12,8,128]{4,3,2,1,0:T(8,128)(2,1)S(1)} collective-permute-done((bf16[4,2,12,8,128]{4,3,2,1,0:T(8,128)(2,1)S(1)}, bf16[4,2,12,8,128]{4,3,2,1,0:T(8,128)(2,1)S(1)}, u32[]{:S(2)}, u32[]{:S(2)}) %collective-permute-start.13) | collective-permute-done | bytes 196640 | tf_op jit(solution)/shard_map/ppermute | solution.py:303
  33.0 3.0 %collective-permute-done.14.refs_3_ = bf16[4,2,12,8,128]{4,3,2,1,0:T(8,128)(2,1)S(1)} collective-permute-done((bf16[4,2,12,8,128]{4,3,2,1,0:T(8,128)(2,1)S(1)}, bf16[4,2,12,8,128]{4,3,2,1,0:T(8,128)(2,1)S(1)}, u32[]{:S(2)}, u32[]{:S(2)}) %collective-permute-start.14) | collective-permute-done | bytes 196640 | tf_op jit(solution)/shard_map/ppermute | solution.py:303
  36.0 2.4 %collective-permute-done.15.refs_4_ = bf16[4,2,12,8,128]{4,3,2,1,0:T(8,128)(2,1)S(1)} collective-permute-done((bf16[4,2,12,8,128]{4,3,2,1,0:T(8,128)(2,1)S(1)}, bf16[4,2,12,8,128]{4,3,2,1,0:T(8,128)(2,1)S(1)}, u32[]{:S(2)}, u32[]{:S(2)}) %collective-permute-start.15) | collective-permute-done | bytes 196640 | tf_op jit(solution)/shard_map/ppermute | solution.py:303
  38.3 3.0 %shard_map.117 = bf16[16,54,128]{2,1,0:T(8,128)(2,1)} custom-call(s32[2]{0:T(128)S(1)} %pad_add_fusion.refs_0_, bf16[4,2,12,8,128]{4,3,2,1,0:T(8,128)(2,1)S(1)} %get-tuple-element.44.refs_1_, bf16[4,2,12,8,128]{4,3,2,1,0:T(8,128)(2,1)S(1)} %collective-permute-done.13.refs_2_, bf16[4,2,12,8,128]{4,3,2,1,0:T(8,128)(2,1)S(1)} %collective-permute-done.14.refs_3_, ...), custom_call_target="tpu_custom_call" | custom-call | tf_op jit(solution)/shard_map/pallas_call | solution.py:56
  41.4 4.6 %all-to-all-start = ((bf16[16,54,128]{2,1,0:T(8,128)(2,1)}), bf16[16,54,128]{2,1,0:T(8,128)(2,1)S(1)}, u32[]{:S(2)}, u32[]{:S(2)}) async-start(bf16[16,54,128]{2,1,0:T(8,128)(2,1)} %shard_map.117), calls=%async_computation | async-start | bytes 458752 | tf_op jit(solution)/shard_map/all_to_all | solution.py:366
  46.0 1.9 %collective-permute-start.2 = (bf16[2,10,8,512]{3,2,1,0:T(8,128)(2,1)S(1)}, bf16[2,10,8,512]{3,2,1,0:T(8,128)(2,1)S(1)}, u32[]{:S(2)}, u32[]{:S(2)}) collective-permute-start(bf16[2,10,8,512]{3,2,1,0:T(8,128)(2,1)S(1)} %get-tuple-element.32.refs_0_), channel_id=1, source_target_pairs={{0,64},{64,128},{128,192},{192,0},{1,65},{65,129},{129,193},{193,1... | collective-permute-start | bytes 491528 | tf_op jit(solution)/shard_map/ppermute | solution.py:303
  47.9 2.7 %collective-permute-start.3 = (bf16[2,10,8,512]{3,2,1,0:T(8,128)(2,1)S(1)}, bf16[2,10,8,512]{3,2,1,0:T(8,128)(2,1)S(1)}, u32[]{:S(2)}, u32[]{:S(2)}) collective-permute-start(bf16[2,10,8,512]{3,2,1,0:T(8,128)(2,1)S(1)} %get-tuple-element.32.refs_0_), channel_id=1, source_target_pairs={{0,128},{64,192},{128,0},{192,64},{1,129},{65,193},{129,1},{193,65... | collective-permute-start | bytes 491528 | tf_op jit(solution)/shard_map/ppermute | solution.py:303
  50.6 1.5 %collective-permute-start.4 = (bf16[2,10,8,512]{3,2,1,0:T(8,128)(2,1)S(1)}, bf16[2,10,8,512]{3,2,1,0:T(8,128)(2,1)S(1)}, u32[]{:S(2)}, u32[]{:S(2)}) collective-permute-start(bf16[2,10,8,512]{3,2,1,0:T(8,128)(2,1)S(1)} %get-tuple-element.32.refs_0_), channel_id=1, source_target_pairs={{0,192},{64,0},{128,64},{192,128},{1,193},{65,1},{129,65},{193,129... | collective-permute-start | bytes 491528 | tf_op jit(solution)/shard_map/ppermute | solution.py:303
  52.0 4.5 %collective-permute-done.2.refs_1_ = bf16[2,10,8,512]{3,2,1,0:T(8,128)(2,1)S(1)} collective-permute-done((bf16[2,10,8,512]{3,2,1,0:T(8,128)(2,1)S(1)}, bf16[2,10,8,512]{3,2,1,0:T(8,128)(2,1)S(1)}, u32[]{:S(2)}, u32[]{:S(2)}) %collective-permute-start.2) | collective-permute-done | bytes 163872 | tf_op jit(solution)/shard_map/ppermute | solution.py:303
  56.5 3.6 %collective-permute-done.3.refs_2_ = bf16[2,10,8,512]{3,2,1,0:T(8,128)(2,1)S(1)} collective-permute-done((bf16[2,10,8,512]{3,2,1,0:T(8,128)(2,1)S(1)}, bf16[2,10,8,512]{3,2,1,0:T(8,128)(2,1)S(1)}, u32[]{:S(2)}, u32[]{:S(2)}) %collective-permute-start.3) | collective-permute-done | bytes 163872 | tf_op jit(solution)/shard_map/ppermute | solution.py:303
  60.0 4.3 %shard_map.113 = (f32[4,2,8,8,128]{4,3,2,1,0:T(8,128)S(1)}, bf16[4,8,8,128]{3,2,1,0:T(8,128)(2,1)S(1)}, bf16[4,8,8,128]{3,2,1,0:T(8,128)(2,1)S(1)}) custom-call(bf16[2,10,8,512]{3,2,1,0:T(8,128)(2,1)S(1)} %get-tuple-element.32.refs_0_, bf16[2,10,8,512]{3,2,1,0:T(8,128)(2,1)S(1)} %collective-permute-done.2.refs_1_, ...), custom_call_target="tpu_custom_call" | custom-call | tf_op jit(solution)/shard_map/pallas_call | solution.py:56
  64.4 1.8 %collective-permute-start.5 = (bf16[4,8,8,128]{3,2,1,0:T(8,128)(2,1)S(1)}, bf16[4,8,8,128]{3,2,1,0:T(8,128)(2,1)S(1)}, u32[]{:S(2)}, u32[]{:S(2)}) collective-permute-start(bf16[4,8,8,128]{3,2,1,0:T(8,128)(2,1)S(1)} %get-tuple-element.34), channel_id=1, source_target_pairs={{0,1},{1,2},{2,3},{3,4},{4,5},{5,6},{6,7},{7,8},{8,9},{9,10},{10,1... | collective-permute-start | bytes 196616 | tf_op jit(solution)/shard_map/ppermute | solution.py:379
  66.2 3.3 %collective-permute-start.6 = (bf16[4,8,8,128]{3,2,1,0:T(8,128)(2,1)S(1)}, bf16[4,8,8,128]{3,2,1,0:T(8,128)(2,1)S(1)}, u32[]{:S(2)}, u32[]{:S(2)}) collective-permute-start(bf16[4,8,8,128]{3,2,1,0:T(8,128)(2,1)S(1)} %get-tuple-element.35), channel_id=1, source_target_pairs={{0,15},{1,0},{2,1},{3,2},{4,3},{5,4},{6,5},{7,6},{8,7},{9,8},{10,9... | collective-permute-start | bytes 196616 | tf_op jit(solution)/shard_map/ppermute | solution.py:378
  69.5 3.1 %collective-permute-done.5.refs_2_ = bf16[4,8,8,128]{3,2,1,0:T(8,128)(2,1)S(1)} collective-permute-done((bf16[4,8,8,128]{3,2,1,0:T(8,128)(2,1)S(1)}, bf16[4,8,8,128]{3,2,1,0:T(8,128)(2,1)S(1)}, u32[]{:S(2)}, u32[]{:S(2)}) %collective-permute-start.5) | collective-permute-done | bytes 65568 | tf_op jit(solution)/shard_map/ppermute | solution.py:379
  73.2 1.5 %collective-permute-start.7 = (bf16[2,8,8,128]{3,2,1,0:T(8,128)(2,1)S(1)}, bf16[2,8,8,128]{3,2,1,0:T(8,128)(2,1)S(1)}, u32[]{:S(2)}, u32[]{:S(2)}) collective-permute-start(bf16[2,8,8,128]{3,2,1,0:T(8,128)(2,1)S(1)} %get-tuple-element.37), channel_id=1, source_target_pairs={{0,192},{64,0},{128,64},{192,128},{1,193},{65,1},{129,65},{193,129... | collective-permute-start | bytes 98312 | tf_op jit(solution)/shard_map/ppermute | solution.py:303
  74.7 0.8 collective-permute-start.8
  76.5 0.7 collective-permute-done.7.refs_3_
  77.2 2.9 %collective-permute-done.8.refs_4_ = bf16[2,8,8,128]{3,2,1,0:T(8,128)(2,1)S(1)} collective-permute-done((bf16[2,8,8,128]{3,2,1,0:T(8,128)(2,1)S(1)}, bf16[2,8,8,128]{3,2,1,0:T(8,128)(2,1)S(1)}, u32[]{:S(2)}, u32[]{:S(2)}) %collective-permute-start.8) | collective-permute-done | bytes 32800 | tf_op jit(solution)/shard_map/ppermute | solution.py:303
  80.6 0.8 %shard_map.115 = bf16[8,8,2,512]{3,2,1,0:T(2,128)(2,1)} custom-call(s32[1]{0:T(128)} %bitcast.refs_0_, bf16[2,8,8,512]{3,2,1,0:T(8,128)(2,1)S(1)} %get-tuple-element.26.refs_1_, bf16[2,8,8,128]{3,2,1,0:T(8,128)(2,1)S(1)} %get-tuple-element.36.refs_2_, bf16[2,8,8,128]{3,2,1,0:T(8,128)(2,1)S(1)} %collective-permute-done.7.refs_3_, ...), custom_call_target="tpu_custom_call" | custom-call | tf_op jit(solution)/shard_map/pallas_call | solution.py:56
  81.5 0.7 multiply_reduce_fusion.1
  (18 shorter events, 2.8 us)
Async XLA Ops:
  3.4 3.3 %collective-permute-start = (bf16[2,8,640]{2,1,0:T(8,128)(2,1)S(1)}, bf16[2,8,640]{2,1,0:T(8,128)(2,1)S(1)}, u32[]{:S(2)}, u32[]{:S(2)}) collective-permute-start(bf16[2,8,640]{2,1,0:T(8,128)(2,1)S(1)} %get-tuple-element.30), channel_id=1, source_target_pairs={{0,16},{16,32},{32,48},{48,0},{1,17},{17,33},{33,49},{49,1},{2,18}... | collective-permute-start | bytes 61448 | tf_op jit(solution)/shard_map/ppermute | solution.py:338
  3.5 3.2 %collective-permute-start.1 = (bf16[2,8,640]{2,1,0:T(8,128)(2,1)S(1)}, bf16[2,8,640]{2,1,0:T(8,128)(2,1)S(1)}, u32[]{:S(2)}, u32[]{:S(2)}) collective-permute-start(bf16[2,8,640]{2,1,0:T(8,128)(2,1)S(1)} %get-tuple-element.31), channel_id=1, source_target_pairs={{0,48},{16,0},{32,16},{48,32},{1,49},{17,1},{33,17},{49,33},{2,50}... | collective-permute-start | bytes 61448 | tf_op jit(solution)/shard_map/ppermute | solution.py:339
  7.3 74.2 %copy-start = (f32[54,128]{1,0:T(8,128)S(1)}, f32[54,128]{1,0:T(8,128)}, u32[]{:S(2)}) copy-start(f32[54,128]{1,0:T(8,128)} %param.13) | copy-start | bytes 82948
  7.3 74.2 %copy-start.1 = (f32[54,128]{1,0:T(8,128)S(1)}, f32[54,128]{1,0:T(8,128)}, u32[]{:S(2)}) copy-start(f32[54,128]{1,0:T(8,128)} %param.12) | copy-start | bytes 82948
  7.3 11.4 %collective-permute-start.10 = (bf16[2,18,8,128]{3,2,1,0:T(8,128)(2,1)S(1)}, bf16[2,18,8,128]{3,2,1,0:T(8,128)(2,1)S(1)}, u32[]{:S(2)}, u32[]{:S(2)}) collective-permute-start(bf16[2,18,8,128]{3,2,1,0:T(8,128)(2,1)S(1)} %get-tuple-element.41), channel_id=1, source_target_pairs={{0,1},{1,2},{2,3},{3,0},{4,5},{5,6},{6,7},{7,4},{8,9},{9,10},{10,1... | collective-permute-start | bytes 221192 | tf_op jit(solution)/shard_map/ppermute | solution.py:303
  10.7 11.3 %collective-permute-start.11 = (bf16[2,18,8,128]{3,2,1,0:T(8,128)(2,1)S(1)}, bf16[2,18,8,128]{3,2,1,0:T(8,128)(2,1)S(1)}, u32[]{:S(2)}, u32[]{:S(2)}) collective-permute-start(bf16[2,18,8,128]{3,2,1,0:T(8,128)(2,1)S(1)} %get-tuple-element.42), channel_id=1, source_target_pairs={{0,2},{1,3},{2,0},{3,1},{4,6},{5,7},{6,4},{7,5},{8,10},{9,11},{10,... | collective-permute-start | bytes 221192 | tf_op jit(solution)/shard_map/ppermute | solution.py:303
  16.1 8.4 %collective-permute-start.12 = (bf16[2,18,8,128]{3,2,1,0:T(8,128)(2,1)S(1)}, bf16[2,18,8,128]{3,2,1,0:T(8,128)(2,1)S(1)}, u32[]{:S(2)}, u32[]{:S(2)}) collective-permute-start(bf16[2,18,8,128]{3,2,1,0:T(8,128)(2,1)S(1)} %get-tuple-element.43), channel_id=1, source_target_pairs={{0,3},{1,0},{2,1},{3,2},{4,7},{5,4},{6,5},{7,6},{8,11},{9,8},{10,9... | collective-permute-start | bytes 221192 | tf_op jit(solution)/shard_map/ppermute | solution.py:303
  25.1 7.8 %collective-permute-start.13 = (bf16[4,2,12,8,128]{4,3,2,1,0:T(8,128)(2,1)S(1)}, bf16[4,2,12,8,128]{4,3,2,1,0:T(8,128)(2,1)S(1)}, u32[]{:S(2)}, u32[]{:S(2)}) collective-permute-start(bf16[4,2,12,8,128]{4,3,2,1,0:T(8,128)(2,1)S(1)} %get-tuple-element.45), channel_id=1, source_target_pairs={{0,4},{4,8},{8,12},{12,0},{1,5},{5,9},{9,13},{13,1},{2,6},{6,10},{... | collective-permute-start | bytes 589832 | tf_op jit(solution)/shard_map/ppermute | solution.py:303
  26.7 9.3 %collective-permute-start.14 = (bf16[4,2,12,8,128]{4,3,2,1,0:T(8,128)(2,1)S(1)}, bf16[4,2,12,8,128]{4,3,2,1,0:T(8,128)(2,1)S(1)}, u32[]{:S(2)}, u32[]{:S(2)}) collective-permute-start(bf16[4,2,12,8,128]{4,3,2,1,0:T(8,128)(2,1)S(1)} %get-tuple-element.46), channel_id=1, source_target_pairs={{0,8},{4,12},{8,0},{12,4},{1,9},{5,13},{9,1},{13,5},{2,10},{6,14},... | collective-permute-start | bytes 589832 | tf_op jit(solution)/shard_map/ppermute | solution.py:303
  27.8 10.5 %collective-permute-start.15 = (bf16[4,2,12,8,128]{4,3,2,1,0:T(8,128)(2,1)S(1)}, bf16[4,2,12,8,128]{4,3,2,1,0:T(8,128)(2,1)S(1)}, u32[]{:S(2)}, u32[]{:S(2)}) collective-permute-start(bf16[4,2,12,8,128]{4,3,2,1,0:T(8,128)(2,1)S(1)} %get-tuple-element.47), channel_id=1, source_target_pairs={{0,12},{4,0},{8,4},{12,8},{1,13},{5,1},{9,5},{13,9},{2,14},{6,2},{... | collective-permute-start | bytes 589832 | tf_op jit(solution)/shard_map/ppermute | solution.py:303
  41.4 40.1 %all-to-all-start = ((bf16[16,54,128]{2,1,0:T(8,128)(2,1)}), bf16[16,54,128]{2,1,0:T(8,128)(2,1)S(1)}, u32[]{:S(2)}, u32[]{:S(2)}) async-start(bf16[16,54,128]{2,1,0:T(8,128)(2,1)} %shard_map.117), calls=%async_computation | async-start | bytes 458752 | tf_op jit(solution)/shard_map/all_to_all | solution.py:366
  46.0 10.5 %collective-permute-start.2 = (bf16[2,10,8,512]{3,2,1,0:T(8,128)(2,1)S(1)}, bf16[2,10,8,512]{3,2,1,0:T(8,128)(2,1)S(1)}, u32[]{:S(2)}, u32[]{:S(2)}) collective-permute-start(bf16[2,10,8,512]{3,2,1,0:T(8,128)(2,1)S(1)} %get-tuple-element.32.refs_0_), channel_id=1, source_target_pairs={{0,64},{64,128},{128,192},{192,0},{1,65},{65,129},{129,193},{193,1... | collective-permute-start | bytes 491528 | tf_op jit(solution)/shard_map/ppermute | solution.py:303
  47.9 12.2 %collective-permute-start.3 = (bf16[2,10,8,512]{3,2,1,0:T(8,128)(2,1)S(1)}, bf16[2,10,8,512]{3,2,1,0:T(8,128)(2,1)S(1)}, u32[]{:S(2)}, u32[]{:S(2)}) collective-permute-start(bf16[2,10,8,512]{3,2,1,0:T(8,128)(2,1)S(1)} %get-tuple-element.32.refs_0_), channel_id=1, source_target_pairs={{0,128},{64,192},{128,0},{192,64},{1,129},{65,193},{129,1},{193,65... | collective-permute-start | bytes 491528 | tf_op jit(solution)/shard_map/ppermute | solution.py:303
  50.6 9.5 %collective-permute-start.4 = (bf16[2,10,8,512]{3,2,1,0:T(8,128)(2,1)S(1)}, bf16[2,10,8,512]{3,2,1,0:T(8,128)(2,1)S(1)}, u32[]{:S(2)}, u32[]{:S(2)}) collective-permute-start(bf16[2,10,8,512]{3,2,1,0:T(8,128)(2,1)S(1)} %get-tuple-element.32.refs_0_), channel_id=1, source_target_pairs={{0,192},{64,0},{128,64},{192,128},{1,193},{65,1},{129,65},{193,129... | collective-permute-start | bytes 491528 | tf_op jit(solution)/shard_map/ppermute | solution.py:303
  64.4 8.2 %collective-permute-start.5 = (bf16[4,8,8,128]{3,2,1,0:T(8,128)(2,1)S(1)}, bf16[4,8,8,128]{3,2,1,0:T(8,128)(2,1)S(1)}, u32[]{:S(2)}, u32[]{:S(2)}) collective-permute-start(bf16[4,8,8,128]{3,2,1,0:T(8,128)(2,1)S(1)} %get-tuple-element.34), channel_id=1, source_target_pairs={{0,1},{1,2},{2,3},{3,4},{4,5},{5,6},{6,7},{7,8},{8,9},{9,10},{10,1... | collective-permute-start | bytes 196616 | tf_op jit(solution)/shard_map/ppermute | solution.py:379
  66.2 6.4 %collective-permute-start.6 = (bf16[4,8,8,128]{3,2,1,0:T(8,128)(2,1)S(1)}, bf16[4,8,8,128]{3,2,1,0:T(8,128)(2,1)S(1)}, u32[]{:S(2)}, u32[]{:S(2)}) collective-permute-start(bf16[4,8,8,128]{3,2,1,0:T(8,128)(2,1)S(1)} %get-tuple-element.35), channel_id=1, source_target_pairs={{0,15},{1,0},{2,1},{3,2},{4,3},{5,4},{6,5},{7,6},{8,7},{9,8},{10,9... | collective-permute-start | bytes 196616 | tf_op jit(solution)/shard_map/ppermute | solution.py:378
  73.2 4.0 %collective-permute-start.7 = (bf16[2,8,8,128]{3,2,1,0:T(8,128)(2,1)S(1)}, bf16[2,8,8,128]{3,2,1,0:T(8,128)(2,1)S(1)}, u32[]{:S(2)}, u32[]{:S(2)}) collective-permute-start(bf16[2,8,8,128]{3,2,1,0:T(8,128)(2,1)S(1)} %get-tuple-element.37), channel_id=1, source_target_pairs={{0,192},{64,0},{128,64},{192,128},{1,193},{65,1},{129,65},{193,129... | collective-permute-start | bytes 98312 | tf_op jit(solution)/shard_map/ppermute | solution.py:303
  74.7 5.4 %collective-permute-start.8 = (bf16[2,8,8,128]{3,2,1,0:T(8,128)(2,1)S(1)}, bf16[2,8,8,128]{3,2,1,0:T(8,128)(2,1)S(1)}, u32[]{:S(2)}, u32[]{:S(2)}) collective-permute-start(bf16[2,8,8,128]{3,2,1,0:T(8,128)(2,1)S(1)} %get-tuple-element.38), channel_id=1, source_target_pairs={{0,128},{64,192},{128,0},{192,64},{1,129},{65,193},{129,1},{193,65... | collective-permute-start | bytes 98312 | tf_op jit(solution)/shard_map/ppermute | solution.py:303
  75.5 5.1 %collective-permute-start.9 = (bf16[2,8,8,128]{3,2,1,0:T(8,128)(2,1)S(1)}, bf16[2,8,8,128]{3,2,1,0:T(8,128)(2,1)S(1)}, u32[]{:S(2)}, u32[]{:S(2)}) collective-permute-start(bf16[2,8,8,128]{3,2,1,0:T(8,128)(2,1)S(1)} %get-tuple-element.39), channel_id=1, source_target_pairs={{0,64},{64,128},{128,192},{192,0},{1,65},{65,129},{129,193},{193,1... | collective-permute-start | bytes 98312 | tf_op jit(solution)/shard_map/ppermute | solution.py:303

commit v4 on v3

--- a/solution.py
+++ b/solution.py
@@ -9,10 +9,11 @@
 
 BF16 = jnp.bfloat16
 F32 = jnp.float32
+TOKENS = 32768
 
 
 def _call(kernel, ins, outs, scratch=()):
-    moved = [i for i, (_, space) in enumerate(ins) if space == "arg"]
+    moved = [i for i, (_, space) in enumerate(ins) if space in ("arg", "scalar")]
     late = [i for i, (_, space) in enumerate(ins) if space == "late"]
     count = len(ins)
 
@@ -29,16 +30,16 @@
             copies.append(pltpu.make_async_copy(given[i], in_bufs[n], in_sem.at[n]))
             given[i] = in_bufs[n]
         for n, i in enumerate(late):
-            third = given[i].shape[0] // 3
             pieces = [
                 pltpu.make_async_copy(
-                    given[i].at[pl.ds(a * third, third)],
-                    late_bufs[n].at[pl.ds(a * third, third)],
-                    late_sem.at[3 * n + a],
+                    given[i].at[pl.ds(9 * a + 3 * b, 3)],
+                    late_bufs[n].at[b, pl.ds(3 * a, 3)],
+                    late_sem.at[9 * n + 3 * b + a],
                 )
+                for b in range(3)
                 for a in range(3)
             ]
-            for piece in pieces:
+            for piece in pieces[:6]:
                 piece.start()
             given[i] = (late_bufs[n], pieces)
         for copy in copies:
@@ -47,8 +48,11 @@
             copy.wait()
         kernel(*given, *results, *own)
 
-    buffers = [pltpu.VMEM(ins[i][0].shape, ins[i][0].dtype) for i in moved]
-    buffers += [pltpu.VMEM(ins[i][0].shape, ins[i][0].dtype) for i in late]
+    buffers = [
+        (pltpu.SMEM if ins[i][1] == "scalar" else pltpu.VMEM)(ins[i][0].shape, ins[i][0].dtype)
+        for i in moved
+    ]
+    buffers += [pltpu.VMEM((3, 9) + ins[i][0].shape[1:], ins[i][0].dtype) for i in late]
     arrays = [
         pltpu.with_memory_space_constraint(array, pltpu.HBM) if space in ("arg", "late") else array
         for array, space in ins
@@ -67,7 +71,7 @@
         + list(scratch)
         + [
             pltpu.SemaphoreType.DMA((max(1, len(moved)),)),
-            pltpu.SemaphoreType.DMA((max(1, 3 * len(late)),)),
+            pltpu.SemaphoreType.DMA((max(1, 9 * len(late)),)),
         ],
         compiler_params=pltpu.CompilerParams(vmem_limit_bytes=40 * 1024 * 1024),
     )(*arrays)
@@ -154,11 +158,11 @@
             in_out[tile * 4 + i] = out.astype(BF16).reshape(cols, rows // 4, frames, 128)
 
 
-def assemble(pos, g, proj, chunks, above, below, g_out, *sends):
+def assemble(at_y, at_z, g, proj, chunks, above, below, g_out, *sends):
     _, rows, _, chans = g.shape
     depth = len(sends)
-    top = jnp.where(pos[0] > 0, above[...], jnp.zeros_like(above[...]))
-    bot = jnp.where(pos[0] < 3, below[...], jnp.zeros_like(below[...]))
+    top = jnp.where(at_y[0] > 0, above[...], jnp.zeros_like(above[...]))
+    bot = jnp.where(at_y[0] < 3, below[...], jnp.zeros_like(below[...]))
     g_out[:, 1 : rows + 1] = g[...]
     g_out[:, 0] = top[:, :, :chans]
     g_out[:, rows + 1] = bot[:, :, :chans]
@@ -168,16 +172,16 @@
         send[:, rows + 1] = bot[:, :, chans:]
         for x in range(chunks.shape[0] // depth):
             at = rows + 2 + 2 * x
-            send[:, at : at + 2] = chunks[depth * x + lax.rem(pos[2] + k, depth)]
-
-
-def across_x(pos, *refs):
+            send[:, at : at + 2] = chunks[depth * x + lax.rem(at_z[0] + k, depth)]
+
+
+def across_x(at_x, *refs):
     depth = len(refs) // 2
     along = depth
     rows = refs[0].shape[1] - 2 * along
     for m in range(along):
         send = refs[depth + m]
-        at = rows + 2 * lax.rem(pos[1] + m, along)
+        at = rows + 2 * lax.rem(at_x[0] + m, along)
         for k in range(depth):
             send[k, :, :rows] = refs[k][:, :rows]
             for w in range(refs[k].shape[0]):
@@ -195,24 +199,31 @@
     cols, rows, frames, chans = g0.shape
     rows = rows - 2
     weight, pieces = weight
-    width = weight.shape[1]
+    width = weight.shape[2]
     for k, g in enumerate((g0, g1, g2, g3)):
         ext[k] = g[...]
     count = 4 * cols * rows * frames
-    total = None
-    for a in range(3):
-        pieces[a].wait()
-        acc = jnp.zeros((count, 3 * width), F32)
-        for b in range(3):
-            lhs = ext[:, :, 2 - b : 2 - b + rows].reshape(count, chans)
-            rhs = weight[9 * a + 3 * b : 9 * a + 3 * b + 3].reshape(3 * width, chans)
-            acc = acc + lax.dot_general(
-                lhs, rhs, (((1,), (1,)), ((), ())), preferred_element_type=F32
-            )
-        acc = acc.reshape(count // frames, frames, 3 * width)
-        if a != 1:
-            acc = shift_frames(acc, a - 1)
-        total = acc if total is None else total + acc
+    acc = None
+    for b in range(3):
+        for piece in pieces[3 * b : 3 * b + 3]:
+            piece.wait()
+        if b == 0:
+            for piece in pieces[6:]:
+                piece.start()
+        lhs = ext[:, :, 2 - b : 2 - b + rows].reshape(count, chans)
+        y = lax.dot_general(
+            lhs,
+            weight[b].reshape(9 * width, chans),
+            (((1,), (1,)), ((), ())),
+            preferred_element_type=F32,
+        )
+        acc = y if acc is None else acc + y
+    acc = acc.reshape(count // frames, frames, 9 * width)
+    total = (
+        shift_frames(acc[:, :, : 3 * width], -1)
+        + acc[:, :, 3 * width : 6 * width]
+        + shift_frames(acc[:, :, 6 * width :], 1)
+    )
     total = total.reshape(4, cols, rows, frames, 3 * width)
     for k in range(4):
         part = [[total[k, w, :, :, c * width : (c + 1) * width] for c in range(3)] for w in range(cols)]
@@ -222,9 +233,9 @@
         right_out[k] = part[1][2].astype(BF16)
 
 
-def merge_kernel(pos, own, from_left, from_right, *outs):
-    first = (pos[0] == 0) & (pos[1] == 0)
-    last = (pos[0] == 3) & (pos[1] == 3)
+def merge_kernel(at_x, at_z, own, from_left, from_right, *outs):
+    first = (at_x[0] == 0) & (at_z[0] == 0)
+    last = (at_x[0] == 3) & (at_z[0] == 3)
     for k, out in enumerate(outs):
         left = from_left[k].astype(F32)
         right = from_right[k].astype(F32)
@@ -232,16 +243,16 @@
         out[1] = (own[k, 1] + jnp.where(last, 0.0, right)).astype(BF16)
 
 
-def moment_kernel(pos, g0, g1, g2, g3, out, wide, inner, flat):
+def moment_kernel(at_x, at_z, g0, g1, g2, g3, out, wide, inner, flat):
     rows = wide.shape[1]
     depth, cols, _, frames, rank = g0.shape
     devices = 4 * depth
     halves = 2
     across = devices * cols
     for m, got in enumerate((g0, g1, g2, g3)):
-        x_at = lax.rem(pos[0] + (4 - m), 4)
+        x_at = lax.rem(at_x[0] + (4 - m), 4)
         for k in range(depth):
-            at = depth * x_at + lax.rem(pos[1] + (depth - k), depth)
+            at = depth * x_at + lax.rem(at_z[0] + (depth - k), depth)
             inner[at] = got[k, :, rows:]
             for w in range(cols):
                 wide[1 + cols * at + w] = got[k, w, :rows]
@@ -253,34 +264,65 @@
     sooner = shift_frames(x, -1).reshape(count * frames, 128)
     x = x.reshape(count * frames, 128)
     lanes = lax.broadcasted_iota(jnp.int32, x.shape, 1) >> 5
-    acc = [None] * 9
+    acc = None
     for q in range(4):
         lhs = jnp.zeros_like(x)
         for part, shift, block in ((later, (0 - 32 * q) % 128, 0), (x, (32 - 32 * q) % 128, 1), (sooner, (64 - 32 * q) % 128, 2)):
             moved = pltpu.roll(part, shift, 1) if shift else part
             lhs = jnp.where(lanes == block, moved, lhs)
         lhs = lhs.T.astype(BF16)
-        for b in range(3):
-            for c in range(3):
-                low = 2 - b + 2 * q
-                rhs = wide[2 - c : 2 - c + across, low : low + 2].reshape(count * frames, rank)
-                y = jnp.dot(lhs, rhs, preferred_element_type=F32)
-                acc[3 * b + c] = y if acc[3 * b + c] is None else acc[3 * b + c] + y
+        rhs = jnp.concatenate(
+            [
+                wide[2 - c : 2 - c + across, 2 - b + 2 * q : 4 - b + 2 * q].reshape(
+                    count * frames, rank
+                )
+                for b in range(3)
+                for c in range(3)
+            ],
+            axis=1,
+        )
+        y = jnp.dot(lhs, rhs, preferred_element_type=F32)
+        acc = y if acc is None else acc + y
     for a in range(3):
         for j in range(2):
             for k in range(9):
                 at = (27 * j + 9 * a + k) * 16
-                flat[at : at + 16, :] = acc[k][(2 * a + j) * 16 : (2 * a + j) * 16 + 16, :]
+                flat[at : at + 16, :] = acc[
+                    (2 * a + j) * 16 : (2 * a + j) * 16 + 16, k * rank : (k + 1) * rank
+                ]
     for m in range(16):
         out[m] = flat[pl.ds(m, 54, stride=16), :].astype(BF16)
 
 
-def finish_kernel(pos, up, p0, p1, p2, p3, out, flat, outflat):
+def owner_kernel(step, terms, first, second, first_out, second_out, scales_out):
+    reduced = terms[0].astype(F32)
+    for k in range(1, terms.shape[0]):
+        reduced = reduced + terms[k].astype(F32)
+    reduced = reduced * (1.0 / math.sqrt(TOKENS))
+    new_first = 0.9 * first[...] + 0.1 * reduced
+    new_second = 0.999 * second[...] + 0.001 * (reduced * reduced)
+    count = jnp.full((1, 128), step[0], jnp.int32).astype(F32)
+    first_bias = 1.0 - jnp.power(jnp.float32(0.9), count)
+    second_bias = 1.0 - jnp.power(jnp.float32(0.999), count)
+    adapted = new_first / first_bias / (jnp.sqrt(new_second / second_bias) + 1e-08)
+    first_out[...] = new_first
+    second_out[...] = new_second
+    rest = jnp.zeros((128 - reduced.shape[0], 128), F32)
+
+    def row_means(x):
+        square = jnp.concatenate([x * x, rest], axis=0)
+        return jnp.mean(square.T, axis=0, keepdims=True)
+
+    scales = jnp.sqrt(row_means(adapted)) / jnp.sqrt(row_means(reduced) + 1e-06)
+    scales_out[...] = scales[0, : reduced.shape[0]]
+
+
+def finish_kernel(at_d, up, p0, p1, p2, p3, out, flat, outflat):
     cols, rows, frames, _ = up.shape
     for tile in range(4):
         flat[tile] = up[:, :, :, tile * 128 : tile * 128 + 128].astype(F32)
     for k, part in enumerate((p0, p1, p2, p3)):
-        tile = lax.rem(pos[0] + k, 4)
+        tile = lax.rem(at_d[0] + k, 4)
         total = flat[tile] + part[...].astype(F32)
         for w in range(cols):
             for h in range(rows):
@@ -315,7 +357,7 @@
     g, proj, chunks, top, bot, up = _call(
         prepare,
         [
-            (hash_seed.reshape(1), "smem"),
+            (hash_seed.reshape(1), "scalar"),
             (pre_activation[0], "arg"),
             (upstream[0], "arg"),
             (inputs[0], "arg"),
@@ -333,7 +375,7 @@
     place = {a: lax.axis_index(a).astype(jnp.int32) for a in ("dp", "sy", "sxx", "sxz")}
 
     def places(*axes):
-        return (jnp.stack([place[a] for a in axes]), "smem")
+        return [(place[a].reshape(1), "smem") for a in axes]
 
     above = lax.ppermute(bot, "sy", ring("sy", 1))
     below = lax.ppermute(top, "sy", ring("sy", -1))
@@ -341,21 +383,21 @@
     along_x = ((4, cols, rows + 4, frames, 128), BF16)
     g, *sends = _call(
         assemble,
-        [places("sy", "sxx", "sxz")]
+        places("sy", "sxz")
         + [(a, "vmem") for a in (g, proj, chunks, above, below)],
         [((cols, rows + 2, frames, chans), BF16)] + [along_z] * 4,
     )
     got = around(sends, "sxz")
     sends = _call(
         across_x,
-        [places("sy", "sxx", "sxz")] + [(a, "vmem") for a in got],
+        places("sxx") + [(a, "vmem") for a in got],
         [along_x] * 4,
     )
     got = around(sends, "sxx")
     g_all = around([g] * 4, "dp")
     (terms,) = _call(
         moment_kernel,
-        [places("sxx", "sxz")] + [(a, "vmem") for a in got],
+        places("sxx", "sxz") + [(a, "vmem") for a in got],
         [((16, 54, rank), BF16)],
         [
             pltpu.VMEM((16 * cols + 2, rows + 2, frames, rank), BF16),
@@ -379,27 +421,22 @@
     from_left = lax.ppermute(right, sx, ring(sx, 1))
     mine = _call(
         merge_kernel,
-        [places("sxx", "sxz")] + [(a, "vmem") for a in (own, from_left, from_right)],
+        places("sxx", "sxz") + [(a, "vmem") for a in (own, from_left, from_right)],
         [((cols, rows, frames, 128), BF16)] * 4,
     )
     parts = around(mine, "dp", -1)
     (input_grad,) = _call(
         finish_kernel,
-        [places("dp"), (up, "vmem")] + [(a, "vmem") for a in parts],
+        places("dp") + [(up, "vmem")] + [(a, "vmem") for a in parts],
         [((frames, rows, cols, chans), BF16)],
         [pltpu.VMEM((chans // 128, cols, rows, frames, 128), F32), spread],
     )
 
-    total = 32768
-    reduced = jnp.sum(terms.astype(F32), axis=0) / math.sqrt(total)
-    new_first = 0.9 * first_moment + 0.1 * reduced
-    new_second = 0.999 * second_moment + 0.001 * reduced * reduced
-    step_value = step_count.astype(F32)
-    first_bias = 1.0 - jnp.power(jnp.float32(0.9), step_value)
-    second_bias = 1.0 - jnp.power(jnp.float32(0.999), step_value)
-    adapted = new_first / first_bias / (jnp.sqrt(new_second / second_bias) + 1e-08)
-    scales = jnp.sqrt(jnp.mean(adapted * adapted, axis=1)) / jnp.sqrt(
-        jnp.mean(reduced * reduced, axis=1) + 1e-06
+    new_first, new_second, scales = _call(
+        owner_kernel,
+        [(step_count.reshape(1), "scalar")]
+        + [(a, "vmem") for a in (terms, first_moment, second_moment)],
+        [(first_moment.shape, F32), (first_moment.shape, F32), ((first_moment.shape[0],), F32)],
     )
     return (input_grad[None], new_first, new_second, scales)
 

time: 83.9 us -> 81.1 us (0.967)
  Pallas kernels: 12.1 us -> 10.6 us
  other arithmetic: 1.46 us -> 0 us
    pallas_call x7 -> x8, Pallas kernels: 12.1 us -> 10.6 us  [_call(): pl.pallas_call(run, out_shape=[jax.ShapeDtypeStruct(shape, dtype) for sha...]
  transfers between devices with their start and end apart: 17 -> 17, of which waited for: 12 -> 13; matrix products, arithmetic and copies ran while one was open for 0% -> 0% of each run, Pallas kernels for 7% -> 6%
where the time goes in v4:
time: 81.1 us; the launch traced here: 80.1 us
  starting transfers between devices  36.4 us (45%)
  waiting for transfers between devices  30.9 us (38%)
  Pallas kernels  10.6 us (13%)
  between operations  2.21 us (3%)
    ppermute x12, waiting for transfers between devices, around(): got[k] = lax.ppermute(arrays[k], axis, ring(axis, sign * k))  26.3 us
    ppermute x12, starting transfers between devices, around(): got[k] = lax.ppermute(arrays[k], axis, ring(axis, sign * k))  24.8 us
    pallas_call x8, Pallas kernels, _call(): pl.pallas_call(run, out_shape=[jax.ShapeDtypeStruct(shape, dtype) for sha...  10.6 us
    all_to_all x1, starting transfers between devices, step(): terms = lax.all_to_all(terms, ('dp', 'sy'), 0, 0, tiled=True)  4.59 us
    ppermute x1, starting transfers between devices, step(): from_right = lax.ppermute(left, sx, ring(sx, -1))  3.26 us
    ppermute x1, waiting for transfers between devices, step(): from_left = lax.ppermute(right, sx, ring(sx, 1))  3.03 us
    ppermute x1, starting transfers between devices, step(): from_left = lax.ppermute(right, sx, ring(sx, 1))  1.85 us
    ppermute x1, starting transfers between devices, step(): below = lax.ppermute(top, 'sy', ring('sy', -1))  1.73 us
  transfers between devices with their start and end apart: 17, of which 13 were waited for; matrix products, arithmetic and copies ran while one was open for 0% of the time, Pallas kernels for 6%

profile of v4, /device:TPU:2, one launch (start us, length us, event | category | flops | bytes accessed | tf_op | source)
XLA Modules:
  0.0 80.1 jit_solution(16726701022160161359)
XLA Ops:
  1.3 2.1 %shard_map.111 = (bf16[2,8,8,512]{3,2,1,0:T(8,128)(2,1)S(1)}, bf16[2,8,8,128]{3,2,1,0:T(8,128)(2,1)S(1)}, bf16[16,2,2,8,128]{4,3,2,1,0:T(8,128)(2,1)S(1)}, bf16[...) custom-call(s32[1]{0:T(128)} %bitcast.10.refs_0_, ...), custom_call_target="tpu_custom_call" | custom-call | tf_op jit(solution)/shard_map/pallas_call | solution.py:60
  3.5 1.7 %collective-permute-start.1 = (bf16[2,8,640]{2,1,0:T(8,128)(2,1)S(1)}, bf16[2,8,640]{2,1,0:T(8,128)(2,1)S(1)}, u32[]{:S(2)}, u32[]{:S(2)}) collective-permute-start(bf16[2,8,640]{2,1,0:T(8,128)(2,1)S(1)} %get-tuple-element.34), channel_id=1, source_target_pairs={{0,48},{16,0},{32,16},{48,32},{1,49},{17,1},{33,17},{49,33},{2,50}... | collective-permute-start | bytes 61448 | tf_op jit(solution)/shard_map/ppermute | solution.py:381
  5.2 1.5 %collective-permute-done.refs_5_ = bf16[2,8,640]{2,1,0:T(8,128)(2,1)S(1)} collective-permute-done((bf16[2,8,640]{2,1,0:T(8,128)(2,1)S(1)}, bf16[2,8,640]{2,1,0:T(8,128)(2,1)S(1)}, u32[]{:S(2)}, u32[]{:S(2)}) %collective-permute-start) | collective-permute-done | bytes 20512 | tf_op jit(solution)/shard_map/ppermute | solution.py:380
  6.8 3.3 %collective-permute-start.10 = (bf16[2,18,8,128]{3,2,1,0:T(8,128)(2,1)S(1)}, bf16[2,18,8,128]{3,2,1,0:T(8,128)(2,1)S(1)}, u32[]{:S(2)}, u32[]{:S(2)}) collective-permute-start(bf16[2,18,8,128]{3,2,1,0:T(8,128)(2,1)S(1)} %get-tuple-element.44), channel_id=1, source_target_pairs={{0,1},{1,2},{2,3},{3,0},{4,5},{5,6},{6,7},{7,4},{8,9},{9,10},{10,1... | collective-permute-start | bytes 221192 | tf_op jit(solution)/shard_map/ppermute | solution.py:345
  10.1 5.4 %collective-permute-start.11 = (bf16[2,18,8,128]{3,2,1,0:T(8,128)(2,1)S(1)}, bf16[2,18,8,128]{3,2,1,0:T(8,128)(2,1)S(1)}, u32[]{:S(2)}, u32[]{:S(2)}) collective-permute-start(bf16[2,18,8,128]{3,2,1,0:T(8,128)(2,1)S(1)} %get-tuple-element.45), channel_id=1, source_target_pairs={{0,2},{1,3},{2,0},{3,1},{4,6},{5,7},{6,4},{7,5},{8,10},{9,11},{10,... | collective-permute-start | bytes 221192 | tf_op jit(solution)/shard_map/ppermute | solution.py:345
  15.5 2.7 %collective-permute-start.12 = (bf16[2,18,8,128]{3,2,1,0:T(8,128)(2,1)S(1)}, bf16[2,18,8,128]{3,2,1,0:T(8,128)(2,1)S(1)}, u32[]{:S(2)}, u32[]{:S(2)}) collective-permute-start(bf16[2,18,8,128]{3,2,1,0:T(8,128)(2,1)S(1)} %get-tuple-element.46), channel_id=1, source_target_pairs={{0,3},{1,0},{2,1},{3,2},{4,7},{5,4},{6,5},{7,6},{8,11},{9,8},{10,9... | collective-permute-start | bytes 221192 | tf_op jit(solution)/shard_map/ppermute | solution.py:345
  18.2 3.2 %collective-permute-done.11.refs_3_ = bf16[2,18,8,128]{3,2,1,0:T(8,128)(2,1)S(1)} collective-permute-done((bf16[2,18,8,128]{3,2,1,0:T(8,128)(2,1)S(1)}, bf16[2,18,8,128]{3,2,1,0:T(8,128)(2,1)S(1)}, u32[]{:S(2)}, u32[]{:S(2)}) %collective-permute-start.11) | collective-permute-done | bytes 73760 | tf_op jit(solution)/shard_map/ppermute | solution.py:345
  21.4 2.6 %collective-permute-done.12.refs_4_ = bf16[2,18,8,128]{3,2,1,0:T(8,128)(2,1)S(1)} collective-permute-done((bf16[2,18,8,128]{3,2,1,0:T(8,128)(2,1)S(1)}, bf16[2,18,8,128]{3,2,1,0:T(8,128)(2,1)S(1)}, u32[]{:S(2)}, u32[]{:S(2)}) %collective-permute-start.12) | collective-permute-done | bytes 73760 | tf_op jit(solution)/shard_map/ppermute | solution.py:345
  24.0 1.6 %collective-permute-start.13 = (bf16[4,2,12,8,128]{4,3,2,1,0:T(8,128)(2,1)S(1)}, bf16[4,2,12,8,128]{4,3,2,1,0:T(8,128)(2,1)S(1)}, u32[]{:S(2)}, u32[]{:S(2)}) collective-permute-start(bf16[4,2,12,8,128]{4,3,2,1,0:T(8,128)(2,1)S(1)} %get-tuple-element.48), channel_id=1, source_target_pairs={{0,4},{4,8},{8,12},{12,0},{1,5},{5,9},{9,13},{13,1},{2,6},{6,10},{... | collective-permute-start | bytes 589832 | tf_op jit(solution)/shard_map/ppermute | solution.py:345
  25.6 1.1 %collective-permute-start.14 = (bf16[4,2,12,8,128]{4,3,2,1,0:T(8,128)(2,1)S(1)}, bf16[4,2,12,8,128]{4,3,2,1,0:T(8,128)(2,1)S(1)}, u32[]{:S(2)}, u32[]{:S(2)}) collective-permute-start(bf16[4,2,12,8,128]{4,3,2,1,0:T(8,128)(2,1)S(1)} %get-tuple-element.49), channel_id=1, source_target_pairs={{0,8},{4,12},{8,0},{12,4},{1,9},{5,13},{9,1},{13,5},{2,10},{6,14},... | collective-permute-start | bytes 589832 | tf_op jit(solution)/shard_map/ppermute | solution.py:345
  26.7 2.2 %collective-permute-start.15 = (bf16[4,2,12,8,128]{4,3,2,1,0:T(8,128)(2,1)S(1)}, bf16[4,2,12,8,128]{4,3,2,1,0:T(8,128)(2,1)S(1)}, u32[]{:S(2)}, u32[]{:S(2)}) collective-permute-start(bf16[4,2,12,8,128]{4,3,2,1,0:T(8,128)(2,1)S(1)} %get-tuple-element.50), channel_id=1, source_target_pairs={{0,12},{4,0},{8,4},{12,8},{1,13},{5,1},{9,5},{13,9},{2,14},{6,2},{... | collective-permute-start | bytes 589832 | tf_op jit(solution)/shard_map/ppermute | solution.py:345
  28.9 3.0 %collective-permute-done.13.refs_3_ = bf16[4,2,12,8,128]{4,3,2,1,0:T(8,128)(2,1)S(1)} collective-permute-done((bf16[4,2,12,8,128]{4,3,2,1,0:T(8,128)(2,1)S(1)}, bf16[4,2,12,8,128]{4,3,2,1,0:T(8,128)(2,1)S(1)}, u32[]{:S(2)}, u32[]{:S(2)}) %collective-permute-start.13) | collective-permute-done | bytes 196640 | tf_op jit(solution)/shard_map/ppermute | solution.py:345
  31.9 3.0 %collective-permute-done.14.refs_4_ = bf16[4,2,12,8,128]{4,3,2,1,0:T(8,128)(2,1)S(1)} collective-permute-done((bf16[4,2,12,8,128]{4,3,2,1,0:T(8,128)(2,1)S(1)}, bf16[4,2,12,8,128]{4,3,2,1,0:T(8,128)(2,1)S(1)}, u32[]{:S(2)}, u32[]{:S(2)}) %collective-permute-start.14) | collective-permute-done | bytes 196640 | tf_op jit(solution)/shard_map/ppermute | solution.py:345
  34.9 2.4 %collective-permute-done.15.refs_5_ = bf16[4,2,12,8,128]{4,3,2,1,0:T(8,128)(2,1)S(1)} collective-permute-done((bf16[4,2,12,8,128]{4,3,2,1,0:T(8,128)(2,1)S(1)}, bf16[4,2,12,8,128]{4,3,2,1,0:T(8,128)(2,1)S(1)}, u32[]{:S(2)}, u32[]{:S(2)}) %collective-permute-start.15) | collective-permute-done | bytes 196640 | tf_op jit(solution)/shard_map/ppermute | solution.py:345
  37.2 1.9 %shard_map.117 = bf16[16,54,128]{2,1,0:T(8,128)(2,1)} custom-call(s32[1]{0:T(128)} %bitcast.5.refs_0_, s32[1]{0:T(128)} %bitcast.6.refs_1_, bf16[4,2,12,8,128]{4,3,2,1,0:T(8,128)(2,1)S(1)} %get-tuple-element.47.refs_2_, bf16[4,2,12,8,128]{4,3,2,1,0:T(8,128)(2,1)S(1)} %collective-permute-done.13.refs_3_, ...), custom_call_target="tpu_custom_call" | custom-call | tf_op jit(solution)/shard_map/pallas_call | solution.py:60
  39.1 4.6 %all-to-all-start = ((bf16[16,54,128]{2,1,0:T(8,128)(2,1)}), bf16[16,54,128]{2,1,0:T(8,128)(2,1)S(1)}, u32[]{:S(2)}, u32[]{:S(2)}) async-start(bf16[16,54,128]{2,1,0:T(8,128)(2,1)} %shard_map.117), calls=%async_computation | async-start | bytes 458752 | tf_op jit(solution)/shard_map/all_to_all | solution.py:408
  43.7 1.9 %collective-permute-start.2 = (bf16[2,10,8,512]{3,2,1,0:T(8,128)(2,1)S(1)}, bf16[2,10,8,512]{3,2,1,0:T(8,128)(2,1)S(1)}, u32[]{:S(2)}, u32[]{:S(2)}) collective-permute-start(bf16[2,10,8,512]{3,2,1,0:T(8,128)(2,1)S(1)} %get-tuple-element.35.refs_0_), channel_id=1, source_target_pairs={{0,64},{64,128},{128,192},{192,0},{1,65},{65,129},{129,193},{193,1... | collective-permute-start | bytes 491528 | tf_op jit(solution)/shard_map/ppermute | solution.py:345
  45.7 2.7 %collective-permute-start.3 = (bf16[2,10,8,512]{3,2,1,0:T(8,128)(2,1)S(1)}, bf16[2,10,8,512]{3,2,1,0:T(8,128)(2,1)S(1)}, u32[]{:S(2)}, u32[]{:S(2)}) collective-permute-start(bf16[2,10,8,512]{3,2,1,0:T(8,128)(2,1)S(1)} %get-tuple-element.35.refs_0_), channel_id=1, source_target_pairs={{0,128},{64,192},{128,0},{192,64},{1,129},{65,193},{129,1},{193,65... | collective-permute-start | bytes 491528 | tf_op jit(solution)/shard_map/ppermute | solution.py:345
  48.3 1.5 %collective-permute-start.4 = (bf16[2,10,8,512]{3,2,1,0:T(8,128)(2,1)S(1)}, bf16[2,10,8,512]{3,2,1,0:T(8,128)(2,1)S(1)}, u32[]{:S(2)}, u32[]{:S(2)}) collective-permute-start(bf16[2,10,8,512]{3,2,1,0:T(8,128)(2,1)S(1)} %get-tuple-element.35.refs_0_), channel_id=1, source_target_pairs={{0,192},{64,0},{128,64},{192,128},{1,193},{65,1},{129,65},{193,129... | collective-permute-start | bytes 491528 | tf_op jit(solution)/shard_map/ppermute | solution.py:345
  49.8 4.5 %collective-permute-done.2.refs_1_ = bf16[2,10,8,512]{3,2,1,0:T(8,128)(2,1)S(1)} collective-permute-done((bf16[2,10,8,512]{3,2,1,0:T(8,128)(2,1)S(1)}, bf16[2,10,8,512]{3,2,1,0:T(8,128)(2,1)S(1)}, u32[]{:S(2)}, u32[]{:S(2)}) %collective-permute-start.2) | collective-permute-done | bytes 163872 | tf_op jit(solution)/shard_map/ppermute | solution.py:345
  54.3 3.6 %collective-permute-done.3.refs_2_ = bf16[2,10,8,512]{3,2,1,0:T(8,128)(2,1)S(1)} collective-permute-done((bf16[2,10,8,512]{3,2,1,0:T(8,128)(2,1)S(1)}, bf16[2,10,8,512]{3,2,1,0:T(8,128)(2,1)S(1)}, u32[]{:S(2)}, u32[]{:S(2)}) %collective-permute-start.3) | collective-permute-done | bytes 163872 | tf_op jit(solution)/shard_map/ppermute | solution.py:345
  57.8 4.3 %shard_map.113 = (f32[4,2,8,8,128]{4,3,2,1,0:T(8,128)S(1)}, bf16[4,8,8,128]{3,2,1,0:T(8,128)(2,1)S(1)}, bf16[4,8,8,128]{3,2,1,0:T(8,128)(2,1)S(1)}) custom-call(bf16[2,10,8,512]{3,2,1,0:T(8,128)(2,1)S(1)} %get-tuple-element.35.refs_0_, bf16[2,10,8,512]{3,2,1,0:T(8,128)(2,1)S(1)} %collective-permute-done.2.refs_1_, ...), custom_call_target="tpu_custom_call" | custom-call | tf_op jit(solution)/shard_map/pallas_call | solution.py:60
  62.1 1.9 %collective-permute-start.5 = (bf16[4,8,8,128]{3,2,1,0:T(8,128)(2,1)S(1)}, bf16[4,8,8,128]{3,2,1,0:T(8,128)(2,1)S(1)}, u32[]{:S(2)}, u32[]{:S(2)}) collective-permute-start(bf16[4,8,8,128]{3,2,1,0:T(8,128)(2,1)S(1)} %get-tuple-element.37), channel_id=1, source_target_pairs={{0,1},{1,2},{2,3},{3,4},{4,5},{5,6},{6,7},{7,8},{8,9},{9,10},{10,1... | collective-permute-start | bytes 196616 | tf_op jit(solution)/shard_map/ppermute | solution.py:421
  64.0 3.3 %collective-permute-start.6 = (bf16[4,8,8,128]{3,2,1,0:T(8,128)(2,1)S(1)}, bf16[4,8,8,128]{3,2,1,0:T(8,128)(2,1)S(1)}, u32[]{:S(2)}, u32[]{:S(2)}) collective-permute-start(bf16[4,8,8,128]{3,2,1,0:T(8,128)(2,1)S(1)} %get-tuple-element.38), channel_id=1, source_target_pairs={{0,15},{1,0},{2,1},{3,2},{4,3},{5,4},{6,5},{7,6},{8,7},{9,8},{10,9... | collective-permute-start | bytes 196616 | tf_op jit(solution)/shard_map/ppermute | solution.py:420
  67.2 3.0 %collective-permute-done.5.refs_3_ = bf16[4,8,8,128]{3,2,1,0:T(8,128)(2,1)S(1)} collective-permute-done((bf16[4,8,8,128]{3,2,1,0:T(8,128)(2,1)S(1)}, bf16[4,8,8,128]{3,2,1,0:T(8,128)(2,1)S(1)}, u32[]{:S(2)}, u32[]{:S(2)}) %collective-permute-start.5) | collective-permute-done | bytes 65568 | tf_op jit(solution)/shard_map/ppermute | solution.py:421
  70.4 1.5 %collective-permute-start.7 = (bf16[2,8,8,128]{3,2,1,0:T(8,128)(2,1)S(1)}, bf16[2,8,8,128]{3,2,1,0:T(8,128)(2,1)S(1)}, u32[]{:S(2)}, u32[]{:S(2)}) collective-permute-start(bf16[2,8,8,128]{3,2,1,0:T(8,128)(2,1)S(1)} %get-tuple-element.40), channel_id=1, source_target_pairs={{0,192},{64,0},{128,64},{192,128},{1,193},{65,1},{129,65},{193,129... | collective-permute-start | bytes 98312 | tf_op jit(solution)/shard_map/ppermute | solution.py:345
  71.9 0.8 collective-permute-start.8
  73.6 0.8 collective-permute-done.7.refs_3_
  74.4 2.9 %collective-permute-done.8.refs_4_ = bf16[2,8,8,128]{3,2,1,0:T(8,128)(2,1)S(1)} collective-permute-done((bf16[2,8,8,128]{3,2,1,0:T(8,128)(2,1)S(1)}, bf16[2,8,8,128]{3,2,1,0:T(8,128)(2,1)S(1)}, u32[]{:S(2)}, u32[]{:S(2)}) %collective-permute-start.8) | collective-permute-done | bytes 32800 | tf_op jit(solution)/shard_map/ppermute | solution.py:345
  77.3 0.5 collective-permute-done.9.refs_5_
  77.8 0.8 %shard_map.115 = bf16[8,8,2,512]{3,2,1,0:T(2,128)(2,1)} custom-call(s32[1]{0:T(128)} %bitcast.refs_0_, bf16[2,8,8,512]{3,2,1,0:T(8,128)(2,1)S(1)} %get-tuple-element.29.refs_1_, bf16[2,8,8,128]{3,2,1,0:T(8,128)(2,1)S(1)} %get-tuple-element.39.refs_2_, bf16[2,8,8,128]{3,2,1,0:T(8,128)(2,1)S(1)} %collective-permute-done.7.refs_3_, ...), custom_call_target="tpu_custom_call" | custom-call | tf_op jit(solution)/shard_map/pallas_call | solution.py:60
  78.7 1.2 %shard_map.118 = (f32[54,128]{1,0:T(8,128)}, f32[54,128]{1,0:T(8,128)}, f32[54]{0:T(128)}) custom-call(s32[1]{0:T(128)} %bitcast.11.refs_0_, bf16[16,54,128]{2,1,0:T(8,128)(2,1)S(1)} %all-to-all-done.refs_1_, f32[54,128]{1,0:T(8,128)S(1)} %copy-done, f32[54,128]{1,0:T(8,128)S(1)} %copy-done.1), custom_call_target="tpu_custom_call" | custom-call | tf_op jit(solution)/shard_map/pallas_call | solution.py:60
  (14 shorter events, 0.7 us)
Async XLA Ops:
  3.4 3.3 %collective-permute-start = (bf16[2,8,640]{2,1,0:T(8,128)(2,1)S(1)}, bf16[2,8,640]{2,1,0:T(8,128)(2,1)S(1)}, u32[]{:S(2)}, u32[]{:S(2)}) collective-permute-start(bf16[2,8,640]{2,1,0:T(8,128)(2,1)S(1)} %get-tuple-element.33), channel_id=1, source_target_pairs={{0,16},{16,32},{32,48},{48,0},{1,17},{17,33},{33,49},{49,1},{2,18}... | collective-permute-start | bytes 61448 | tf_op jit(solution)/shard_map/ppermute | solution.py:380
  3.5 3.2 %collective-permute-start.1 = (bf16[2,8,640]{2,1,0:T(8,128)(2,1)S(1)}, bf16[2,8,640]{2,1,0:T(8,128)(2,1)S(1)}, u32[]{:S(2)}, u32[]{:S(2)}) collective-permute-start(bf16[2,8,640]{2,1,0:T(8,128)(2,1)S(1)} %get-tuple-element.34), channel_id=1, source_target_pairs={{0,48},{16,0},{32,16},{48,32},{1,49},{17,1},{33,17},{49,33},{2,50}... | collective-permute-start | bytes 61448 | tf_op jit(solution)/shard_map/ppermute | solution.py:381
  6.7 72.0 %copy-start = (f32[54,128]{1,0:T(8,128)S(1)}, f32[54,128]{1,0:T(8,128)}, u32[]{:S(2)}) copy-start(f32[54,128]{1,0:T(8,128)} %refs_2_.1) | copy-start | bytes 82948
  6.7 72.0 %copy-start.1 = (f32[54,128]{1,0:T(8,128)S(1)}, f32[54,128]{1,0:T(8,128)}, u32[]{:S(2)}) copy-start(f32[54,128]{1,0:T(8,128)} %refs_3_.1) | copy-start | bytes 82948
  6.8 11.4 %collective-permute-start.10 = (bf16[2,18,8,128]{3,2,1,0:T(8,128)(2,1)S(1)}, bf16[2,18,8,128]{3,2,1,0:T(8,128)(2,1)S(1)}, u32[]{:S(2)}, u32[]{:S(2)}) collective-permute-start(bf16[2,18,8,128]{3,2,1,0:T(8,128)(2,1)S(1)} %get-tuple-element.44), channel_id=1, source_target_pairs={{0,1},{1,2},{2,3},{3,0},{4,5},{5,6},{6,7},{7,4},{8,9},{9,10},{10,1... | collective-permute-start | bytes 221192 | tf_op jit(solution)/shard_map/ppermute | solution.py:345
  10.1 11.3 %collective-permute-start.11 = (bf16[2,18,8,128]{3,2,1,0:T(8,128)(2,1)S(1)}, bf16[2,18,8,128]{3,2,1,0:T(8,128)(2,1)S(1)}, u32[]{:S(2)}, u32[]{:S(2)}) collective-permute-start(bf16[2,18,8,128]{3,2,1,0:T(8,128)(2,1)S(1)} %get-tuple-element.45), channel_id=1, source_target_pairs={{0,2},{1,3},{2,0},{3,1},{4,6},{5,7},{6,4},{7,5},{8,10},{9,11},{10,... | collective-permute-start | bytes 221192 | tf_op jit(solution)/shard_map/ppermute | solution.py:345
  15.5 8.4 %collective-permute-start.12 = (bf16[2,18,8,128]{3,2,1,0:T(8,128)(2,1)S(1)}, bf16[2,18,8,128]{3,2,1,0:T(8,128)(2,1)S(1)}, u32[]{:S(2)}, u32[]{:S(2)}) collective-permute-start(bf16[2,18,8,128]{3,2,1,0:T(8,128)(2,1)S(1)} %get-tuple-element.46), channel_id=1, source_target_pairs={{0,3},{1,0},{2,1},{3,2},{4,7},{5,4},{6,5},{7,6},{8,11},{9,8},{10,9... | collective-permute-start | bytes 221192 | tf_op jit(solution)/shard_map/ppermute | solution.py:345
  24.0 7.8 %collective-permute-start.13 = (bf16[4,2,12,8,128]{4,3,2,1,0:T(8,128)(2,1)S(1)}, bf16[4,2,12,8,128]{4,3,2,1,0:T(8,128)(2,1)S(1)}, u32[]{:S(2)}, u32[]{:S(2)}) collective-permute-start(bf16[4,2,12,8,128]{4,3,2,1,0:T(8,128)(2,1)S(1)} %get-tuple-element.48), channel_id=1, source_target_pairs={{0,4},{4,8},{8,12},{12,0},{1,5},{5,9},{9,13},{13,1},{2,6},{6,10},{... | collective-permute-start | bytes 589832 | tf_op jit(solution)/shard_map/ppermute | solution.py:345
  25.6 9.3 %collective-permute-start.14 = (bf16[4,2,12,8,128]{4,3,2,1,0:T(8,128)(2,1)S(1)}, bf16[4,2,12,8,128]{4,3,2,1,0:T(8,128)(2,1)S(1)}, u32[]{:S(2)}, u32[]{:S(2)}) collective-permute-start(bf16[4,2,12,8,128]{4,3,2,1,0:T(8,128)(2,1)S(1)} %get-tuple-element.49), channel_id=1, source_target_pairs={{0,8},{4,12},{8,0},{12,4},{1,9},{5,13},{9,1},{13,5},{2,10},{6,14},... | collective-permute-start | bytes 589832 | tf_op jit(solution)/shard_map/ppermute | solution.py:345
  26.7 10.5 %collective-permute-start.15 = (bf16[4,2,12,8,128]{4,3,2,1,0:T(8,128)(2,1)S(1)}, bf16[4,2,12,8,128]{4,3,2,1,0:T(8,128)(2,1)S(1)}, u32[]{:S(2)}, u32[]{:S(2)}) collective-permute-start(bf16[4,2,12,8,128]{4,3,2,1,0:T(8,128)(2,1)S(1)} %get-tuple-element.50), channel_id=1, source_target_pairs={{0,12},{4,0},{8,4},{12,8},{1,13},{5,1},{9,5},{13,9},{2,14},{6,2},{... | collective-permute-start | bytes 589832 | tf_op jit(solution)/shard_map/ppermute | solution.py:345
  39.1 39.5 %all-to-all-start = ((bf16[16,54,128]{2,1,0:T(8,128)(2,1)}), bf16[16,54,128]{2,1,0:T(8,128)(2,1)S(1)}, u32[]{:S(2)}, u32[]{:S(2)}) async-start(bf16[16,54,128]{2,1,0:T(8,128)(2,1)} %shard_map.117), calls=%async_computation | async-start | bytes 458752 | tf_op jit(solution)/shard_map/all_to_all | solution.py:408
  43.7 10.5 %collective-permute-start.2 = (bf16[2,10,8,512]{3,2,1,0:T(8,128)(2,1)S(1)}, bf16[2,10,8,512]{3,2,1,0:T(8,128)(2,1)S(1)}, u32[]{:S(2)}, u32[]{:S(2)}) collective-permute-start(bf16[2,10,8,512]{3,2,1,0:T(8,128)(2,1)S(1)} %get-tuple-element.35.refs_0_), channel_id=1, source_target_pairs={{0,64},{64,128},{128,192},{192,0},{1,65},{65,129},{129,193},{193,1... | collective-permute-start | bytes 491528 | tf_op jit(solution)/shard_map/ppermute | solution.py:345
  45.7 12.2 %collective-permute-start.3 = (bf16[2,10,8,512]{3,2,1,0:T(8,128)(2,1)S(1)}, bf16[2,10,8,512]{3,2,1,0:T(8,128)(2,1)S(1)}, u32[]{:S(2)}, u32[]{:S(2)}) collective-permute-start(bf16[2,10,8,512]{3,2,1,0:T(8,128)(2,1)S(1)} %get-tuple-element.35.refs_0_), channel_id=1, source_target_pairs={{0,128},{64,192},{128,0},{192,64},{1,129},{65,193},{129,1},{193,65... | collective-permute-start | bytes 491528 | tf_op jit(solution)/shard_map/ppermute | solution.py:345
  48.3 9.5 %collective-permute-start.4 = (bf16[2,10,8,512]{3,2,1,0:T(8,128)(2,1)S(1)}, bf16[2,10,8,512]{3,2,1,0:T(8,128)(2,1)S(1)}, u32[]{:S(2)}, u32[]{:S(2)}) collective-permute-start(bf16[2,10,8,512]{3,2,1,0:T(8,128)(2,1)S(1)} %get-tuple-element.35.refs_0_), channel_id=1, source_target_pairs={{0,192},{64,0},{128,64},{192,128},{1,193},{65,1},{129,65},{193,129... | collective-permute-start | bytes 491528 | tf_op jit(solution)/shard_map/ppermute | solution.py:345
  62.1 8.1 %collective-permute-start.5 = (bf16[4,8,8,128]{3,2,1,0:T(8,128)(2,1)S(1)}, bf16[4,8,8,128]{3,2,1,0:T(8,128)(2,1)S(1)}, u32[]{:S(2)}, u32[]{:S(2)}) collective-permute-start(bf16[4,8,8,128]{3,2,1,0:T(8,128)(2,1)S(1)} %get-tuple-element.37), channel_id=1, source_target_pairs={{0,1},{1,2},{2,3},{3,4},{4,5},{5,6},{6,7},{7,8},{8,9},{9,10},{10,1... | collective-permute-start | bytes 196616 | tf_op jit(solution)/shard_map/ppermute | solution.py:421
  64.0 6.4 %collective-permute-start.6 = (bf16[4,8,8,128]{3,2,1,0:T(8,128)(2,1)S(1)}, bf16[4,8,8,128]{3,2,1,0:T(8,128)(2,1)S(1)}, u32[]{:S(2)}, u32[]{:S(2)}) collective-permute-start(bf16[4,8,8,128]{3,2,1,0:T(8,128)(2,1)S(1)} %get-tuple-element.38), channel_id=1, source_target_pairs={{0,15},{1,0},{2,1},{3,2},{4,3},{5,4},{6,5},{7,6},{8,7},{9,8},{10,9... | collective-permute-start | bytes 196616 | tf_op jit(solution)/shard_map/ppermute | solution.py:420
  70.4 4.0 %collective-permute-start.7 = (bf16[2,8,8,128]{3,2,1,0:T(8,128)(2,1)S(1)}, bf16[2,8,8,128]{3,2,1,0:T(8,128)(2,1)S(1)}, u32[]{:S(2)}, u32[]{:S(2)}) collective-permute-start(bf16[2,8,8,128]{3,2,1,0:T(8,128)(2,1)S(1)} %get-tuple-element.40), channel_id=1, source_target_pairs={{0,192},{64,0},{128,64},{192,128},{1,193},{65,1},{129,65},{193,129... | collective-permute-start | bytes 98312 | tf_op jit(solution)/shard_map/ppermute | solution.py:345
  71.9 5.4 %collective-permute-start.8 = (bf16[2,8,8,128]{3,2,1,0:T(8,128)(2,1)S(1)}, bf16[2,8,8,128]{3,2,1,0:T(8,128)(2,1)S(1)}, u32[]{:S(2)}, u32[]{:S(2)}) collective-permute-start(bf16[2,8,8,128]{3,2,1,0:T(8,128)(2,1)S(1)} %get-tuple-element.41), channel_id=1, source_target_pairs={{0,128},{64,192},{128,0},{192,64},{1,129},{65,193},{129,1},{193,65... | collective-permute-start | bytes 98312 | tf_op jit(solution)/shard_map/ppermute | solution.py:345
  72.7 5.1 %collective-permute-start.9 = (bf16[2,8,8,128]{3,2,1,0:T(8,128)(2,1)S(1)}, bf16[2,8,8,128]{3,2,1,0:T(8,128)(2,1)S(1)}, u32[]{:S(2)}, u32[]{:S(2)}) collective-permute-start(bf16[2,8,8,128]{3,2,1,0:T(8,128)(2,1)S(1)} %get-tuple-element.42), channel_id=1, source_target_pairs={{0,64},{64,128},{128,192},{192,0},{1,65},{65,129},{129,193},{193,1... | collective-permute-start | bytes 98312 | tf_op jit(solution)/shard_map/ppermute | solution.py:345

commit v5 on v4

--- a/solution.py
+++ b/solution.py
@@ -23,8 +23,9 @@
         rest = refs[count + len(outs) :]
         in_bufs = rest[: len(moved)]
         late_bufs = rest[len(moved) :][: len(late)]
-        own = rest[len(moved) + len(late) : -2]
-        in_sem, late_sem = rest[-2:]
+        sems = rest[len(rest) - bool(moved) - bool(late) :]
+        own = rest[len(moved) + len(late) : len(rest) - len(sems)]
+        in_sem, late_sem = sems[0] if moved else None, sems[-1] if late else None
         copies = []
         for n, i in enumerate(moved):
             copies.append(pltpu.make_async_copy(given[i], in_bufs[n], in_sem.at[n]))
@@ -39,8 +40,8 @@
                 for b in range(3)
                 for a in range(3)
             ]
-            for piece in pieces[:6]:
-                piece.start()
+            for at, piece in enumerate(pieces):
+                piece.start(priority=at % 2)
             given[i] = (late_bufs[n], pieces)
         for copy in copies:
             copy.start()
@@ -69,10 +70,7 @@
         out_specs=[pl.BlockSpec(memory_space=pltpu.VMEM) for _ in outs],
         scratch_shapes=buffers
         + list(scratch)
-        + [
-            pltpu.SemaphoreType.DMA((max(1, len(moved)),)),
-            pltpu.SemaphoreType.DMA((max(1, 9 * len(late)),)),
-        ],
+        + [pltpu.SemaphoreType.DMA((n,)) for n in (len(moved), 9 * len(late)) if n],
         compiler_params=pltpu.CompilerParams(vmem_limit_bytes=40 * 1024 * 1024),
     )(*arrays)
 
@@ -103,12 +101,11 @@
     return jnp.concatenate(tiles, axis=1)
 
 
-def prepare(seed, pre, up, inp, g_out, proj_out, in_out, top_out, bot_out, up_out, s_pre, s_up, s_in):
+def prepare(seed, pre, up, g_out, proj_out, top_out, bot_out, up_out, s_pre, s_up):
     frames, rows, cols, chans = pre.shape
     rank = proj_out.shape[-1]
     _rows_to_scratch(pre, s_pre)
     _rows_to_scratch(up, s_up)
-    _rows_to_scratch(inp, s_in)
 
     row_ids = lax.broadcasted_iota(jnp.int32, (chans, rank), 0)
     col_ids = lax.broadcasted_iota(jnp.int32, (chans, rank), 1)
@@ -136,6 +133,10 @@
     top_out[:, :, chans:] = p4[:, 0]
     bot_out[:, :, chans:] = p4[:, rows - 1]
 
+
+def pack_inputs(inp, in_out, s_in):
+    frames, rows, cols, chans = inp.shape
+    _rows_to_scratch(inp, s_in)
     dest = in_out.shape[0]
     r = lax.broadcasted_iota(jnp.int32, (chans, chans), 0)
     c = lax.broadcasted_iota(jnp.int32, (chans, chans), 1)
@@ -207,9 +208,6 @@
     for b in range(3):
         for piece in pieces[3 * b : 3 * b + 3]:
             piece.wait()
-        if b == 0:
-            for piece in pieces[6:]:
-                piece.start()
         lhs = ext[:, :, 2 - b : 2 - b + rows].reshape(count, chans)
         y = lax.dot_general(
             lhs,
@@ -294,7 +292,25 @@
         out[m] = flat[pl.ds(m, 54, stride=16), :].astype(BF16)
 
 
-def owner_kernel(step, terms, first, second, first_out, second_out, scales_out):
+def end_kernel(
+    step,
+    at_d,
+    up,
+    p0,
+    p1,
+    p2,
+    p3,
+    terms,
+    first,
+    second,
+    out,
+    first_out,
+    second_out,
+    scales_out,
+    flat,
+    outflat,
+):
+    finish_kernel(at_d, up, p0, p1, p2, p3, out, flat, outflat)
     reduced = terms[0].astype(F32)
     for k in range(1, terms.shape[0]):
         reduced = reduced + terms[k].astype(F32)
@@ -354,23 +370,21 @@
     tokens = frames * rows * cols
     sx = ("sxx", "sxz")
     spread = pltpu.VMEM((chans // 128, tokens, 128), F32)
-    g, proj, chunks, top, bot, up = _call(
+    g, proj, top, bot, up = _call(
         prepare,
         [
             (hash_seed.reshape(1), "scalar"),
             (pre_activation[0], "arg"),
             (upstream[0], "arg"),
-            (inputs[0], "arg"),
         ],
         [
             ((cols, rows, frames, chans), BF16),
             ((cols, rows, frames, rank), BF16),
-            ((16, cols, 2, frames, 128), BF16),
             ((cols, frames, chans + rank), BF16),
             ((cols, frames, chans + rank), BF16),
             ((cols, rows, frames, chans), BF16),
         ],
-        [spread] * 3,
+        [spread] * 2,
     )
     place = {a: lax.axis_index(a).astype(jnp.int32) for a in ("dp", "sy", "sxx", "sxz")}
 
@@ -379,6 +393,9 @@
 
     above = lax.ppermute(bot, "sy", ring("sy", 1))
     below = lax.ppermute(top, "sy", ring("sy", -1))
+    (chunks,) = _call(
+        pack_inputs, [(inputs[0], "arg")], [((16, cols, 2, frames, 128), BF16)], [spread]
+    )
     along_z = ((cols, rows + 2 + 8, frames, 128), BF16)
     along_x = ((4, cols, rows + 4, frames, 128), BF16)
     g, *sends = _call(
@@ -425,18 +442,18 @@
         [((cols, rows, frames, 128), BF16)] * 4,
     )
     parts = around(mine, "dp", -1)
-    (input_grad,) = _call(
-        finish_kernel,
-        places("dp") + [(up, "vmem")] + [(a, "vmem") for a in parts],
-        [((frames, rows, cols, chans), BF16)],
+    input_grad, new_first, new_second, scales = _call(
+        end_kernel,
+        [(step_count.reshape(1), "scalar")]
+        + places("dp")
+        + [(a, "vmem") for a in (up, *parts, terms, first_moment, second_moment)],
+        [
+            ((frames, rows, cols, chans), BF16),
+            (first_moment.shape, F32),
+            (first_moment.shape, F32),
+            ((first_moment.shape[0],), F32),
+        ],
         [pltpu.VMEM((chans // 128, cols, rows, frames, 128), F32), spread],
-    )
-
-    new_first, new_second, scales = _call(
-        owner_kernel,
-        [(step_count.reshape(1), "scalar")]
-        + [(a, "vmem") for a in (terms, first_moment, second_moment)],
-        [(first_moment.shape, F32), (first_moment.shape, F32), ((first_moment.shape[0],), F32)],
     )
     return (input_grad[None], new_first, new_second, scales)
 

time: 81.1 us -> 80.1 us (0.988)
  waiting for transfers between devices: 30.9 us -> 29.5 us
    ppermute x1, waiting for transfers between devices: 1.46 us -> 0.01 us  [step(): above = lax.ppermute(bot, 'sy', ring('sy', 1))]
  transfers between devices with their start and end apart: 17 -> 17, of which waited for: 13 -> 12; matrix products, arithmetic and copies ran while one was open for 0% -> 0% of each run, Pallas kernels for 6% -> 8%
where the time goes in v5:
time: 80.1 us; the launch traced here: 79.1 us
  starting transfers between devices  36.3 us (45%)
  waiting for transfers between devices  29.5 us (37%)
  Pallas kernels  11.1 us (14%)
  between operations  2.19 us (3%)
    ppermute x12, waiting for transfers between devices, around(): got[k] = lax.ppermute(arrays[k], axis, ring(axis, sign * k))  26.4 us
    ppermute x12, starting transfers between devices, around(): got[k] = lax.ppermute(arrays[k], axis, ring(axis, sign * k))  24.8 us
    pallas_call x8, Pallas kernels, _call(): pl.pallas_call(run, out_shape=[jax.ShapeDtypeStruct(shape, dtype) for sha...  11.1 us
    all_to_all x1, starting transfers between devices, step(): terms = lax.all_to_all(terms, ('dp', 'sy'), 0, 0, tiled=True)  4.57 us
    ppermute x1, starting transfers between devices, step(): from_right = lax.ppermute(left, sx, ring(sx, -1))  3.3 us
    ppermute x1, waiting for transfers between devices, step(): from_left = lax.ppermute(right, sx, ring(sx, 1))  2.97 us
    ppermute x1, starting transfers between devices, step(): from_left = lax.ppermute(right, sx, ring(sx, 1))  1.81 us
    ppermute x1, starting transfers between devices, step(): below = lax.ppermute(top, 'sy', ring('sy', -1))  1.73 us
  transfers between devices with their start and end apart: 17, of which 12 were waited for; matrix products, arithmetic and copies ran while one was open for 0% of the time, Pallas kernels for 8%

profile of v5, /device:TPU:2, one launch (start us, length us, event | category | flops | bytes accessed | tf_op | source)
XLA Modules:
  0.0 79.1 jit_solution(2161751621008575515)
XLA Ops:
  1.3 1.6 %shard_map.111 = (bf16[2,8,8,512]{3,2,1,0:T(8,128)(2,1)S(1)}, bf16[2,8,8,128]{3,2,1,0:T(8,128)(2,1)S(1)}, bf16[2,8,640]{2,1,0:T(8,128)(2,1)S(1)}, bf16[2,8,640]{...) custom-call(s32[1]{0:T(128)} %bitcast.10.refs_0_, bf16[8,8,2,512]{3,2,1,0:T(2,128)(2,1)} %bitcast.12, ...), custom_call_target="tpu_custom_call" | custom-call | tf_op jit(solution)/shard_map/pallas_call | solution.py:61
  3.0 1.7 %collective-permute-start.1 = (bf16[2,8,640]{2,1,0:T(8,128)(2,1)S(1)}, bf16[2,8,640]{2,1,0:T(8,128)(2,1)S(1)}, u32[]{:S(2)}, u32[]{:S(2)}) collective-permute-start(bf16[2,8,640]{2,1,0:T(8,128)(2,1)S(1)} %get-tuple-element.33), channel_id=1, source_target_pairs={{0,48},{16,0},{32,16},{48,32},{1,49},{17,1},{33,17},{49,33},{2,50}... | collective-permute-start | bytes 61448 | tf_op jit(solution)/shard_map/ppermute | solution.py:395
  4.7 1.5 %shard_map.112.refs_4_ = bf16[16,2,2,8,128]{4,3,2,1,0:T(8,128)(2,1)S(1)} custom-call(bf16[8,8,2,512]{3,2,1,0:T(2,128)(2,1)} %bitcast.14), custom_call_target="tpu_custom_call" | custom-call | tf_op jit(solution)/shard_map/pallas_call | solution.py:61
  6.3 3.3 %collective-permute-start.10 = (bf16[2,18,8,128]{3,2,1,0:T(8,128)(2,1)S(1)}, bf16[2,18,8,128]{3,2,1,0:T(8,128)(2,1)S(1)}, u32[]{:S(2)}, u32[]{:S(2)}) collective-permute-start(bf16[2,18,8,128]{3,2,1,0:T(8,128)(2,1)S(1)} %get-tuple-element.43), channel_id=1, source_target_pairs={{0,1},{1,2},{2,3},{3,0},{4,5},{5,6},{6,7},{7,4},{8,9},{9,10},{10,1... | collective-permute-start | bytes 221192 | tf_op jit(solution)/shard_map/ppermute | solution.py:361
  9.6 5.4 %collective-permute-start.11 = (bf16[2,18,8,128]{3,2,1,0:T(8,128)(2,1)S(1)}, bf16[2,18,8,128]{3,2,1,0:T(8,128)(2,1)S(1)}, u32[]{:S(2)}, u32[]{:S(2)}) collective-permute-start(bf16[2,18,8,128]{3,2,1,0:T(8,128)(2,1)S(1)} %get-tuple-element.44), channel_id=1, source_target_pairs={{0,2},{1,3},{2,0},{3,1},{4,6},{5,7},{6,4},{7,5},{8,10},{9,11},{10,... | collective-permute-start | bytes 221192 | tf_op jit(solution)/shard_map/ppermute | solution.py:361
  15.0 2.7 %collective-permute-start.12 = (bf16[2,18,8,128]{3,2,1,0:T(8,128)(2,1)S(1)}, bf16[2,18,8,128]{3,2,1,0:T(8,128)(2,1)S(1)}, u32[]{:S(2)}, u32[]{:S(2)}) collective-permute-start(bf16[2,18,8,128]{3,2,1,0:T(8,128)(2,1)S(1)} %get-tuple-element.45), channel_id=1, source_target_pairs={{0,3},{1,0},{2,1},{3,2},{4,7},{5,4},{6,5},{7,6},{8,11},{9,8},{10,9... | collective-permute-start | bytes 221192 | tf_op jit(solution)/shard_map/ppermute | solution.py:361
  17.7 3.2 %collective-permute-done.11.refs_3_ = bf16[2,18,8,128]{3,2,1,0:T(8,128)(2,1)S(1)} collective-permute-done((bf16[2,18,8,128]{3,2,1,0:T(8,128)(2,1)S(1)}, bf16[2,18,8,128]{3,2,1,0:T(8,128)(2,1)S(1)}, u32[]{:S(2)}, u32[]{:S(2)}) %collective-permute-start.11) | collective-permute-done | bytes 73760 | tf_op jit(solution)/shard_map/ppermute | solution.py:361
  20.9 2.6 %collective-permute-done.12.refs_4_ = bf16[2,18,8,128]{3,2,1,0:T(8,128)(2,1)S(1)} collective-permute-done((bf16[2,18,8,128]{3,2,1,0:T(8,128)(2,1)S(1)}, bf16[2,18,8,128]{3,2,1,0:T(8,128)(2,1)S(1)}, u32[]{:S(2)}, u32[]{:S(2)}) %collective-permute-start.12) | collective-permute-done | bytes 73760 | tf_op jit(solution)/shard_map/ppermute | solution.py:361
  23.5 1.6 %collective-permute-start.13 = (bf16[4,2,12,8,128]{4,3,2,1,0:T(8,128)(2,1)S(1)}, bf16[4,2,12,8,128]{4,3,2,1,0:T(8,128)(2,1)S(1)}, u32[]{:S(2)}, u32[]{:S(2)}) collective-permute-start(bf16[4,2,12,8,128]{4,3,2,1,0:T(8,128)(2,1)S(1)} %get-tuple-element.47), channel_id=1, source_target_pairs={{0,4},{4,8},{8,12},{12,0},{1,5},{5,9},{9,13},{13,1},{2,6},{6,10},{... | collective-permute-start | bytes 589832 | tf_op jit(solution)/shard_map/ppermute | solution.py:361
  25.1 1.1 %collective-permute-start.14 = (bf16[4,2,12,8,128]{4,3,2,1,0:T(8,128)(2,1)S(1)}, bf16[4,2,12,8,128]{4,3,2,1,0:T(8,128)(2,1)S(1)}, u32[]{:S(2)}, u32[]{:S(2)}) collective-permute-start(bf16[4,2,12,8,128]{4,3,2,1,0:T(8,128)(2,1)S(1)} %get-tuple-element.48), channel_id=1, source_target_pairs={{0,8},{4,12},{8,0},{12,4},{1,9},{5,13},{9,1},{13,5},{2,10},{6,14},... | collective-permute-start | bytes 589832 | tf_op jit(solution)/shard_map/ppermute | solution.py:361
  26.2 2.1 %collective-permute-start.15 = (bf16[4,2,12,8,128]{4,3,2,1,0:T(8,128)(2,1)S(1)}, bf16[4,2,12,8,128]{4,3,2,1,0:T(8,128)(2,1)S(1)}, u32[]{:S(2)}, u32[]{:S(2)}) collective-permute-start(bf16[4,2,12,8,128]{4,3,2,1,0:T(8,128)(2,1)S(1)} %get-tuple-element.49), channel_id=1, source_target_pairs={{0,12},{4,0},{8,4},{12,8},{1,13},{5,1},{9,5},{13,9},{2,14},{6,2},{... | collective-permute-start | bytes 589832 | tf_op jit(solution)/shard_map/ppermute | solution.py:361
  28.4 3.0 %collective-permute-done.13.refs_3_ = bf16[4,2,12,8,128]{4,3,2,1,0:T(8,128)(2,1)S(1)} collective-permute-done((bf16[4,2,12,8,128]{4,3,2,1,0:T(8,128)(2,1)S(1)}, bf16[4,2,12,8,128]{4,3,2,1,0:T(8,128)(2,1)S(1)}, u32[]{:S(2)}, u32[]{:S(2)}) %collective-permute-start.13) | collective-permute-done | bytes 196640 | tf_op jit(solution)/shard_map/ppermute | solution.py:361
  31.4 3.0 %collective-permute-done.14.refs_4_ = bf16[4,2,12,8,128]{4,3,2,1,0:T(8,128)(2,1)S(1)} collective-permute-done((bf16[4,2,12,8,128]{4,3,2,1,0:T(8,128)(2,1)S(1)}, bf16[4,2,12,8,128]{4,3,2,1,0:T(8,128)(2,1)S(1)}, u32[]{:S(2)}, u32[]{:S(2)}) %collective-permute-start.14) | collective-permute-done | bytes 196640 | tf_op jit(solution)/shard_map/ppermute | solution.py:361
  34.4 2.4 %collective-permute-done.15.refs_5_ = bf16[4,2,12,8,128]{4,3,2,1,0:T(8,128)(2,1)S(1)} collective-permute-done((bf16[4,2,12,8,128]{4,3,2,1,0:T(8,128)(2,1)S(1)}, bf16[4,2,12,8,128]{4,3,2,1,0:T(8,128)(2,1)S(1)}, u32[]{:S(2)}, u32[]{:S(2)}) %collective-permute-start.15) | collective-permute-done | bytes 196640 | tf_op jit(solution)/shard_map/ppermute | solution.py:361
  36.7 1.9 %shard_map.117 = bf16[16,54,128]{2,1,0:T(8,128)(2,1)} custom-call(s32[1]{0:T(128)} %bitcast.5.refs_0_, s32[1]{0:T(128)} %bitcast.6.refs_1_, bf16[4,2,12,8,128]{4,3,2,1,0:T(8,128)(2,1)S(1)} %get-tuple-element.46.refs_2_, bf16[4,2,12,8,128]{4,3,2,1,0:T(8,128)(2,1)S(1)} %collective-permute-done.13.refs_3_, ...), custom_call_target="tpu_custom_call" | custom-call | tf_op jit(solution)/shard_map/pallas_call | solution.py:61
  38.6 4.6 %all-to-all-start = ((bf16[16,54,128]{2,1,0:T(8,128)(2,1)}), bf16[16,54,128]{2,1,0:T(8,128)(2,1)S(1)}, u32[]{:S(2)}, u32[]{:S(2)}) async-start(bf16[16,54,128]{2,1,0:T(8,128)(2,1)} %shard_map.117), calls=%async_computation | async-start | bytes 458752 | tf_op jit(solution)/shard_map/all_to_all | solution.py:425
  43.2 1.9 %collective-permute-start.2 = (bf16[2,10,8,512]{3,2,1,0:T(8,128)(2,1)S(1)}, bf16[2,10,8,512]{3,2,1,0:T(8,128)(2,1)S(1)}, u32[]{:S(2)}, u32[]{:S(2)}) collective-permute-start(bf16[2,10,8,512]{3,2,1,0:T(8,128)(2,1)S(1)} %get-tuple-element.34.refs_0_), channel_id=1, source_target_pairs={{0,64},{64,128},{128,192},{192,0},{1,65},{65,129},{129,193},{193,1... | collective-permute-start | bytes 491528 | tf_op jit(solution)/shard_map/ppermute | solution.py:361
  45.1 2.7 %collective-permute-start.3 = (bf16[2,10,8,512]{3,2,1,0:T(8,128)(2,1)S(1)}, bf16[2,10,8,512]{3,2,1,0:T(8,128)(2,1)S(1)}, u32[]{:S(2)}, u32[]{:S(2)}) collective-permute-start(bf16[2,10,8,512]{3,2,1,0:T(8,128)(2,1)S(1)} %get-tuple-element.34.refs_0_), channel_id=1, source_target_pairs={{0,128},{64,192},{128,0},{192,64},{1,129},{65,193},{129,1},{193,65... | collective-permute-start | bytes 491528 | tf_op jit(solution)/shard_map/ppermute | solution.py:361
  47.8 1.5 %collective-permute-start.4 = (bf16[2,10,8,512]{3,2,1,0:T(8,128)(2,1)S(1)}, bf16[2,10,8,512]{3,2,1,0:T(8,128)(2,1)S(1)}, u32[]{:S(2)}, u32[]{:S(2)}) collective-permute-start(bf16[2,10,8,512]{3,2,1,0:T(8,128)(2,1)S(1)} %get-tuple-element.34.refs_0_), channel_id=1, source_target_pairs={{0,192},{64,0},{128,64},{192,128},{1,193},{65,1},{129,65},{193,129... | collective-permute-start | bytes 491528 | tf_op jit(solution)/shard_map/ppermute | solution.py:361
  49.3 4.5 %collective-permute-done.2.refs_1_ = bf16[2,10,8,512]{3,2,1,0:T(8,128)(2,1)S(1)} collective-permute-done((bf16[2,10,8,512]{3,2,1,0:T(8,128)(2,1)S(1)}, bf16[2,10,8,512]{3,2,1,0:T(8,128)(2,1)S(1)}, u32[]{:S(2)}, u32[]{:S(2)}) %collective-permute-start.2) | collective-permute-done | bytes 163872 | tf_op jit(solution)/shard_map/ppermute | solution.py:361
  53.7 3.6 %collective-permute-done.3.refs_2_ = bf16[2,10,8,512]{3,2,1,0:T(8,128)(2,1)S(1)} collective-permute-done((bf16[2,10,8,512]{3,2,1,0:T(8,128)(2,1)S(1)}, bf16[2,10,8,512]{3,2,1,0:T(8,128)(2,1)S(1)}, u32[]{:S(2)}, u32[]{:S(2)}) %collective-permute-start.3) | collective-permute-done | bytes 163872 | tf_op jit(solution)/shard_map/ppermute | solution.py:361
  57.3 4.5 %shard_map.114 = (f32[4,2,8,8,128]{4,3,2,1,0:T(8,128)S(1)}, bf16[4,8,8,128]{3,2,1,0:T(8,128)(2,1)S(1)}, bf16[4,8,8,128]{3,2,1,0:T(8,128)(2,1)S(1)}) custom-call(bf16[2,10,8,512]{3,2,1,0:T(8,128)(2,1)S(1)} %get-tuple-element.34.refs_0_, bf16[2,10,8,512]{3,2,1,0:T(8,128)(2,1)S(1)} %collective-permute-done.2.refs_1_, ...), custom_call_target="tpu_custom_call" | custom-call | tf_op jit(solution)/shard_map/pallas_call | solution.py:61
  61.8 1.8 %collective-permute-start.5 = (bf16[4,8,8,128]{3,2,1,0:T(8,128)(2,1)S(1)}, bf16[4,8,8,128]{3,2,1,0:T(8,128)(2,1)S(1)}, u32[]{:S(2)}, u32[]{:S(2)}) collective-permute-start(bf16[4,8,8,128]{3,2,1,0:T(8,128)(2,1)S(1)} %get-tuple-element.36), channel_id=1, source_target_pairs={{0,1},{1,2},{2,3},{3,4},{4,5},{5,6},{6,7},{7,8},{8,9},{9,10},{10,1... | collective-permute-start | bytes 196616 | tf_op jit(solution)/shard_map/ppermute | solution.py:438
  63.6 3.3 %collective-permute-start.6 = (bf16[4,8,8,128]{3,2,1,0:T(8,128)(2,1)S(1)}, bf16[4,8,8,128]{3,2,1,0:T(8,128)(2,1)S(1)}, u32[]{:S(2)}, u32[]{:S(2)}) collective-permute-start(bf16[4,8,8,128]{3,2,1,0:T(8,128)(2,1)S(1)} %get-tuple-element.37), channel_id=1, source_target_pairs={{0,15},{1,0},{2,1},{3,2},{4,3},{5,4},{6,5},{7,6},{8,7},{9,8},{10,9... | collective-permute-start | bytes 196616 | tf_op jit(solution)/shard_map/ppermute | solution.py:437
  66.9 3.0 %collective-permute-done.5.refs_3_ = bf16[4,8,8,128]{3,2,1,0:T(8,128)(2,1)S(1)} collective-permute-done((bf16[4,8,8,128]{3,2,1,0:T(8,128)(2,1)S(1)}, bf16[4,8,8,128]{3,2,1,0:T(8,128)(2,1)S(1)}, u32[]{:S(2)}, u32[]{:S(2)}) %collective-permute-start.5) | collective-permute-done | bytes 65568 | tf_op jit(solution)/shard_map/ppermute | solution.py:438
  70.0 1.5 %collective-permute-start.7 = (bf16[2,8,8,128]{3,2,1,0:T(8,128)(2,1)S(1)}, bf16[2,8,8,128]{3,2,1,0:T(8,128)(2,1)S(1)}, u32[]{:S(2)}, u32[]{:S(2)}) collective-permute-start(bf16[2,8,8,128]{3,2,1,0:T(8,128)(2,1)S(1)} %get-tuple-element.39), channel_id=1, source_target_pairs={{0,192},{64,0},{128,64},{192,128},{1,193},{65,1},{129,65},{193,129... | collective-permute-start | bytes 98312 | tf_op jit(solution)/shard_map/ppermute | solution.py:361
  71.5 0.9 %collective-permute-start.8 = (bf16[2,8,8,128]{3,2,1,0:T(8,128)(2,1)S(1)}, bf16[2,8,8,128]{3,2,1,0:T(8,128)(2,1)S(1)}, u32[]{:S(2)}, u32[]{:S(2)}) collective-permute-start(bf16[2,8,8,128]{3,2,1,0:T(8,128)(2,1)S(1)} %get-tuple-element.40), channel_id=1, source_target_pairs={{0,128},{64,192},{128,0},{192,64},{1,129},{65,193},{129,1},{193,65... | collective-permute-start | bytes 98312 | tf_op jit(solution)/shard_map/ppermute | solution.py:361
  72.4 0.2 collective-permute-start.9
  73.2 0.8 collective-permute-done.7.refs_4_
  74.0 2.9 %collective-permute-done.8.refs_5_ = bf16[2,8,8,128]{3,2,1,0:T(8,128)(2,1)S(1)} collective-permute-done((bf16[2,8,8,128]{3,2,1,0:T(8,128)(2,1)S(1)}, bf16[2,8,8,128]{3,2,1,0:T(8,128)(2,1)S(1)}, u32[]{:S(2)}, u32[]{:S(2)}) %collective-permute-start.8) | collective-permute-done | bytes 32800 | tf_op jit(solution)/shard_map/ppermute | solution.py:361
  76.9 0.6 collective-permute-done.9.refs_6_
  77.5 1.4 %shard_map.118 = (bf16[8,8,2,512]{3,2,1,0:T(2,128)(2,1)}, f32[54,128]{1,0:T(8,128)}, f32[54,128]{1,0:T(8,128)}, f32[54]{0:T(128)}) custom-call(s32[1]{0:T(128)} %bitcast.11.refs_0_, s32[1]{0:T(128)} %bitcast.1.refs_1_, bf16[2,8,8,512]{3,2,1,0:T(8,128)(2,1)S(1)} %get-tuple-element.29.refs_2_, bf16[2,8,8,128]{3,2,1,0:T(8,128)(2,1)S(1)} %get-tuple-element.38.refs_3_, ...), custom_call_target="tpu_custom_call" | custom-call | tf_op jit(solution)/shard_map/pallas_call | solution.py:61
  (14 shorter events, 0.4 us)
Async XLA Ops:
  2.9 74.6 %copy-start = (f32[54,128]{1,0:T(8,128)S(1)}, f32[54,128]{1,0:T(8,128)}, u32[]{:S(2)}) copy-start(f32[54,128]{1,0:T(8,128)} %refs_8_.1) | copy-start | bytes 82948
  2.9 74.6 %copy-start.1 = (f32[54,128]{1,0:T(8,128)S(1)}, f32[54,128]{1,0:T(8,128)}, u32[]{:S(2)}) copy-start(f32[54,128]{1,0:T(8,128)} %refs_9_.1) | copy-start | bytes 82948
  2.9 3.3 %collective-permute-start = (bf16[2,8,640]{2,1,0:T(8,128)(2,1)S(1)}, bf16[2,8,640]{2,1,0:T(8,128)(2,1)S(1)}, u32[]{:S(2)}, u32[]{:S(2)}) collective-permute-start(bf16[2,8,640]{2,1,0:T(8,128)(2,1)S(1)} %get-tuple-element.32), channel_id=1, source_target_pairs={{0,16},{16,32},{32,48},{48,0},{1,17},{17,33},{33,49},{49,1},{2,18}... | collective-permute-start | bytes 61448 | tf_op jit(solution)/shard_map/ppermute | solution.py:394
  3.0 3.2 %collective-permute-start.1 = (bf16[2,8,640]{2,1,0:T(8,128)(2,1)S(1)}, bf16[2,8,640]{2,1,0:T(8,128)(2,1)S(1)}, u32[]{:S(2)}, u32[]{:S(2)}) collective-permute-start(bf16[2,8,640]{2,1,0:T(8,128)(2,1)S(1)} %get-tuple-element.33), channel_id=1, source_target_pairs={{0,48},{16,0},{32,16},{48,32},{1,49},{17,1},{33,17},{49,33},{2,50}... | collective-permute-start | bytes 61448 | tf_op jit(solution)/shard_map/ppermute | solution.py:395
  6.3 11.4 %collective-permute-start.10 = (bf16[2,18,8,128]{3,2,1,0:T(8,128)(2,1)S(1)}, bf16[2,18,8,128]{3,2,1,0:T(8,128)(2,1)S(1)}, u32[]{:S(2)}, u32[]{:S(2)}) collective-permute-start(bf16[2,18,8,128]{3,2,1,0:T(8,128)(2,1)S(1)} %get-tuple-element.43), channel_id=1, source_target_pairs={{0,1},{1,2},{2,3},{3,0},{4,5},{5,6},{6,7},{7,4},{8,9},{9,10},{10,1... | collective-permute-start | bytes 221192 | tf_op jit(solution)/shard_map/ppermute | solution.py:361
  9.6 11.3 %collective-permute-start.11 = (bf16[2,18,8,128]{3,2,1,0:T(8,128)(2,1)S(1)}, bf16[2,18,8,128]{3,2,1,0:T(8,128)(2,1)S(1)}, u32[]{:S(2)}, u32[]{:S(2)}) collective-permute-start(bf16[2,18,8,128]{3,2,1,0:T(8,128)(2,1)S(1)} %get-tuple-element.44), channel_id=1, source_target_pairs={{0,2},{1,3},{2,0},{3,1},{4,6},{5,7},{6,4},{7,5},{8,10},{9,11},{10,... | collective-permute-start | bytes 221192 | tf_op jit(solution)/shard_map/ppermute | solution.py:361
  15.0 8.4 %collective-permute-start.12 = (bf16[2,18,8,128]{3,2,1,0:T(8,128)(2,1)S(1)}, bf16[2,18,8,128]{3,2,1,0:T(8,128)(2,1)S(1)}, u32[]{:S(2)}, u32[]{:S(2)}) collective-permute-start(bf16[2,18,8,128]{3,2,1,0:T(8,128)(2,1)S(1)} %get-tuple-element.45), channel_id=1, source_target_pairs={{0,3},{1,0},{2,1},{3,2},{4,7},{5,4},{6,5},{7,6},{8,11},{9,8},{10,9... | collective-permute-start | bytes 221192 | tf_op jit(solution)/shard_map/ppermute | solution.py:361
  23.5 7.8 %collective-permute-start.13 = (bf16[4,2,12,8,128]{4,3,2,1,0:T(8,128)(2,1)S(1)}, bf16[4,2,12,8,128]{4,3,2,1,0:T(8,128)(2,1)S(1)}, u32[]{:S(2)}, u32[]{:S(2)}) collective-permute-start(bf16[4,2,12,8,128]{4,3,2,1,0:T(8,128)(2,1)S(1)} %get-tuple-element.47), channel_id=1, source_target_pairs={{0,4},{4,8},{8,12},{12,0},{1,5},{5,9},{9,13},{13,1},{2,6},{6,10},{... | collective-permute-start | bytes 589832 | tf_op jit(solution)/shard_map/ppermute | solution.py:361
  25.1 9.3 %collective-permute-start.14 = (bf16[4,2,12,8,128]{4,3,2,1,0:T(8,128)(2,1)S(1)}, bf16[4,2,12,8,128]{4,3,2,1,0:T(8,128)(2,1)S(1)}, u32[]{:S(2)}, u32[]{:S(2)}) collective-permute-start(bf16[4,2,12,8,128]{4,3,2,1,0:T(8,128)(2,1)S(1)} %get-tuple-element.48), channel_id=1, source_target_pairs={{0,8},{4,12},{8,0},{12,4},{1,9},{5,13},{9,1},{13,5},{2,10},{6,14},... | collective-permute-start | bytes 589832 | tf_op jit(solution)/shard_map/ppermute | solution.py:361
  26.2 10.5 %collective-permute-start.15 = (bf16[4,2,12,8,128]{4,3,2,1,0:T(8,128)(2,1)S(1)}, bf16[4,2,12,8,128]{4,3,2,1,0:T(8,128)(2,1)S(1)}, u32[]{:S(2)}, u32[]{:S(2)}) collective-permute-start(bf16[4,2,12,8,128]{4,3,2,1,0:T(8,128)(2,1)S(1)} %get-tuple-element.49), channel_id=1, source_target_pairs={{0,12},{4,0},{8,4},{12,8},{1,13},{5,1},{9,5},{13,9},{2,14},{6,2},{... | collective-permute-start | bytes 589832 | tf_op jit(solution)/shard_map/ppermute | solution.py:361
  38.6 38.9 %all-to-all-start = ((bf16[16,54,128]{2,1,0:T(8,128)(2,1)}), bf16[16,54,128]{2,1,0:T(8,128)(2,1)S(1)}, u32[]{:S(2)}, u32[]{:S(2)}) async-start(bf16[16,54,128]{2,1,0:T(8,128)(2,1)} %shard_map.117), calls=%async_computation | async-start | bytes 458752 | tf_op jit(solution)/shard_map/all_to_all | solution.py:425
  43.2 10.5 %collective-permute-start.2 = (bf16[2,10,8,512]{3,2,1,0:T(8,128)(2,1)S(1)}, bf16[2,10,8,512]{3,2,1,0:T(8,128)(2,1)S(1)}, u32[]{:S(2)}, u32[]{:S(2)}) collective-permute-start(bf16[2,10,8,512]{3,2,1,0:T(8,128)(2,1)S(1)} %get-tuple-element.34.refs_0_), channel_id=1, source_target_pairs={{0,64},{64,128},{128,192},{192,0},{1,65},{65,129},{129,193},{193,1... | collective-permute-start | bytes 491528 | tf_op jit(solution)/shard_map/ppermute | solution.py:361
  45.1 12.2 %collective-permute-start.3 = (bf16[2,10,8,512]{3,2,1,0:T(8,128)(2,1)S(1)}, bf16[2,10,8,512]{3,2,1,0:T(8,128)(2,1)S(1)}, u32[]{:S(2)}, u32[]{:S(2)}) collective-permute-start(bf16[2,10,8,512]{3,2,1,0:T(8,128)(2,1)S(1)} %get-tuple-element.34.refs_0_), channel_id=1, source_target_pairs={{0,128},{64,192},{128,0},{192,64},{1,129},{65,193},{129,1},{193,65... | collective-permute-start | bytes 491528 | tf_op jit(solution)/shard_map/ppermute | solution.py:361
  47.8 9.5 %collective-permute-start.4 = (bf16[2,10,8,512]{3,2,1,0:T(8,128)(2,1)S(1)}, bf16[2,10,8,512]{3,2,1,0:T(8,128)(2,1)S(1)}, u32[]{:S(2)}, u32[]{:S(2)}) collective-permute-start(bf16[2,10,8,512]{3,2,1,0:T(8,128)(2,1)S(1)} %get-tuple-element.34.refs_0_), channel_id=1, source_target_pairs={{0,192},{64,0},{128,64},{192,128},{1,193},{65,1},{129,65},{193,129... | collective-permute-start | bytes 491528 | tf_op jit(solution)/shard_map/ppermute | solution.py:361
  61.8 8.1 %collective-permute-start.5 = (bf16[4,8,8,128]{3,2,1,0:T(8,128)(2,1)S(1)}, bf16[4,8,8,128]{3,2,1,0:T(8,128)(2,1)S(1)}, u32[]{:S(2)}, u32[]{:S(2)}) collective-permute-start(bf16[4,8,8,128]{3,2,1,0:T(8,128)(2,1)S(1)} %get-tuple-element.36), channel_id=1, source_target_pairs={{0,1},{1,2},{2,3},{3,4},{4,5},{5,6},{6,7},{7,8},{8,9},{9,10},{10,1... | collective-permute-start | bytes 196616 | tf_op jit(solution)/shard_map/ppermute | solution.py:438
  63.6 6.4 %collective-permute-start.6 = (bf16[4,8,8,128]{3,2,1,0:T(8,128)(2,1)S(1)}, bf16[4,8,8,128]{3,2,1,0:T(8,128)(2,1)S(1)}, u32[]{:S(2)}, u32[]{:S(2)}) collective-permute-start(bf16[4,8,8,128]{3,2,1,0:T(8,128)(2,1)S(1)} %get-tuple-element.37), channel_id=1, source_target_pairs={{0,15},{1,0},{2,1},{3,2},{4,3},{5,4},{6,5},{7,6},{8,7},{9,8},{10,9... | collective-permute-start | bytes 196616 | tf_op jit(solution)/shard_map/ppermute | solution.py:437
  70.0 4.0 %collective-permute-start.7 = (bf16[2,8,8,128]{3,2,1,0:T(8,128)(2,1)S(1)}, bf16[2,8,8,128]{3,2,1,0:T(8,128)(2,1)S(1)}, u32[]{:S(2)}, u32[]{:S(2)}) collective-permute-start(bf16[2,8,8,128]{3,2,1,0:T(8,128)(2,1)S(1)} %get-tuple-element.39), channel_id=1, source_target_pairs={{0,192},{64,0},{128,64},{192,128},{1,193},{65,1},{129,65},{193,129... | collective-permute-start | bytes 98312 | tf_op jit(solution)/shard_map/ppermute | solution.py:361
  71.5 5.4 %collective-permute-start.8 = (bf16[2,8,8,128]{3,2,1,0:T(8,128)(2,1)S(1)}, bf16[2,8,8,128]{3,2,1,0:T(8,128)(2,1)S(1)}, u32[]{:S(2)}, u32[]{:S(2)}) collective-permute-start(bf16[2,8,8,128]{3,2,1,0:T(8,128)(2,1)S(1)} %get-tuple-element.40), channel_id=1, source_target_pairs={{0,128},{64,192},{128,0},{192,64},{1,129},{65,193},{129,1},{193,65... | collective-permute-start | bytes 98312 | tf_op jit(solution)/shard_map/ppermute | solution.py:361
  72.4 5.1 %collective-permute-start.9 = (bf16[2,8,8,128]{3,2,1,0:T(8,128)(2,1)S(1)}, bf16[2,8,8,128]{3,2,1,0:T(8,128)(2,1)S(1)}, u32[]{:S(2)}, u32[]{:S(2)}) collective-permute-start(bf16[2,8,8,128]{3,2,1,0:T(8,128)(2,1)S(1)} %get-tuple-element.41), channel_id=1, source_target_pairs={{0,64},{64,128},{128,192},{192,0},{1,65},{65,129},{129,193},{193,1... | collective-permute-start | bytes 98312 | tf_op jit(solution)/shard_map/ppermute | solution.py:361
